TPU v7x, 32 devices: a whole 2x2x4 slice. The times are simulated.
32 devices in a mesh: node: 16 (over z, y, x), head: 2 (over core).
Axes of the slice: x: 2, y: 2, z: 4, core: 2. Of those that a mesh axis runs over, the one named last changes fastest.
Arguments:
- inputs: bfloat16 [8192, 8192], P('node', 'head'), may hold values from -6 to 6
- b_matrix: bfloat16 [8192, 128], P('node'), may hold values from -0.5390625 to 0.5390625
- c_matrix: bfloat16 [8192, 128], P('node'), may hold values from -0.5390625 to 0.5390625
- step_size: float32 [128, 8192], P('head', 'node'), may hold values from 0 to 4, as said below
- decay_rate: float32 [128], P('head'), may hold values from 0 to 1, as said below
- parents: int32 [16], replicated, may hold values from -1 to 15, as said below
- cotangent: bfloat16 [8192, 8192], P('node', 'head'), may hold values from -0.59765625 to 0.59765625
Outputs:
- outputs: bfloat16 [8192, 8192], P('node', 'head')
- grad_inputs: bfloat16 [8192, 8192], P('node', 'head')
- grad_b: float32 [8192, 128], P(('node', 'head'))
- grad_c: float32 [8192, 128], P(('node', 'head'))
Inputs may be any that keep to these rules, and one draw needn't show every extreme that they name: parents[n] is -1 for a root or the index of another node; following parents from any node reaches a root within 3 steps, and some node is exactly 3 steps from its root. `step_size`: positive. `decay_rate`: positive.
All inputs are finite; a program needn't handle non-finite values.
Results may differ from a plain program's by a relative error of at most 0.019.
Values may be sent and summed in bfloat16 or wider, within the bound.
No kernel may reach another device: no remote copies, remote signals or barrier semaphores. Data moves between devices by JAX's collectives and lax.ppermute only.
A program may use at most 128 MiB of HBM per device.

v0:
```python
import functools
import math

import jax
import jax.numpy as jnp
from jax import lax
from jax.experimental import pallas as pl
from jax.experimental.pallas import tpu as pltpu
from jax.sharding import PartitionSpec as P

LEVELS = 3
LANES = 128
CHUNKS = 2

f32 = jnp.float32
bf16 = jnp.bfloat16
NN = (((1,), (0,)), ((), ()))
NT = (((1,), (1,)), ((), ()))


def mm(a, b, dims=NN):
    return lax.dot_general(a, b, dims, preferred_element_type=f32)


def split_two(v):
    high = v.astype(bf16)
    return high, (v - high.astype(f32)).astype(bf16)


def spread_matrix(rows, heads, width, head_width, offset):
    row = lax.broadcasted_iota(jnp.int32, (rows, width), 0) % heads
    lane = (lax.broadcasted_iota(jnp.int32, (rows, width), 1) + offset) // head_width
    return (row == lane).astype(bf16)


def states_kernel(
    heads,
    head_width,
    x_ref,
    cot_ref,
    b_ref,
    c_ref,
    step_ref,
    rate_ref,
    send_ref,
    low_ref,
    src_ref,
    grow_ref,
    tail_ref,
    bt_ref,
    ct_ref,
):
    block = x_ref.shape[1]
    length = step_ref.shape[1]
    index = pl.program_id(0)
    width = heads * head_width

    @pl.when(index == 0)
    def _():
        step = step_ref[...]
        terms = -step * rate_ref[...]
        row = lax.broadcasted_iota(jnp.int32, (length, length), 0)
        col = lax.broadcasted_iota(jnp.int32, (length, length), 1)
        upper = (row <= col).astype(bf16)
        first = terms.astype(bf16)
        rest = terms - first.astype(f32)
        second, third = split_two(rest)
        cumulative = mm(third, upper) + mm(second, upper) + mm(first, upper)
        last = cumulative[:, length - 1 :]
        low_ref[...] = cumulative
        src_ref[...] = cumulative - jnp.log(step)
        growth = jnp.exp(cumulative)
        tail = jnp.exp(last - cumulative) * step
        grow_ref[...] = jnp.concatenate(split_two(growth.T), axis=1)
        tail_ref[...] = jnp.concatenate(split_two(tail.T), axis=1)
        bt_ref[...] = b_ref[...].T
        ct_ref[...] = c_ref[...].T
        total = jnp.exp(jnp.broadcast_to(last, (heads, send_ref.shape[0])))
        pad = jnp.zeros((LANES - heads, send_ref.shape[0]), f32)
        totals = jnp.concatenate([total, pad], axis=0).T
        send_ref[:, 2 * width :] = totals.astype(bf16)

    spread = spread_matrix(2 * heads, heads, block, head_width, index * block)
    tail_wide = mm(tail_ref[...], spread)
    grow_wide = mm(grow_ref[...], spread)
    tailed = (tail_wide * x_ref[...].astype(f32)).astype(bf16)
    emitted = (grow_wide * cot_ref[...].astype(f32)).astype(bf16)
    at = pl.multiple_of(index * block, block)
    send_ref[:, pl.ds(at, block)] = mm(bt_ref[...], tailed).astype(bf16)
    send_ref[:, pl.ds(at + width, block)] = mm(ct_ref[...], emitted).astype(bf16)


def node_states(x, cot, b, c, step, rate, chunk, heads, head_width):
    length, state = b.shape
    width = heads * head_width
    block = min(width, 4 * LANES)
    count = width // block
    whole = lambda i: (0, 0)
    return pl.pallas_call(
        functools.partial(states_kernel, heads, head_width),
        grid=(count,),
        in_specs=[
            pl.BlockSpec((length, block), lambda i: (0, chunk * count + i)),
            pl.BlockSpec((length, block), lambda i: (0, chunk * count + i)),
            pl.BlockSpec((length, state), whole),
            pl.BlockSpec((length, state), whole),
            pl.BlockSpec((heads, length), lambda i: (chunk, 0)),
            pl.BlockSpec((heads, 1), lambda i: (chunk, 0)),
        ],
        out_specs=[
            pl.BlockSpec((state, 2 * width + LANES), whole),
            pl.BlockSpec((heads, length), whole),
            pl.BlockSpec((heads, length), whole),
            pl.BlockSpec((length, 2 * heads), whole),
            pl.BlockSpec((length, 2 * heads), whole),
        ],
        out_shape=[
            jax.ShapeDtypeStruct((state, 2 * width + LANES), bf16),
            jax.ShapeDtypeStruct((heads, length), f32),
            jax.ShapeDtypeStruct((heads, length), f32),
            jax.ShapeDtypeStruct((length, 2 * heads), bf16),
            jax.ShapeDtypeStruct((length, 2 * heads), bf16),
        ],
        scratch_shapes=[pltpu.VMEM((state, length), bf16), pltpu.VMEM((state, length), bf16)],
        name="node_states",
        cost_estimate=pl.CostEstimate(
            flops=4 * length * state * width,
            bytes_accessed=4 * length * width + 4 * state * width,
            transcendentals=0,
        ),
    )(x, cot, b, c, step, rate)


def inner_kernel(
    heads,
    head_width,
    x_ref,
    cot_ref,
    b_ref,
    c_ref,
    low_ref,
    src_ref,
    out_ref,
    grad_ref,
    gc_ref,
    gb_ref,
    gram_ref,
    mixed_ref,
    wa_ref,
    wb_ref,
):
    length = x_ref.shape[0]
    index = pl.program_id(0)
    pack = LANES // head_width
    blocks = length // LANES
    half = length // 2
    weights = (wa_ref, wb_ref)

    @pl.when(index == 0)
    def _():
        gram_ref[...] = mm(c_ref[...], b_ref[...], NT)
        mixed_ref[...] = jnp.zeros_like(mixed_ref)
        for ref in weights:
            ref[...] = jnp.zeros_like(ref)

    lane = lax.broadcasted_iota(jnp.int32, (1, LANES), 1) // head_width
    causal = lax.broadcasted_iota(jnp.int32, (LANES, LANES), 0) >= lax.broadcasted_iota(
        jnp.int32, (LANES, LANES), 1
    )
    x = x_ref[...]
    cot = cot_ref[...]
    cots = [jnp.where(lane == a, cot, jnp.zeros_like(cot)) for a in range(pack)]
    columns = [
        jnp.broadcast_to(low_ref[pl.ds(index * pack + a, 1), :], (LANES, length)).T
        for a in range(pack)
    ]
    sources = [src_ref[pl.ds(index * pack + a, 1), :] for a in range(pack)]
    for i in range(blocks):
        rows = slice(i * LANES, (i + 1) * LANES)
        until = (i + 1) * LANES
        scores = [mm(cots[a][rows], x[:until], NT) for a in range(pack)]
        for j in range(i + 1):
            cols = slice(j * LANES, (j + 1) * LANES)
            gram = gram_ref[rows, cols]
            mixed = mixed_ref[rows, cols]
            for a in range(pack):
                differ = columns[a][rows] - sources[a][:, cols]
                if i == j:
                    differ = jnp.where(causal, differ, -jnp.inf)
                decay = jnp.exp(differ)
                weights[a][rows, cols] = (decay * gram).astype(bf16)
                mixed = mixed + decay * scores[a][:, cols]
            mixed_ref[rows, cols] = mixed
    cot_turned = cot.T
    turned = []
    for a in range(pack):
        w = weights[a]
        top = mm(w[:half, :half], x[:half])
        bottom = mm(w[half:, :], x)
        both = jnp.concatenate([top, bottom], axis=0)
        out = both if a == 0 else jnp.where(lane == a, both, out)
        part = cot_turned[a * head_width : (a + 1) * head_width]
        left = mm(part, w[:, :half])
        right = mm(part[:, half:], w[half:, half:])
        turned.append(jnp.concatenate([left, right], axis=1))
    out_ref[...] = out.astype(out_ref.dtype)
    grad_ref[...] = jnp.concatenate(turned, axis=0).T.astype(grad_ref.dtype)

    @pl.when(index == pl.num_programs(0) - 1)
    def _():
        high, low = split_two(mixed_ref[...])
        gc_ref[...] = mm(high, b_ref[...]) + mm(low, b_ref[...])
        high, low = split_two(mixed_ref[...].T)
        gb_ref[...] = mm(high, c_ref[...]) + mm(low, c_ref[...])


def node_inner(x, cot, b, c, low, src, chunk, heads, head_width):
    length, state = b.shape
    width = heads * head_width
    count = width // LANES
    whole = lambda i: (0, 0)
    spot = lambda i: (0, i)
    return pl.pallas_call(
        functools.partial(inner_kernel, heads, head_width),
        grid=(count,),
        in_specs=[
            pl.BlockSpec((length, LANES), lambda i: (0, chunk * count + i)),
            pl.BlockSpec((length, LANES), lambda i: (0, chunk * count + i)),
            pl.BlockSpec((length, state), whole),
            pl.BlockSpec((length, state), whole),
            pl.BlockSpec((heads, length), whole),
            pl.BlockSpec((heads, length), whole),
        ],
        out_specs=[
            pl.BlockSpec((length, LANES), spot),
            pl.BlockSpec((length, LANES), spot),
            pl.BlockSpec((length, state), whole),
            pl.BlockSpec((length, state), whole),
        ],
        out_shape=[
            jax.ShapeDtypeStruct((length, width), f32),
            jax.ShapeDtypeStruct((length, width), f32),
            jax.ShapeDtypeStruct((length, state), f32),
            jax.ShapeDtypeStruct((length, state), f32),
        ],
        scratch_shapes=[
            pltpu.VMEM((length, length), f32),
            pltpu.VMEM((length, length), f32),
            pltpu.VMEM((length, length), bf16),
            pltpu.VMEM((length, length), bf16),
        ],
        name="node_inner",
        cost_estimate=pl.CostEstimate(
            flops=24 * length * length * width,
            bytes_accessed=12 * length * width,
            transcendentals=length * length * heads,
        ),
    )(x, cot, b, c, low, src)


def tree_kernel(heads, head_width, parents_ref, recv_ref, out_ref, decay_ref, back_ref):
    nodes, rows = recv_ref.shape[:2]
    width = heads * head_width
    totals = recv_ref[:, :, 2 * width :].astype(f32).reshape(nodes * rows, LANES).astype(bf16)
    spread = spread_matrix(LANES, LANES, width, head_width, 0)
    decay_ref[...] = mm(totals, spread).reshape(nodes, rows, width)
    back_ref[...] = jnp.zeros_like(back_ref)

    def visit(n, carry):
        seed = recv_ref[n, :, width : 2 * width].astype(f32)
        start = jnp.zeros((rows, width), f32)
        factor = jnp.ones((rows, width), f32)
        at = n
        valid = jnp.bool_(True)
        for level in range(LEVELS):
            up = parents_ref[at]
            valid = jnp.logical_and(valid, up >= 0)
            at = jnp.maximum(up, 0)
            keep = jnp.where(valid, f32(1), f32(0))
            factor = factor * keep
            start = start + factor * recv_ref[at, :, :width].astype(f32)
            back_ref[at] = back_ref[at] + factor * seed
            if level < LEVELS - 1:
                factor = factor * decay_ref[at]
        out_ref[n, :, :width] = start.astype(bf16)
        return carry

    lax.fori_loop(0, nodes, visit, 0)
    out_ref[:, :, width:] = back_ref[...].astype(bf16)


def combine(parents, recv, heads, head_width):
    nodes, rows, _ = recv.shape
    width = heads * head_width
    return pl.pallas_call(
        functools.partial(tree_kernel, heads, head_width),
        in_specs=[
            pl.BlockSpec(memory_space=pltpu.SMEM),
            pl.BlockSpec(memory_space=pltpu.VMEM),
        ],
        out_specs=pl.BlockSpec(memory_space=pltpu.VMEM),
        out_shape=jax.ShapeDtypeStruct((nodes, rows, 2 * width), bf16),
        scratch_shapes=[
            pltpu.VMEM((nodes, rows, width), f32),
            pltpu.VMEM((nodes, rows, width), f32),
        ],
        name="tree_combine",
        cost_estimate=pl.CostEstimate(
            flops=20 * nodes * rows * width,
            bytes_accessed=8 * nodes * rows * width,
            transcendentals=0,
        ),
    )(parents, recv)


def outer_kernel(
    heads,
    head_width,
    aliased,
    x_ref,
    cot_ref,
    b_ref,
    c_ref,
    grow_ref,
    tail_ref,
    start_ref,
    back_ref,
    inner_ref,
    grad_ref,
    *refs,
):
    out_ref, gx_ref, gc_ref, gb_ref = refs[2:] if aliased else refs
    block = x_ref.shape[1]
    index = pl.program_id(0)
    spread = spread_matrix(2 * heads, heads, block, head_width, index * block)
    grow_wide = mm(grow_ref[...], spread)
    tail_wide = mm(tail_ref[...], spread)
    start = start_ref[...]
    back = back_ref[...]
    out_ref[...] = (inner_ref[...] + grow_wide * mm(c_ref[...], start)).astype(bf16)
    gx_ref[...] = (grad_ref[...] + tail_wide * mm(b_ref[...], back)).astype(bf16)
    emitted = (grow_wide * cot_ref[...].astype(f32)).astype(bf16)
    tailed = (tail_wide * x_ref[...].astype(f32)).astype(bf16)
    gc = mm(emitted, start, NT)
    gb = mm(tailed, back, NT)

    @pl.when(index == 0)
    def _():
        gc_ref[...] = gc
        gb_ref[...] = gb

    @pl.when(index > 0)
    def _():
        gc_ref[...] += gc
        gb_ref[...] += gb


def node_outer(x, cot, b, c, grow, tail, states, inner, grad, prior, chunk, heads, head_width):
    length, state = b.shape
    width = heads * head_width
    block = min(width, 4 * LANES)
    count = width // block
    whole = lambda i: (0, 0)
    spot = lambda i: (0, i)
    place = lambda i: (0, chunk * count + i)
    aliased = prior is not None
    operands = [x, cot, b, c, grow, tail, states, states, inner, grad]
    in_specs = [
        pl.BlockSpec((length, block), place),
        pl.BlockSpec((length, block), place),
        pl.BlockSpec((length, state), whole),
        pl.BlockSpec((length, state), whole),
        pl.BlockSpec((length, 2 * heads), whole),
        pl.BlockSpec((length, 2 * heads), whole),
        pl.BlockSpec((state, block), spot),
        pl.BlockSpec((state, block), lambda i: (0, count + i)),
        pl.BlockSpec((length, block), spot),
        pl.BlockSpec((length, block), spot),
    ]
    aliases = {}
    if aliased:
        aliases = {len(operands): 0, len(operands) + 1: 1}
        operands += list(prior)
        in_specs += [pl.BlockSpec(memory_space=pl.ANY)] * 2
    return pl.pallas_call(
        functools.partial(outer_kernel, heads, head_width, aliased),
        grid=(count,),
        in_specs=in_specs,
        out_specs=[
            pl.BlockSpec((length, block), place),
            pl.BlockSpec((length, block), place),
            pl.BlockSpec((length, state), whole),
            pl.BlockSpec((length, state), whole),
        ],
        out_shape=[
            jax.ShapeDtypeStruct(x.shape, bf16),
            jax.ShapeDtypeStruct(x.shape, bf16),
            jax.ShapeDtypeStruct((length, state), f32),
            jax.ShapeDtypeStruct((length, state), f32),
        ],
        input_output_aliases=aliases,
        name="node_outer",
        cost_estimate=pl.CostEstimate(
            flops=8 * length * state * width,
            bytes_accessed=16 * length * width,
            transcendentals=0,
        ),
    )(*operands)


def scatter_sum(parts):
    size = lax.axis_size("head")
    me = lax.axis_index("head")
    rows = parts.shape[1] // size
    total = lax.dynamic_slice_in_dim(parts, me * rows, rows, axis=1)
    for shift in range(1, size):
        target = (me + shift) % size
        piece = lax.dynamic_slice_in_dim(parts, target * rows, rows, axis=1).astype(bf16)
        moved = lax.ppermute(piece, "head", [(i, (i + shift) % size) for i in range(size)])
        total = total + moved.astype(f32)
    return total


def on_device(inputs, b_matrix, c_matrix, step_size, decay_rate, parents, cotangent):
    state = b_matrix.shape[1]
    head_count = step_size.shape[0]
    head_width = inputs.shape[1] // head_count
    nodes = lax.axis_size("node")
    heads = head_count // CHUNKS
    rows = state // nodes
    rate = decay_rate[:, None]

    def swap(v):
        moved = lax.all_to_all(
            v.reshape(nodes, rows, v.shape[-1]), "node", split_axis=0, concat_axis=0, tiled=True
        )
        return moved

    chunks = range(CHUNKS)
    made = [
        node_states(
            inputs, cotangent, b_matrix, c_matrix, step_size, rate, k, heads, head_width
        )
        for k in chunks
    ]
    received = [swap(made[k][0]) for k in chunks]
    inner = [
        node_inner(
            inputs, cotangent, b_matrix, c_matrix, made[k][1], made[k][2], k, heads, head_width
        )
        for k in chunks
    ]
    joined = [combine(parents, received[k], heads, head_width) for k in chunks]
    states = [swap(joined[k]).reshape(state, -1) for k in chunks]
    prior = None
    grad_c = sum(inner[k][2] for k in chunks)
    grad_b = sum(inner[k][3] for k in chunks)
    for k in chunks:
        result = node_outer(
            inputs,
            cotangent,
            b_matrix,
            c_matrix,
            made[k][3],
            made[k][4],
            states[k],
            inner[k][0],
            inner[k][1],
            prior,
            k,
            heads,
            head_width,
        )
        prior = result[:2]
        grad_c = grad_c + result[2]
        grad_b = grad_b + result[3]
    grads = scatter_sum(jnp.stack([grad_b, grad_c]))
    return prior[0], prior[1], grads[0], grads[1]


def solution(mesh):
    return jax.shard_map(
        on_device,
        mesh=mesh,
        in_specs=(
            P("node", "head"),
            P("node", None),
            P("node", None),
            P("head", "node"),
            P("head"),
            P(),
            P("node", "head"),
        ),
        out_specs=(
            P("node", "head"),
            P("node", "head"),
            P(("node", "head"), None),
            P(("node", "head"), None),
        ),
        check_vma=False,
    )
```

profile of v0, /device:TPU:0, one launch (start us, length us, event | category | flops | bytes accessed | tf_op | source)
XLA Modules:
  0.0 168.6 jit_solution(11606709009751316811)
XLA Ops:
  0.6 1.3 copy.13.rate_ref
  2.0 6.2 %node_states.3 = (bf16[128,4224]{1,0:T(8,128)(2,1)}, f32[32,512]{1,0:T(8,128)}, f32[32,512]{1,0:T(8,128)}, bf16[512,64]{1,0:T(8,128)(2,1)}, bf16[512,64]{1,0:T(8,128)(2,1)}) custom-call(bf16[512,4096]{1,0:T(8,128)(2,1)} %x_ref.11, bf16[512,4096]{1,0:T(8,128)(2,1)} %cot_ref.11, bf16[512,128]{1,0:T(8,128)(2,1)} %b_ref.11, bf16[512,128]{1,0:T(8,128)(2,1)} %c_ref.11, ...), custom_call_target="tpu_custom_call" | custom-call | flops 536870912 | bytes 5242880 | tf_op jit(solution)/shard_map/node_states/pallas_call | solution.py:99
  8.2 8.4 %all-to-all-start.2 = ((bf16[16,8,4224]{2,1,0:T(8,128)(2,1)}), bf16[16,8,4224]{2,1,0:T(8,128)(2,1)S(1)}, u32[]{:S(2)}, u32[]{:S(2)}) async-start(bf16[16,8,4224]{2,1,0:T(8,128)(2,1)} %bitcast.18), calls=%async_computation.2 | async-start | bytes 2162688 | tf_op jit(solution)/shard_map/all_to_all | solution.py:434
  16.5 6.2 %node_states.2 = (bf16[128,4224]{1,0:T(8,128)(2,1)}, f32[32,512]{1,0:T(8,128)}, f32[32,512]{1,0:T(8,128)}, bf16[512,64]{1,0:T(8,128)(2,1)}, bf16[512,64]{1,0:T(8,128)(2,1)}) custom-call(bf16[512,4096]{1,0:T(8,128)(2,1)} %x_ref.11, bf16[512,4096]{1,0:T(8,128)(2,1)} %cot_ref.11, bf16[512,128]{1,0:T(8,128)(2,1)} %b_ref.11, bf16[512,128]{1,0:T(8,128)(2,1)} %c_ref.11, ...), custom_call_target="tpu_custom_call" | custom-call | flops 536870912 | bytes 5242880 | tf_op jit(solution)/shard_map/node_states/pallas_call | solution.py:99
  22.8 18.8 %all-to-all-done.2.recv_ref = bf16[16,8,4224]{2,1,0:T(8,128)(2,1)S(1)} async-done(((bf16[16,8,4224]{2,1,0:T(8,128)(2,1)}), bf16[16,8,4224]{2,1,0:T(8,128)(2,1)S(1)}, u32[]{:S(2)}, u32[]{:S(2)}) %all-to-all-start.2) | async-done | bytes 1081376 | tf_op jit(solution)/shard_map/all_to_all | solution.py:434
  41.6 5.9 %all-to-all-start = ((bf16[16,8,4224]{2,1,0:T(8,128)(2,1)}), bf16[16,8,4224]{2,1,0:T(8,128)(2,1)S(1)}, u32[]{:S(2)}, u32[]{:S(2)}) async-start(bf16[16,8,4224]{2,1,0:T(8,128)(2,1)} %bitcast.17), calls=%async_computation | async-start | bytes 2162688 | tf_op jit(solution)/shard_map/all_to_all | solution.py:434
  47.5 0.0 copy-done.3
  47.5 3.5 %tree_combine.3 = bf16[16,8,4096]{2,1,0:T(8,128)(2,1)} custom-call(s32[16]{0:T(128)} %parents_ref.3, bf16[16,8,4224]{2,1,0:T(8,128)(2,1)} %copy-done.3), custom_call_target="tpu_custom_call" | custom-call | flops 5242880 | bytes 2097152 | tf_op jit(solution)/shard_map/tree_combine/pallas_call | solution.py:295
  51.0 20.1 %all-to-all-done.recv_ref = bf16[16,8,4224]{2,1,0:T(8,128)(2,1)S(1)} async-done(((bf16[16,8,4224]{2,1,0:T(8,128)(2,1)}), bf16[16,8,4224]{2,1,0:T(8,128)(2,1)S(1)}, u32[]{:S(2)}, u32[]{:S(2)}) %all-to-all-start) | async-done | bytes 1081376 | tf_op jit(solution)/shard_map/all_to_all | solution.py:434
  71.1 6.1 %all-to-all-start.3 = ((bf16[16,8,4096]{2,1,0:T(8,128)(2,1)}), bf16[16,8,4096]{2,1,0:T(8,128)(2,1)S(1)}, u32[]{:S(2)}, u32[]{:S(2)}) async-start(bf16[16,8,4096]{2,1,0:T(8,128)(2,1)} %tree_combine.3), calls=%async_computation.3 | async-start | bytes 2097152 | tf_op jit(solution)/shard_map/all_to_all | solution.py:434
  77.2 0.0 copy-done.2
  77.2 3.5 %tree_combine.2 = bf16[16,8,4096]{2,1,0:T(8,128)(2,1)} custom-call(s32[16]{0:T(128)} %parents_ref.3, bf16[16,8,4224]{2,1,0:T(8,128)(2,1)} %copy-done.2), custom_call_target="tpu_custom_call" | custom-call | flops 5242880 | bytes 2097152 | tf_op jit(solution)/shard_map/tree_combine/pallas_call | solution.py:295
  80.7 19.4 %all-to-all-done.3 = bf16[16,8,4096]{2,1,0:T(8,128)(2,1)S(1)} async-done(((bf16[16,8,4096]{2,1,0:T(8,128)(2,1)}), bf16[16,8,4096]{2,1,0:T(8,128)(2,1)S(1)}, u32[]{:S(2)}, u32[]{:S(2)}) %all-to-all-start.3) | async-done | bytes 1048608 | tf_op jit(solution)/shard_map/all_to_all | solution.py:434
  100.1 6.0 %all-to-all-start.1 = ((bf16[16,8,4096]{2,1,0:T(8,128)(2,1)}), bf16[16,8,4096]{2,1,0:T(8,128)(2,1)S(1)}, u32[]{:S(2)}, u32[]{:S(2)}) async-start(bf16[16,8,4096]{2,1,0:T(8,128)(2,1)} %tree_combine.2), calls=%async_computation.1 | async-start | bytes 2097152 | tf_op jit(solution)/shard_map/all_to_all | solution.py:434
  106.1 19.5 %node_inner.3 = (f32[512,2048]{1,0:T(8,128)}, f32[512,2048]{1,0:T(8,128)}, f32[512,128]{1,0:T(8,128)}, f32[512,128]{1,0:T(8,128)}) custom-call(bf16[512,4096]{1,0:T(8,128)(2,1)} %x_ref.11, bf16[512,4096]{1,0:T(8,128)(2,1)} %cot_ref.11, bf16[512,128]{1,0:T(8,128)(2,1)} %b_ref.11, bf16[512,128]{1,0:T(8,128)(2,1)} %c_ref.11, ...), custom_call_target="tpu_custom_call" | custom-call | flops 12884901888 | bytes 12582912 | tf_op jit(solution)/shard_map/node_inner/pallas_call | solution.py:223
  125.6 0.0 copy-done
  125.6 19.5 %node_inner.2 = (f32[512,2048]{1,0:T(8,128)}, f32[512,2048]{1,0:T(8,128)}, f32[512,128]{1,0:T(8,128)}, f32[512,128]{1,0:T(8,128)}) custom-call(bf16[512,4096]{1,0:T(8,128)(2,1)} %x_ref.11, bf16[512,4096]{1,0:T(8,128)(2,1)} %cot_ref.11, bf16[512,128]{1,0:T(8,128)(2,1)} %b_ref.11, bf16[512,128]{1,0:T(8,128)(2,1)} %c_ref.11, ...), custom_call_target="tpu_custom_call" | custom-call | flops 12884901888 | bytes 12582912 | tf_op jit(solution)/shard_map/node_inner/pallas_call | solution.py:223
  145.1 9.4 %node_outer.2 = (bf16[512,4096]{1,0:T(8,128)(2,1)}, bf16[512,4096]{1,0:T(8,128)(2,1)}, f32[512,128]{1,0:T(8,128)}, f32[512,128]{1,0:T(8,128)}) custom-call(bf16[512,4096]{1,0:T(8,128)(2,1)} %x_ref.11, bf16[512,4096]{1,0:T(8,128)(2,1)} %cot_ref.11, bf16[512,128]{1,0:T(8,128)(2,1)} %b_ref.11, bf16[512,128]{1,0:T(8,128)(2,1)} %c_ref.11, ...), custom_call_target="tpu_custom_call" | custom-call | flops 1073741824 | bytes 16777216 | tf_op jit(solution)/shard_map/node_outer/pallas_call | solution.py:385
  154.5 0.0 all-to-all-done.1
  154.6 0.0 copy-start.1
  154.6 1.1 copy-done.1
  155.6 0.0 copy-start.8
  155.7 0.0 copy-start.9
  155.7 9.5 %node_outer.3 = (bf16[512,4096]{1,0:T(8,128)(2,1)}, bf16[512,4096]{1,0:T(8,128)(2,1)}, f32[512,128]{1,0:T(8,128)}, f32[512,128]{1,0:T(8,128)}) custom-call(bf16[512,4096]{1,0:T(8,128)(2,1)} %x_ref.11, bf16[512,4096]{1,0:T(8,128)(2,1)} %cot_ref.11, bf16[512,128]{1,0:T(8,128)(2,1)} %b_ref.11, ...), custom_call_target="tpu_custom_call", output_to_operand_aliasing={{0}: (10, {}), {1}: (11, {})} | custom-call | flops 1073741824 | bytes 16777216 | tf_op jit(solution)/shard_map/node_outer/pallas_call | solution.py:385
  165.2 0.0 copy-done.4
  165.2 0.0 copy-done.5
  165.2 0.0 copy-done.6
  165.2 0.0 copy-done.7
  165.2 1.1 add_bitcast_fusion
  166.4 0.1 collective-permute-start
  166.5 1.3 collective-permute-done
  167.8 0.7 slice_bitcast_fusion
  (11 shorter events, 0.1 us)
Async XLA Ops:
  8.2 33.4 %all-to-all-start.2 = ((bf16[16,8,4224]{2,1,0:T(8,128)(2,1)}), bf16[16,8,4224]{2,1,0:T(8,128)(2,1)S(1)}, u32[]{:S(2)}, u32[]{:S(2)}) async-start(bf16[16,8,4224]{2,1,0:T(8,128)(2,1)} %bitcast.18), calls=%async_computation.2 | async-start | bytes 2162688 | tf_op jit(solution)/shard_map/all_to_all | solution.py:434
  41.6 5.9 %copy-start.3 = (bf16[16,8,4224]{2,1,0:T(8,128)(2,1)}, bf16[16,8,4224]{2,1,0:T(8,128)(2,1)S(1)}, u32[]{:S(2)}) copy-start(bf16[16,8,4224]{2,1,0:T(8,128)(2,1)S(1)} %all-to-all-done.2.recv_ref) | copy-start | bytes 3244036
  41.6 29.5 %all-to-all-start = ((bf16[16,8,4224]{2,1,0:T(8,128)(2,1)}), bf16[16,8,4224]{2,1,0:T(8,128)(2,1)S(1)}, u32[]{:S(2)}, u32[]{:S(2)}) async-start(bf16[16,8,4224]{2,1,0:T(8,128)(2,1)} %bitcast.17), calls=%async_computation | async-start | bytes 2162688 | tf_op jit(solution)/shard_map/all_to_all | solution.py:434
  71.1 6.1 %copy-start.2 = (bf16[16,8,4224]{2,1,0:T(8,128)(2,1)}, bf16[16,8,4224]{2,1,0:T(8,128)(2,1)S(1)}, u32[]{:S(2)}) copy-start(bf16[16,8,4224]{2,1,0:T(8,128)(2,1)S(1)} %all-to-all-done.recv_ref) | copy-start | bytes 3244036
  71.1 29.0 %all-to-all-start.3 = ((bf16[16,8,4096]{2,1,0:T(8,128)(2,1)}), bf16[16,8,4096]{2,1,0:T(8,128)(2,1)S(1)}, u32[]{:S(2)}, u32[]{:S(2)}) async-start(bf16[16,8,4096]{2,1,0:T(8,128)(2,1)} %tree_combine.3), calls=%async_computation.3 | async-start | bytes 2097152 | tf_op jit(solution)/shard_map/all_to_all | solution.py:434
  100.1 25.5 %copy-start = (bf16[16,8,4096]{2,1,0:T(8,128)(2,1)}, bf16[16,8,4096]{2,1,0:T(8,128)(2,1)S(1)}, u32[]{:S(2)}) copy-start(bf16[16,8,4096]{2,1,0:T(8,128)(2,1)S(1)} %all-to-all-done.3) | copy-start | bytes 3145732
  100.1 54.5 %all-to-all-start.1 = ((bf16[16,8,4096]{2,1,0:T(8,128)(2,1)}), bf16[16,8,4096]{2,1,0:T(8,128)(2,1)S(1)}, u32[]{:S(2)}, u32[]{:S(2)}) async-start(bf16[16,8,4096]{2,1,0:T(8,128)(2,1)} %tree_combine.2), calls=%async_computation.1 | async-start | bytes 2097152 | tf_op jit(solution)/shard_map/all_to_all | solution.py:434
  154.6 1.1 copy-start.1
  155.6 9.5 %copy-start.4 = (f32[512,128]{1,0:T(8,128)S(1)}, f32[512,128]{1,0:T(8,128)}, u32[]{:S(2)}) copy-start(f32[512,128]{1,0:T(8,128)} %get-tuple-element.52) | copy-start | bytes 786436
  155.6 9.5 %copy-start.5 = (f32[512,128]{1,0:T(8,128)S(1)}, f32[512,128]{1,0:T(8,128)}, u32[]{:S(2)}) copy-start(f32[512,128]{1,0:T(8,128)} %get-tuple-element.48) | copy-start | bytes 786436
  155.6 9.6 %copy-start.6 = (f32[512,128]{1,0:T(8,128)S(1)}, f32[512,128]{1,0:T(8,128)}, u32[]{:S(2)}) copy-start(f32[512,128]{1,0:T(8,128)} %get-tuple-element.53) | copy-start | bytes 786436
  155.6 9.6 %copy-start.7 = (f32[512,128]{1,0:T(8,128)S(1)}, f32[512,128]{1,0:T(8,128)}, u32[]{:S(2)}) copy-start(f32[512,128]{1,0:T(8,128)} %get-tuple-element.49) | copy-start | bytes 786436
  155.6 9.6 %copy-start.8 = (f32[512,128]{1,0:T(8,128)S(1)}, f32[512,128]{1,0:T(8,128)}, u32[]{:S(2)}) copy-start(f32[512,128]{1,0:T(8,128)} %get-tuple-element.54) | copy-start | bytes 786436
  155.7 9.6 %copy-start.9 = (f32[512,128]{1,0:T(8,128)S(1)}, f32[512,128]{1,0:T(8,128)}, u32[]{:S(2)}) copy-start(f32[512,128]{1,0:T(8,128)} %get-tuple-element.50) | copy-start | bytes 786436
  166.4 1.4 collective-permute-start
where the time goes:
time: 170 us; the launch traced here: 169 us
  Pallas kernels  77.3 us (45%)
  waiting for transfers between devices  59.6 us (35%)
  starting transfers between devices  26.5 us (16%)
  local copies, waits for them, and re-layouts  3.16 us (2%)
    all_to_all x4, waiting for transfers between devices, swap(): lax.all_to_all(v.reshape(nodes, rows, v.shape[-1]), 'node', split_axis=0,...  58.3 us
    pallas_call x2, Pallas kernels, node_inner(): pl.pallas_call(functools.partial(inner_kernel, heads, head_width), grid=(...  39 us
    all_to_all x4, starting transfers between devices, swap(): lax.all_to_all(v.reshape(nodes, rows, v.shape[-1]), 'node', split_axis=0,...  26.4 us
    pallas_call x2, Pallas kernels, node_outer(): pl.pallas_call(functools.partial(outer_kernel, heads, head_width, aliased...  18.9 us
    pallas_call x2, Pallas kernels, node_states(): pl.pallas_call(functools.partial(states_kernel, heads, head_width), grid=...  12.4 us
    pallas_call x2, Pallas kernels, combine(): pl.pallas_call(functools.partial(tree_kernel, heads, head_width), in_spec...  6.97 us
  transfers between devices with their start and end apart: 5, of which 4 were waited for; matrix products, arithmetic and copies ran while one was open for 0% of the time, Pallas kernels for 37%

commit v1 on v0

--- a/solution.py
+++ b/solution.py
@@ -11,6 +11,7 @@
 LEVELS = 3
 LANES = 128
 CHUNKS = 2
+PARTS = 2
 
 f32 = jnp.float32
 bf16 = jnp.bfloat16
@@ -22,6 +23,17 @@
     return lax.dot_general(a, b, dims, preferred_element_type=f32)
 
 
+def ordered(kernel, in_specs, operands, after, aliases=None):
+    if after is None:
+        return kernel, in_specs, operands, aliases or {}
+
+    def body(after_ref, *refs):
+        kernel(*refs)
+
+    shifted = {key + 1: value for key, value in (aliases or {}).items()}
+    return body, [pl.BlockSpec(memory_space=pl.ANY)] + in_specs, [after] + operands, shifted
+
+
 def split_two(v):
     high = v.astype(bf16)
     return high, (v - high.astype(f32)).astype(bf16)
@@ -36,6 +48,7 @@
 def states_kernel(
     heads,
     head_width,
+    chunk,
     x_ref,
     cot_ref,
     b_ref,
@@ -58,7 +71,8 @@
     @pl.when(index == 0)
     def _():
         step = step_ref[...]
-        terms = -step * rate_ref[...]
+        rates = jnp.broadcast_to(rate_ref[...], (LANES, rate_ref.shape[1])).T
+        terms = -step * rates[chunk * heads : (chunk + 1) * heads, :1]
         row = lax.broadcasted_iota(jnp.int32, (length, length), 0)
         col = lax.broadcasted_iota(jnp.int32, (length, length), 1)
         upper = (row <= col).astype(bf16)
@@ -97,7 +111,7 @@
     count = width // block
     whole = lambda i: (0, 0)
     return pl.pallas_call(
-        functools.partial(states_kernel, heads, head_width),
+        functools.partial(states_kernel, heads, head_width, chunk),
         grid=(count,),
         in_specs=[
             pl.BlockSpec((length, block), lambda i: (0, chunk * count + i)),
@@ -105,7 +119,7 @@
             pl.BlockSpec((length, state), whole),
             pl.BlockSpec((length, state), whole),
             pl.BlockSpec((heads, length), lambda i: (chunk, 0)),
-            pl.BlockSpec((heads, 1), lambda i: (chunk, 0)),
+            pl.BlockSpec(rate.shape, whole),
         ],
         out_specs=[
             pl.BlockSpec((state, 2 * width + LANES), whole),
@@ -134,21 +148,19 @@
 def inner_kernel(
     heads,
     head_width,
+    first,
+    aliased,
     x_ref,
     cot_ref,
     b_ref,
     c_ref,
     low_ref,
     src_ref,
-    out_ref,
-    grad_ref,
-    gc_ref,
-    gb_ref,
-    gram_ref,
-    mixed_ref,
-    wa_ref,
-    wb_ref,
+    *refs,
 ):
+    if aliased:
+        refs = refs[2:]
+    out_ref, grad_ref, gc_ref, gb_ref, gram_ref, mixed_ref, wa_ref, wb_ref = refs
     length = x_ref.shape[0]
     index = pl.program_id(0)
     pack = LANES // head_width
@@ -170,11 +182,11 @@
     x = x_ref[...]
     cot = cot_ref[...]
     cots = [jnp.where(lane == a, cot, jnp.zeros_like(cot)) for a in range(pack)]
+    place = (first + index) * pack
     columns = [
-        jnp.broadcast_to(low_ref[pl.ds(index * pack + a, 1), :], (LANES, length)).T
-        for a in range(pack)
+        jnp.broadcast_to(low_ref[pl.ds(place + a, 1), :], (LANES, length)).T for a in range(pack)
     ]
-    sources = [src_ref[pl.ds(index * pack + a, 1), :] for a in range(pack)]
+    sources = [src_ref[pl.ds(place + a, 1), :] for a in range(pack)]
     for i in range(blocks):
         rows = slice(i * LANES, (i + 1) * LANES)
         until = (i + 1) * LANES
@@ -214,32 +226,43 @@
         gb_ref[...] = mm(high, c_ref[...]) + mm(low, c_ref[...])
 
 
-def node_inner(x, cot, b, c, low, src, chunk, heads, head_width):
+def node_inner(x, cot, b, c, low, src, prior, after, chunk, part, parts, heads, head_width):
     length, state = b.shape
     width = heads * head_width
-    count = width // LANES
+    count = width // LANES // parts
+    offset = (chunk * parts + part) * count
     whole = lambda i: (0, 0)
-    spot = lambda i: (0, i)
+    place = lambda i: (0, offset + i)
+    aliased = prior is not None
+    operands = [x, cot, b, c, low, src]
+    in_specs = [
+        pl.BlockSpec((length, LANES), place),
+        pl.BlockSpec((length, LANES), place),
+        pl.BlockSpec((length, state), whole),
+        pl.BlockSpec((length, state), whole),
+        pl.BlockSpec((heads, length), whole),
+        pl.BlockSpec((heads, length), whole),
+    ]
+    aliases = {}
+    if aliased:
+        aliases = {len(operands): 0, len(operands) + 1: 1}
+        operands += list(prior)
+        in_specs += [pl.BlockSpec(memory_space=pl.ANY)] * 2
+    kernel = functools.partial(inner_kernel, heads, head_width, part * count, aliased)
+    kernel, in_specs, operands, aliases = ordered(kernel, in_specs, operands, after, aliases)
     return pl.pallas_call(
-        functools.partial(inner_kernel, heads, head_width),
+        kernel,
         grid=(count,),
-        in_specs=[
-            pl.BlockSpec((length, LANES), lambda i: (0, chunk * count + i)),
-            pl.BlockSpec((length, LANES), lambda i: (0, chunk * count + i)),
+        in_specs=in_specs,
+        out_specs=[
+            pl.BlockSpec((length, LANES), place),
+            pl.BlockSpec((length, LANES), place),
             pl.BlockSpec((length, state), whole),
             pl.BlockSpec((length, state), whole),
-            pl.BlockSpec((heads, length), whole),
-            pl.BlockSpec((heads, length), whole),
-        ],
-        out_specs=[
-            pl.BlockSpec((length, LANES), spot),
-            pl.BlockSpec((length, LANES), spot),
-            pl.BlockSpec((length, state), whole),
-            pl.BlockSpec((length, state), whole),
         ],
         out_shape=[
-            jax.ShapeDtypeStruct((length, width), f32),
-            jax.ShapeDtypeStruct((length, width), f32),
+            jax.ShapeDtypeStruct(x.shape, bf16),
+            jax.ShapeDtypeStruct(x.shape, bf16),
             jax.ShapeDtypeStruct((length, state), f32),
             jax.ShapeDtypeStruct((length, state), f32),
         ],
@@ -249,16 +272,19 @@
             pltpu.VMEM((length, length), bf16),
             pltpu.VMEM((length, length), bf16),
         ],
+        input_output_aliases=aliases,
         name="node_inner",
         cost_estimate=pl.CostEstimate(
-            flops=24 * length * length * width,
-            bytes_accessed=12 * length * width,
-            transcendentals=length * length * heads,
+            flops=24 * length * length * count * LANES,
+            bytes_accessed=12 * length * count * LANES,
+            transcendentals=length * length * heads // parts,
         ),
-    )(x, cot, b, c, low, src)
-
-
-def tree_kernel(heads, head_width, parents_ref, recv_ref, out_ref, decay_ref, back_ref):
+    )(*operands)
+
+
+def tree_kernel(
+    heads, head_width, parents_ref, recv_ref, out_ref, token_ref, decay_ref, back_ref
+):
     nodes, rows = recv_ref.shape[:2]
     width = heads * head_width
     totals = recv_ref[:, :, 2 * width :].astype(f32).reshape(nodes * rows, LANES).astype(bf16)
@@ -287,19 +313,29 @@
 
     lax.fori_loop(0, nodes, visit, 0)
     out_ref[:, :, width:] = back_ref[...].astype(bf16)
-
-
-def combine(parents, recv, heads, head_width):
+    token_ref[...] = jnp.zeros_like(token_ref)
+
+
+def combine(parents, recv, after, heads, head_width):
     nodes, rows, _ = recv.shape
     width = heads * head_width
+    in_specs = [
+        pl.BlockSpec(memory_space=pltpu.SMEM),
+        pl.BlockSpec(memory_space=pltpu.VMEM),
+    ]
+    kernel = functools.partial(tree_kernel, heads, head_width)
+    kernel, in_specs, operands, _ = ordered(kernel, in_specs, [parents, recv], after)
     return pl.pallas_call(
-        functools.partial(tree_kernel, heads, head_width),
-        in_specs=[
-            pl.BlockSpec(memory_space=pltpu.SMEM),
+        kernel,
+        in_specs=in_specs,
+        out_specs=[
             pl.BlockSpec(memory_space=pltpu.VMEM),
-        ],
-        out_specs=pl.BlockSpec(memory_space=pltpu.VMEM),
-        out_shape=jax.ShapeDtypeStruct((nodes, rows, 2 * width), bf16),
+            pl.BlockSpec(memory_space=pltpu.VMEM),
+        ],
+        out_shape=[
+            jax.ShapeDtypeStruct((nodes, rows, 2 * width), bf16),
+            jax.ShapeDtypeStruct((8, LANES), f32),
+        ],
         scratch_shapes=[
             pltpu.VMEM((nodes, rows, width), f32),
             pltpu.VMEM((nodes, rows, width), f32),
@@ -310,7 +346,7 @@
             bytes_accessed=8 * nodes * rows * width,
             transcendentals=0,
         ),
-    )(parents, recv)
+    )(*operands)
 
 
 def outer_kernel(
@@ -337,8 +373,8 @@
     tail_wide = mm(tail_ref[...], spread)
     start = start_ref[...]
     back = back_ref[...]
-    out_ref[...] = (inner_ref[...] + grow_wide * mm(c_ref[...], start)).astype(bf16)
-    gx_ref[...] = (grad_ref[...] + tail_wide * mm(b_ref[...], back)).astype(bf16)
+    out_ref[...] = (inner_ref[...].astype(f32) + grow_wide * mm(c_ref[...], start)).astype(bf16)
+    gx_ref[...] = (grad_ref[...].astype(f32) + tail_wide * mm(b_ref[...], back)).astype(bf16)
     emitted = (grow_wide * cot_ref[...].astype(f32)).astype(bf16)
     tailed = (tail_wide * x_ref[...].astype(f32)).astype(bf16)
     gc = mm(emitted, start, NT)
@@ -374,8 +410,8 @@
         pl.BlockSpec((length, 2 * heads), whole),
         pl.BlockSpec((state, block), spot),
         pl.BlockSpec((state, block), lambda i: (0, count + i)),
-        pl.BlockSpec((length, block), spot),
-        pl.BlockSpec((length, block), spot),
+        pl.BlockSpec((length, block), place),
+        pl.BlockSpec((length, block), place),
     ]
     aliases = {}
     if aliased:
@@ -428,7 +464,7 @@
     nodes = lax.axis_size("node")
     heads = head_count // CHUNKS
     rows = state // nodes
-    rate = decay_rate[:, None]
+    rate = decay_rate[None, :]
 
     def swap(v):
         moved = lax.all_to_all(
@@ -436,44 +472,35 @@
         )
         return moved
 
-    chunks = range(CHUNKS)
-    made = [
-        node_states(
-            inputs, cotangent, b_matrix, c_matrix, step_size, rate, k, heads, head_width
+    shared = (inputs, cotangent, b_matrix, c_matrix)
+    sizes = (heads, head_width)
+    made = [node_states(*shared, step_size, rate, k, *sizes) for k in range(CHUNKS)]
+    received = [swap(made[k][0]) for k in range(CHUNKS)]
+    prior = None
+    token = made[CHUNKS - 1][1]
+    grad_c = grad_b = 0.0
+    waiting = list(range(CHUNKS))
+    states = []
+    for k in range(CHUNKS):
+        for part in range(PARTS):
+            *prior, gc, gb = node_inner(
+                *shared, made[k][1], made[k][2], prior, token, k, part, PARTS, *sizes
+            )
+            token = gc
+            grad_c += gc
+            grad_b += gb
+            if waiting:
+                which = waiting.pop(0)
+                joined, token = combine(parents, received[which], token, *sizes)
+                states.append(swap(joined).reshape(state, -1))
+    inner = prior
+    prior = None
+    for k in range(CHUNKS):
+        *prior, gc, gb = node_outer(
+            *shared, made[k][3], made[k][4], states[k], *inner, prior, k, *sizes
         )
-        for k in chunks
-    ]
-    received = [swap(made[k][0]) for k in chunks]
-    inner = [
-        node_inner(
-            inputs, cotangent, b_matrix, c_matrix, made[k][1], made[k][2], k, heads, head_width
-        )
-        for k in chunks
-    ]
-    joined = [combine(parents, received[k], heads, head_width) for k in chunks]
-    states = [swap(joined[k]).reshape(state, -1) for k in chunks]
-    prior = None
-    grad_c = sum(inner[k][2] for k in chunks)
-    grad_b = sum(inner[k][3] for k in chunks)
-    for k in chunks:
-        result = node_outer(
-            inputs,
-            cotangent,
-            b_matrix,
-            c_matrix,
-            made[k][3],
-            made[k][4],
-            states[k],
-            inner[k][0],
-            inner[k][1],
-            prior,
-            k,
-            heads,
-            head_width,
-        )
-        prior = result[:2]
-        grad_c = grad_c + result[2]
-        grad_b = grad_b + result[3]
+        grad_c += gc
+        grad_b += gb
     grads = scatter_sum(jnp.stack([grad_b, grad_c]))
     return prior[0], prior[1], grads[0], grads[1]
 

time: 170 us -> 150 us (0.88)
  waiting for transfers between devices: 59.6 us -> 38 us
  Pallas kernels: 77.3 us -> 79.7 us
    all_to_all x4, waiting for transfers between devices: 58.3 us -> 36.7 us  [swap(): lax.all_to_all(v.reshape(nodes, rows, v.shape[-1]), 'node', split_axis=0,...]
    pallas_call x6 -> x8, Pallas kernels: 58.4 us -> 62.7 us  [the longest x4 43.2 us: node_inner(): pl.pallas_call(kernel, grid=(count,), in_specs=in_specs, out_specs=[pl.Bl...]
    pallas_call x2, Pallas kernels: 18.9 us -> 17 us  [node_outer(): pl.pallas_call(functools.partial(outer_kernel, heads, head_width, aliased...]
  transfers between devices with their start and end apart: 5 -> 5, of which waited for: 4 -> 4; matrix products, arithmetic and copies ran while one was open for 0% -> 0% of each run, Pallas kernels for 37% -> 44%
where the time goes in v1:
time: 150 us; the launch traced here: 148 us
  Pallas kernels  79.7 us (53%)
  waiting for transfers between devices  38 us (25%)
  starting transfers between devices  26.5 us (18%)
  local copies, waits for them, and re-layouts  1.78 us (1%)
    pallas_call x4, Pallas kernels, node_inner(): pl.pallas_call(kernel, grid=(count,), in_specs=in_specs, out_specs=[pl.Bl...  43.2 us
    all_to_all x4, waiting for transfers between devices, swap(): lax.all_to_all(v.reshape(nodes, rows, v.shape[-1]), 'node', split_axis=0,...  36.7 us
    all_to_all x4, starting transfers between devices, swap(): lax.all_to_all(v.reshape(nodes, rows, v.shape[-1]), 'node', split_axis=0,...  26.4 us
    pallas_call x2, Pallas kernels, node_outer(): pl.pallas_call(functools.partial(outer_kernel, heads, head_width, aliased...  17 us
    pallas_call x2, Pallas kernels, node_states(): pl.pallas_call(functools.partial(states_kernel, heads, head_width, chunk)...  12.5 us
    pallas_call x2, Pallas kernels, combine(): pl.pallas_call(kernel, in_specs=in_specs, out_specs=[pl.BlockSpec(memory_...  6.98 us
  transfers between devices with their start and end apart: 5, of which 4 were waited for; matrix products, arithmetic and copies ran while one was open for 0% of the time, Pallas kernels for 44%

profile of v1, /device:TPU:0, one launch (start us, length us, event | category | flops | bytes accessed | tf_op | source)
XLA Modules:
  0.0 148.1 jit_solution(18028066836854249143)
XLA Ops:
  0.6 6.3 %node_states.3 = (bf16[128,4224]{1,0:T(8,128)(2,1)}, f32[32,512]{1,0:T(8,128)}, f32[32,512]{1,0:T(8,128)}, bf16[512,64]{1,0:T(8,128)(2,1)}, bf16[512,64]{1,0:T(8,128)(2,1)}) custom-call(bf16[512,4096]{1,0:T(8,128)(2,1)} %x_ref.7, bf16[512,4096]{1,0:T(8,128)(2,1)} %cot_ref.7, bf16[512,128]{1,0:T(8,128)(2,1)} %b_ref.7, bf16[512,128]{1,0:T(8,128)(2,1)} %c_ref.7, ...), custom_call_target="tpu_custom_call" | custom-call | flops 536870912 | bytes 5242880 | tf_op jit(solution)/shard_map/node_states/pallas_call | solution.py:113
  6.9 8.4 %all-to-all-start = ((bf16[16,8,4224]{2,1,0:T(8,128)(2,1)}), bf16[16,8,4224]{2,1,0:T(8,128)(2,1)S(1)}, u32[]{:S(2)}, u32[]{:S(2)}) async-start(bf16[16,8,4224]{2,1,0:T(8,128)(2,1)} %bitcast.18), calls=%async_computation | async-start | bytes 2162688 | tf_op jit(solution)/shard_map/all_to_all | solution.py:470
  15.3 6.3 %node_states.2 = (bf16[128,4224]{1,0:T(8,128)(2,1)}, f32[32,512]{1,0:T(8,128)}, f32[32,512]{1,0:T(8,128)}, bf16[512,64]{1,0:T(8,128)(2,1)}, bf16[512,64]{1,0:T(8,128)(2,1)}) custom-call(bf16[512,4096]{1,0:T(8,128)(2,1)} %x_ref.7, bf16[512,4096]{1,0:T(8,128)(2,1)} %cot_ref.7, bf16[512,128]{1,0:T(8,128)(2,1)} %b_ref.7, bf16[512,128]{1,0:T(8,128)(2,1)} %c_ref.7, ...), custom_call_target="tpu_custom_call" | custom-call | flops 536870912 | bytes 5242880 | tf_op jit(solution)/shard_map/node_states/pallas_call | solution.py:113
  21.5 18.8 %all-to-all-done.refs_1_ = bf16[16,8,4224]{2,1,0:T(8,128)(2,1)S(1)} async-done(((bf16[16,8,4224]{2,1,0:T(8,128)(2,1)}), bf16[16,8,4224]{2,1,0:T(8,128)(2,1)S(1)}, u32[]{:S(2)}, u32[]{:S(2)}) %all-to-all-start) | async-done | bytes 1081376 | tf_op jit(solution)/shard_map/all_to_all | solution.py:470
  40.3 5.9 %all-to-all-start.1 = ((bf16[16,8,4224]{2,1,0:T(8,128)(2,1)}), bf16[16,8,4224]{2,1,0:T(8,128)(2,1)S(1)}, u32[]{:S(2)}, u32[]{:S(2)}) async-start(bf16[16,8,4224]{2,1,0:T(8,128)(2,1)} %bitcast.17), calls=%async_computation.1 | async-start | bytes 2162688 | tf_op jit(solution)/shard_map/all_to_all | solution.py:470
  46.2 10.8 %node_inner.4 = (bf16[512,4096]{1,0:T(8,128)(2,1)}, bf16[512,4096]{1,0:T(8,128)(2,1)}, f32[512,128]{1,0:T(8,128)}, f32[512,128]{1,0:T(8,128)}) custom-call(f32[32,512]{1,0:T(8,128)} %get-tuple-element.44.after_ref.refs_4_, bf16[512,4096]{1,0:T(8,128)(2,1)} %x_ref.7, bf16[512,4096]{1,0:T(8,128)(2,1)} %cot_ref.7, bf16[512,128]{1,0:T(8,128)(2,1)} %b_ref.7, ...), custom_call_target="tpu_custom_call" | custom-call | flops 6442450944 | bytes 6291456 | tf_op jit(solution)/shard_map/node_inner/pallas_call | solution.py:253
  57.0 0.0 copy-done.3
  57.0 3.5 %tree_combine.2 = (bf16[16,8,4096]{2,1,0:T(8,128)(2,1)}, f32[8,128]{1,0:T(8,128)}) custom-call(f32[512,128]{1,0:T(8,128)} %get-tuple-element.47.after_ref, s32[16]{0:T(128)} %refs_0_.9, bf16[16,8,4224]{2,1,0:T(8,128)(2,1)} %copy-done.3), custom_call_target="tpu_custom_call" | custom-call | flops 5242880 | bytes 2097152 | tf_op jit(solution)/shard_map/tree_combine/pallas_call | solution.py:328
  60.5 9.3 %all-to-all-done.1.refs_1_ = bf16[16,8,4224]{2,1,0:T(8,128)(2,1)S(1)} async-done(((bf16[16,8,4224]{2,1,0:T(8,128)(2,1)}), bf16[16,8,4224]{2,1,0:T(8,128)(2,1)S(1)}, u32[]{:S(2)}, u32[]{:S(2)}) %all-to-all-start.1) | async-done | bytes 1081376 | tf_op jit(solution)/shard_map/all_to_all | solution.py:470
  69.8 6.1 %all-to-all-start.3 = ((bf16[16,8,4096]{2,1,0:T(8,128)(2,1)}), bf16[16,8,4096]{2,1,0:T(8,128)(2,1)S(1)}, u32[]{:S(2)}, u32[]{:S(2)}) async-start(bf16[16,8,4096]{2,1,0:T(8,128)(2,1)} %get-tuple-element.66), calls=%async_computation.3 | async-start | bytes 2097152 | tf_op jit(solution)/shard_map/all_to_all | solution.py:470
  75.9 10.8 %node_inner.5 = (bf16[512,4096]{1,0:T(8,128)(2,1)}, bf16[512,4096]{1,0:T(8,128)(2,1)}, f32[512,128]{1,0:T(8,128)}, f32[512,128]{1,0:T(8,128)}) custom-call(f32[8,128]{1,0:T(8,128)} %get-tuple-element.49.after_ref, bf16[512,4096]{1,0:T(8,128)(2,1)} %x_ref.7, bf16[512,4096]{1,0:T(8,128)(2,1)} %cot_ref.7, ...), custom_call_target="tpu_custom_call", output_to_operand_aliasing={{0}: (7, {}), {1}: (8, {})} | custom-call | flops 6442450944 | bytes 6291456 | tf_op jit(solution)/shard_map/node_inner/pallas_call | solution.py:253
  86.7 0.0 copy-done.2
  86.7 3.5 %tree_combine.3 = (bf16[16,8,4096]{2,1,0:T(8,128)(2,1)}, f32[8,128]{1,0:T(8,128)}) custom-call(f32[512,128]{1,0:T(8,128)} %get-tuple-element.52.after_ref, s32[16]{0:T(128)} %refs_0_.9, bf16[16,8,4224]{2,1,0:T(8,128)(2,1)} %copy-done.2), custom_call_target="tpu_custom_call" | custom-call | flops 5242880 | bytes 2097152 | tf_op jit(solution)/shard_map/tree_combine/pallas_call | solution.py:328
  90.2 8.6 %all-to-all-done.3 = bf16[16,8,4096]{2,1,0:T(8,128)(2,1)S(1)} async-done(((bf16[16,8,4096]{2,1,0:T(8,128)(2,1)}), bf16[16,8,4096]{2,1,0:T(8,128)(2,1)S(1)}, u32[]{:S(2)}, u32[]{:S(2)}) %all-to-all-start.3) | async-done | bytes 1048608 | tf_op jit(solution)/shard_map/all_to_all | solution.py:470
  98.8 6.0 %all-to-all-start.2 = ((bf16[16,8,4096]{2,1,0:T(8,128)(2,1)}), bf16[16,8,4096]{2,1,0:T(8,128)(2,1)S(1)}, u32[]{:S(2)}, u32[]{:S(2)}) async-start(bf16[16,8,4096]{2,1,0:T(8,128)(2,1)} %get-tuple-element.54), calls=%async_computation.2 | async-start | bytes 2097152 | tf_op jit(solution)/shard_map/all_to_all | solution.py:470
  104.9 10.8 %node_inner.6 = (bf16[512,4096]{1,0:T(8,128)(2,1)}, bf16[512,4096]{1,0:T(8,128)(2,1)}, f32[512,128]{1,0:T(8,128)}, f32[512,128]{1,0:T(8,128)}) custom-call(f32[8,128]{1,0:T(8,128)} %get-tuple-element.55.after_ref, bf16[512,4096]{1,0:T(8,128)(2,1)} %x_ref.7, bf16[512,4096]{1,0:T(8,128)(2,1)} %cot_ref.7, ...), custom_call_target="tpu_custom_call", output_to_operand_aliasing={{0}: (7, {}), {1}: (8, {})} | custom-call | flops 6442450944 | bytes 6291456 | tf_op jit(solution)/shard_map/node_inner/pallas_call | solution.py:253
  115.7 0.0 copy-done
  115.7 10.8 %node_inner.7 = (bf16[512,4096]{1,0:T(8,128)(2,1)}, bf16[512,4096]{1,0:T(8,128)(2,1)}, f32[512,128]{1,0:T(8,128)}, f32[512,128]{1,0:T(8,128)}) custom-call(f32[512,128]{1,0:T(8,128)} %get-tuple-element.59.after_ref, bf16[512,4096]{1,0:T(8,128)(2,1)} %x_ref.7, bf16[512,4096]{1,0:T(8,128)(2,1)} %cot_ref.7, ...), custom_call_target="tpu_custom_call", output_to_operand_aliasing={{0}: (7, {}), {1}: (8, {})} | custom-call | flops 6442450944 | bytes 6291456 | tf_op jit(solution)/shard_map/node_inner/pallas_call | solution.py:253
  126.5 8.4 %node_outer.2 = (bf16[512,4096]{1,0:T(8,128)(2,1)}, bf16[512,4096]{1,0:T(8,128)(2,1)}, f32[512,128]{1,0:T(8,128)}, f32[512,128]{1,0:T(8,128)}) custom-call(bf16[512,4096]{1,0:T(8,128)(2,1)} %x_ref.7, bf16[512,4096]{1,0:T(8,128)(2,1)} %cot_ref.7, bf16[512,128]{1,0:T(8,128)(2,1)} %b_ref.7, bf16[512,128]{1,0:T(8,128)(2,1)} %c_ref.7, ...), custom_call_target="tpu_custom_call" | custom-call | flops 1073741824 | bytes 16777216 | tf_op jit(solution)/shard_map/node_outer/pallas_call | solution.py:421
  134.9 0.0 all-to-all-done.2
  134.9 0.0 copy-start.1
  134.9 1.0 copy-done.1
  136.0 0.0 copy-start.8
  136.0 0.0 copy-start.9
  136.0 0.0 copy-start.10
  136.0 0.0 copy-start.11
  136.0 0.0 copy-start.12
  136.0 8.6 %node_outer.3 = (bf16[512,4096]{1,0:T(8,128)(2,1)}, bf16[512,4096]{1,0:T(8,128)(2,1)}, f32[512,128]{1,0:T(8,128)}, f32[512,128]{1,0:T(8,128)}) custom-call(bf16[512,4096]{1,0:T(8,128)(2,1)} %x_ref.7, bf16[512,4096]{1,0:T(8,128)(2,1)} %cot_ref.7, bf16[512,128]{1,0:T(8,128)(2,1)} %b_ref.7, ...), custom_call_target="tpu_custom_call", output_to_operand_aliasing={{0}: (10, {}), {1}: (11, {})} | custom-call | flops 1073741824 | bytes 16777216 | tf_op jit(solution)/shard_map/node_outer/pallas_call | solution.py:421
  144.7 1.3 add_bitcast_fusion
  146.0 0.1 collective-permute-start
  146.1 1.3 collective-permute-done
  147.4 0.7 slice_bitcast_fusion
  (18 shorter events, 0.1 us)
Async XLA Ops:
  6.9 33.4 %all-to-all-start = ((bf16[16,8,4224]{2,1,0:T(8,128)(2,1)}), bf16[16,8,4224]{2,1,0:T(8,128)(2,1)S(1)}, u32[]{:S(2)}, u32[]{:S(2)}) async-start(bf16[16,8,4224]{2,1,0:T(8,128)(2,1)} %bitcast.18), calls=%async_computation | async-start | bytes 2162688 | tf_op jit(solution)/shard_map/all_to_all | solution.py:470
  40.3 16.7 %copy-start.3 = (bf16[16,8,4224]{2,1,0:T(8,128)(2,1)}, bf16[16,8,4224]{2,1,0:T(8,128)(2,1)S(1)}, u32[]{:S(2)}) copy-start(bf16[16,8,4224]{2,1,0:T(8,128)(2,1)S(1)} %all-to-all-done.refs_1_) | copy-start | bytes 3244036
  40.3 29.5 %all-to-all-start.1 = ((bf16[16,8,4224]{2,1,0:T(8,128)(2,1)}), bf16[16,8,4224]{2,1,0:T(8,128)(2,1)S(1)}, u32[]{:S(2)}, u32[]{:S(2)}) async-start(bf16[16,8,4224]{2,1,0:T(8,128)(2,1)} %bitcast.17), calls=%async_computation.1 | async-start | bytes 2162688 | tf_op jit(solution)/shard_map/all_to_all | solution.py:470
  69.8 16.9 %copy-start.2 = (bf16[16,8,4224]{2,1,0:T(8,128)(2,1)}, bf16[16,8,4224]{2,1,0:T(8,128)(2,1)S(1)}, u32[]{:S(2)}) copy-start(bf16[16,8,4224]{2,1,0:T(8,128)(2,1)S(1)} %all-to-all-done.1.refs_1_) | copy-start | bytes 3244036
  69.8 29.0 %all-to-all-start.3 = ((bf16[16,8,4096]{2,1,0:T(8,128)(2,1)}), bf16[16,8,4096]{2,1,0:T(8,128)(2,1)S(1)}, u32[]{:S(2)}, u32[]{:S(2)}) async-start(bf16[16,8,4096]{2,1,0:T(8,128)(2,1)} %get-tuple-element.66), calls=%async_computation.3 | async-start | bytes 2097152 | tf_op jit(solution)/shard_map/all_to_all | solution.py:470
  98.8 16.9 %copy-start = (bf16[16,8,4096]{2,1,0:T(8,128)(2,1)}, bf16[16,8,4096]{2,1,0:T(8,128)(2,1)S(1)}, u32[]{:S(2)}) copy-start(bf16[16,8,4096]{2,1,0:T(8,128)(2,1)S(1)} %all-to-all-done.3) | copy-start | bytes 3145732
  98.8 36.1 %all-to-all-start.2 = ((bf16[16,8,4096]{2,1,0:T(8,128)(2,1)}), bf16[16,8,4096]{2,1,0:T(8,128)(2,1)S(1)}, u32[]{:S(2)}, u32[]{:S(2)}) async-start(bf16[16,8,4096]{2,1,0:T(8,128)(2,1)} %get-tuple-element.54), calls=%async_computation.2 | async-start | bytes 2097152 | tf_op jit(solution)/shard_map/all_to_all | solution.py:470
  134.9 1.0 copy-start.1
  136.0 8.6 %copy-start.4 = (f32[512,128]{1,0:T(8,128)S(1)}, f32[512,128]{1,0:T(8,128)}, u32[]{:S(2)}) copy-start(f32[512,128]{1,0:T(8,128)} %get-tuple-element.47.after_ref) | copy-start | bytes 786436
  136.0 8.6 %copy-start.5 = (f32[512,128]{1,0:T(8,128)S(1)}, f32[512,128]{1,0:T(8,128)}, u32[]{:S(2)}) copy-start(f32[512,128]{1,0:T(8,128)} %get-tuple-element.52.after_ref) | copy-start | bytes 786436
  136.0 8.6 %copy-start.6 = (f32[512,128]{1,0:T(8,128)S(1)}, f32[512,128]{1,0:T(8,128)}, u32[]{:S(2)}) copy-start(f32[512,128]{1,0:T(8,128)} %get-tuple-element.71) | copy-start | bytes 786436
  136.0 8.7 %copy-start.7 = (f32[512,128]{1,0:T(8,128)S(1)}, f32[512,128]{1,0:T(8,128)}, u32[]{:S(2)}) copy-start(f32[512,128]{1,0:T(8,128)} %get-tuple-element.72) | copy-start | bytes 786436
  136.0 8.7 %copy-start.8 = (f32[512,128]{1,0:T(8,128)S(1)}, f32[512,128]{1,0:T(8,128)}, u32[]{:S(2)}) copy-start(f32[512,128]{1,0:T(8,128)} %get-tuple-element.59.after_ref) | copy-start | bytes 786436
  136.0 8.7 %copy-start.9 = (f32[512,128]{1,0:T(8,128)S(1)}, f32[512,128]{1,0:T(8,128)}, u32[]{:S(2)}) copy-start(f32[512,128]{1,0:T(8,128)} %get-tuple-element.73) | copy-start | bytes 786436
  136.0 8.7 %copy-start.10 = (f32[512,128]{1,0:T(8,128)S(1)}, f32[512,128]{1,0:T(8,128)}, u32[]{:S(2)}) copy-start(f32[512,128]{1,0:T(8,128)} %get-tuple-element.77) | copy-start | bytes 786436
  136.0 8.7 %copy-start.11 = (f32[512,128]{1,0:T(8,128)S(1)}, f32[512,128]{1,0:T(8,128)}, u32[]{:S(2)}) copy-start(f32[512,128]{1,0:T(8,128)} %get-tuple-element.74) | copy-start | bytes 786436
  136.0 8.7 %copy-start.12 = (f32[512,128]{1,0:T(8,128)S(1)}, f32[512,128]{1,0:T(8,128)}, u32[]{:S(2)}) copy-start(f32[512,128]{1,0:T(8,128)} %get-tuple-element.78) | copy-start | bytes 786436
  146.0 1.4 collective-permute-start

commit v2 on v1

--- a/solution.py
+++ b/solution.py
@@ -282,68 +282,248 @@
     )(*operands)
 
 
-def tree_kernel(
-    heads, head_width, parents_ref, recv_ref, out_ref, token_ref, decay_ref, back_ref
+def rank_nodes(parents_ref, rank_ref, half):
+    nodes = rank_ref.shape[0]
+
+    def clear(n, carry):
+        rank_ref[n] = 0
+        return carry
+
+    def mark(n, carry):
+        up = parents_ref[n]
+
+        @pl.when(jnp.logical_and(up >= 0, (up >= half) != (n >= half)))
+        def _():
+            rank_ref[up] = 1
+
+        return carry
+
+    def place(n, count):
+        crosses = rank_ref[n]
+        rank_ref[n] = jnp.where(crosses > 0, count, -1)
+        return count + crosses
+
+    lax.fori_loop(0, nodes, clear, 0)
+    lax.fori_loop(0, nodes, mark, 0)
+    lax.fori_loop(0, nodes, place, 0)
+
+
+def widen(narrow, heads, head_width):
+    count, rows = narrow.shape[:2]
+    width = heads * head_width
+    flat = narrow.astype(f32).reshape(count * rows, LANES).astype(bf16)
+    spread = spread_matrix(LANES, LANES, width, head_width, 0)
+    return mm(flat, spread).reshape(count, rows, width)
+
+
+def pack_kernel(
+    heads, head_width, parents_ref, recv_ref, main_ref, more_ref, decay_ref, slot_ref, chain_ref, rank_ref
 ):
-    nodes, rows = recv_ref.shape[:2]
-    width = heads * head_width
-    totals = recv_ref[:, :, 2 * width :].astype(f32).reshape(nodes * rows, LANES).astype(bf16)
-    spread = spread_matrix(LANES, LANES, width, head_width, 0)
-    decay_ref[...] = mm(totals, spread).reshape(nodes, rows, width)
-    back_ref[...] = jnp.zeros_like(back_ref)
-
-    def visit(n, carry):
-        seed = recv_ref[n, :, width : 2 * width].astype(f32)
-        start = jnp.zeros((rows, width), f32)
-        factor = jnp.ones((rows, width), f32)
-        at = n
-        valid = jnp.bool_(True)
+    half = recv_ref.shape[0]
+    width = heads * head_width
+    base = lax.axis_index("node") // half * half
+    rank_nodes(parents_ref, rank_ref, half)
+    decay_ref[...] = widen(recv_ref[:, :, 2 * width :], heads, head_width)
+    slot_ref[...] = jnp.zeros_like(slot_ref)
+    chain_ref[...] = jnp.zeros_like(chain_ref)
+
+    def inside(n):
+        return jnp.logical_and(n >= base, n < base + half)
+
+    def spot(n):
+        return jnp.clip(n - base, 0, half - 1)
+
+    def visit(m, carry):
+        node = base + m
+        flow = recv_ref[m, :, width : 2 * width].astype(f32)
+        at = node
+        live = jnp.bool_(True)
         for level in range(LEVELS):
             up = parents_ref[at]
-            valid = jnp.logical_and(valid, up >= 0)
-            at = jnp.maximum(up, 0)
-            keep = jnp.where(valid, f32(1), f32(0))
-            factor = factor * keep
-            start = start + factor * recv_ref[at, :, :width].astype(f32)
-            back_ref[at] = back_ref[at] + factor * seed
+            exists = jnp.logical_and(live, up >= 0)
+            live = jnp.logical_and(exists, inside(up))
+            away = jnp.logical_and(exists, jnp.logical_not(live))
+
+            @pl.when(away)
+            def _(flow=flow, up=up):
+                slot = rank_ref[up]
+                slot_ref[slot] = slot_ref[slot] + flow
+
             if level < LEVELS - 1:
-                factor = factor * decay_ref[at]
-        out_ref[n, :, :width] = start.astype(bf16)
+                flow = flow * jnp.where(live, decay_ref[spot(up)], 1.0)
+            at = jnp.where(live, up, at)
+
+        @pl.when(rank_ref[node] >= 0)
+        def _():
+            total = recv_ref[m, :, :width].astype(f32)
+            factor = decay_ref[m]
+            chain = recv_ref[m, :, 2 * width :].astype(f32)
+            at = node
+            live = jnp.bool_(True)
+            for level in range(LEVELS - 1):
+                up = parents_ref[at]
+                live = jnp.logical_and(jnp.logical_and(live, up >= 0), inside(up))
+                where = spot(up)
+                total = total + jnp.where(live, factor * recv_ref[where, :, :width].astype(f32), 0.0)
+                factor = factor * jnp.where(live, decay_ref[where], 1.0)
+                chain = chain * jnp.where(live, recv_ref[where, :, 2 * width :].astype(f32), 1.0)
+                at = jnp.where(live, up, at)
+            slot_ref[rank_ref[node]] = total
+            chain_ref[rank_ref[node]] = chain
+
         return carry
 
-    lax.fori_loop(0, nodes, visit, 0)
-    out_ref[:, :, width:] = back_ref[...].astype(bf16)
-    token_ref[...] = jnp.zeros_like(token_ref)
-
-
-def combine(parents, recv, after, heads, head_width):
-    nodes, rows, _ = recv.shape
-    width = heads * head_width
-    in_specs = [
-        pl.BlockSpec(memory_space=pltpu.SMEM),
-        pl.BlockSpec(memory_space=pltpu.VMEM),
-    ]
-    kernel = functools.partial(tree_kernel, heads, head_width)
+    lax.fori_loop(0, half, visit, 0)
+    main = main_ref.shape[0]
+    main_ref[:, :, :width] = slot_ref[:main].astype(bf16)
+    main_ref[:, :, width:] = chain_ref[:main].astype(bf16)
+    more_ref[:, :, :width] = slot_ref[main:].astype(bf16)
+    more_ref[:, :, width:] = chain_ref[main:].astype(bf16)
+
+
+def slot_counts(nodes):
+    most = nodes * LEVELS // (LEVELS + 1)
+    return most // 2, most - most // 2
+
+
+def pack_slots(parents, recv, after, nodes, heads, head_width):
+    half, rows, _ = recv.shape
+    width = heads * head_width
+    main, more = slot_counts(nodes)
+    in_specs = [pl.BlockSpec(memory_space=pltpu.SMEM), pl.BlockSpec(memory_space=pltpu.VMEM)]
+    kernel = functools.partial(pack_kernel, heads, head_width)
     kernel, in_specs, operands, _ = ordered(kernel, in_specs, [parents, recv], after)
     return pl.pallas_call(
         kernel,
         in_specs=in_specs,
-        out_specs=[
-            pl.BlockSpec(memory_space=pltpu.VMEM),
-            pl.BlockSpec(memory_space=pltpu.VMEM),
-        ],
+        out_specs=[pl.BlockSpec(memory_space=pltpu.VMEM)] * 2,
         out_shape=[
-            jax.ShapeDtypeStruct((nodes, rows, 2 * width), bf16),
+            jax.ShapeDtypeStruct((main, rows, width + LANES), bf16),
+            jax.ShapeDtypeStruct((more, rows, width + LANES), bf16),
+        ],
+        scratch_shapes=[
+            pltpu.VMEM((half, rows, width), f32),
+            pltpu.VMEM((main + more, rows, width), f32),
+            pltpu.VMEM((main + more, rows, LANES), f32),
+            pltpu.SMEM((nodes,), jnp.int32),
+        ],
+        name="pack_slots",
+        cost_estimate=pl.CostEstimate(
+            flops=20 * half * rows * width,
+            bytes_accessed=8 * half * rows * width,
+            transcendentals=0,
+        ),
+    )(*operands)
+
+
+def join_kernel(
+    heads,
+    head_width,
+    parents_ref,
+    recv_ref,
+    main_ref,
+    more_ref,
+    out_ref,
+    token_ref,
+    decay_ref,
+    slot_ref,
+    chain_ref,
+    back_ref,
+    rank_ref,
+):
+    half = recv_ref.shape[0]
+    nodes = rank_ref.shape[0]
+    width = heads * head_width
+    main = main_ref.shape[0]
+    base = lax.axis_index("node") // half * half
+    rank_nodes(parents_ref, rank_ref, half)
+    decay_ref[...] = widen(recv_ref[:, :, 2 * width :], heads, head_width)
+    slot_ref[:main] = main_ref[:, :, :width].astype(f32)
+    slot_ref[main:] = more_ref[:, :, :width].astype(f32)
+    chain_ref[:main] = widen(main_ref[:, :, width:], heads, head_width)
+    chain_ref[main:] = widen(more_ref[:, :, width:], heads, head_width)
+    back_ref[...] = jnp.zeros_like(back_ref)
+
+    def inside(n):
+        return jnp.logical_and(n >= base, n < base + half)
+
+    def climb(at, flow, start):
+        factor = None
+        live = jnp.bool_(True)
+        for level in range(LEVELS):
+            up = parents_ref[at]
+            live = jnp.logical_and(live, up >= 0)
+            near = jnp.logical_and(live, inside(up))
+            far = jnp.logical_and(live, jnp.logical_not(near))
+            where = jnp.clip(up - base, 0, half - 1)
+            slot = jnp.where(far, rank_ref[jnp.maximum(up, 0)], 0)
+
+            @pl.when(near)
+            def _(flow=flow, where=where):
+                back_ref[where] = back_ref[where] + flow
+
+            if start is not None:
+                value = jnp.where(near, recv_ref[where, :, :width].astype(f32), slot_ref[slot])
+                value = jnp.where(live, value, 0.0)
+                start = start + (value if factor is None else factor * value)
+            if level < LEVELS - 1:
+                step = jnp.where(near, decay_ref[where], chain_ref[slot])
+                flow = flow * step
+                factor = step if factor is None else factor * step
+                top = jnp.maximum(up, 0)
+                for _ in range(LEVELS - 1):
+                    above = parents_ref[top]
+                    more = jnp.logical_and(far, above >= 0)
+                    more = jnp.logical_and(more, jnp.logical_not(inside(above)))
+                    top = jnp.where(more, above, top)
+                at = top
+        return start
+
+    def visit(m, carry):
+        node = base + m
+        seed = recv_ref[m, :, width : 2 * width].astype(f32)
+        start = climb(node, seed, jnp.zeros(seed.shape, f32))
+        out_ref[m, :, :width] = start.astype(bf16)
+
+        @pl.when(rank_ref[node] >= 0)
+        def _():
+            extra = slot_ref[rank_ref[node]]
+            back_ref[m] = back_ref[m] + extra
+            climb(node, extra * decay_ref[m], None)
+
+        return carry
+
+    lax.fori_loop(0, half, visit, 0)
+    out_ref[:, :, width:] = back_ref[...].astype(bf16)
+    token_ref[...] = jnp.zeros_like(token_ref)
+
+
+def join_slots(parents, recv, main, more, after, nodes, heads, head_width):
+    half, rows, _ = recv.shape
+    width = heads * head_width
+    in_specs = [pl.BlockSpec(memory_space=pltpu.SMEM)] + [pl.BlockSpec(memory_space=pltpu.VMEM)] * 3
+    kernel = functools.partial(join_kernel, heads, head_width)
+    kernel, in_specs, operands, _ = ordered(kernel, in_specs, [parents, recv, main, more], after)
+    slots = main.shape[0] + more.shape[0]
+    return pl.pallas_call(
+        kernel,
+        in_specs=in_specs,
+        out_specs=[pl.BlockSpec(memory_space=pltpu.VMEM)] * 2,
+        out_shape=[
+            jax.ShapeDtypeStruct((half, rows, 2 * width), bf16),
             jax.ShapeDtypeStruct((8, LANES), f32),
         ],
         scratch_shapes=[
-            pltpu.VMEM((nodes, rows, width), f32),
-            pltpu.VMEM((nodes, rows, width), f32),
-        ],
-        name="tree_combine",
+            pltpu.VMEM((half, rows, width), f32),
+            pltpu.VMEM((slots, rows, width), f32),
+            pltpu.VMEM((slots, rows, width), f32),
+            pltpu.VMEM((half, rows, width), f32),
+            pltpu.SMEM((nodes,), jnp.int32),
+        ],
+        name="join_slots",
         cost_estimate=pl.CostEstimate(
-            flops=20 * nodes * rows * width,
-            bytes_accessed=8 * nodes * rows * width,
+            flops=20 * half * rows * width,
+            bytes_accessed=8 * half * rows * width,
             transcendentals=0,
         ),
     )(*operands)
@@ -463,44 +643,75 @@
     head_width = inputs.shape[1] // head_count
     nodes = lax.axis_size("node")
     heads = head_count // CHUNKS
-    rows = state // nodes
+    half = nodes // 2
     rate = decay_rate[None, :]
+    groups = [list(range(half)), list(range(half, nodes))]
+    across = [(n, (n + half) % nodes) for n in range(nodes)]
 
     def swap(v):
-        moved = lax.all_to_all(
-            v.reshape(nodes, rows, v.shape[-1]), "node", split_axis=0, concat_axis=0, tiled=True
+        return lax.all_to_all(
+            v.reshape(half, state // half, v.shape[-1]),
+            "node",
+            split_axis=0,
+            concat_axis=0,
+            tiled=True,
+            axis_index_groups=groups,
         )
-        return moved
+
+    def cross(v):
+        return lax.ppermute(v, "node", across)
+
+    places = jnp.arange(nodes)
+    child = jnp.logical_and(
+        parents[:, None] == places[None, :], (places[:, None] < half) != (places[None, :] < half)
+    )
+    crossing = jnp.sum(jnp.any(child, axis=0).astype(jnp.int32))
+    crowded = crossing > slot_counts(nodes)[0]
 
     shared = (inputs, cotangent, b_matrix, c_matrix)
     sizes = (heads, head_width)
     made = [node_states(*shared, step_size, rate, k, *sizes) for k in range(CHUNKS)]
     received = [swap(made[k][0]) for k in range(CHUNKS)]
+    grads_found = []
     prior = None
     token = made[CHUNKS - 1][1]
-    grad_c = grad_b = 0.0
-    waiting = list(range(CHUNKS))
+
+    def inner_part(prior, token, k, part):
+        *prior, gc, gb = node_inner(
+            *shared, made[k][1], made[k][2], prior, token, k, part, PARTS, *sizes
+        )
+        grads_found.append((gb, gc))
+        return prior, gc
+
+    todo = [(k, part) for k in range(CHUNKS) for part in range(PARTS)]
+    packed = []
+    for k in range(CHUNKS):
+        prior, token = inner_part(prior, token, *todo.pop(0))
+        main, more = pack_slots(parents, received[k], token, nodes, *sizes)
+        packed.append((main, more, cross(main)))
+        token = more
+    others = lax.cond(
+        crowded,
+        lambda vs: tuple(cross(v) for v in vs),
+        lambda vs: vs,
+        tuple(p[1] for p in packed),
+    )
     states = []
     for k in range(CHUNKS):
-        for part in range(PARTS):
-            *prior, gc, gb = node_inner(
-                *shared, made[k][1], made[k][2], prior, token, k, part, PARTS, *sizes
-            )
-            token = gc
-            grad_c += gc
-            grad_b += gb
-            if waiting:
-                which = waiting.pop(0)
-                joined, token = combine(parents, received[which], token, *sizes)
-                states.append(swap(joined).reshape(state, -1))
+        joined, token = join_slots(
+            parents, received[k], packed[k][2], others[k], token, nodes, *sizes
+        )
+        states.append(swap(joined).reshape(state, -1))
+        prior, token = inner_part(prior, token, *todo.pop(0))
     inner = prior
     prior = None
     for k in range(CHUNKS):
         *prior, gc, gb = node_outer(
             *shared, made[k][3], made[k][4], states[k], *inner, prior, k, *sizes
         )
-        grad_c += gc
-        grad_b += gb
+        grads_found.append((gb, gc))
+    grad_b = sum(g[0] for g in grads_found)
+    grad_c = sum(g[1] for g in grads_found)
     grads = scatter_sum(jnp.stack([grad_b, grad_c]))
     return prior[0], prior[1], grads[0], grads[1]
 

time: 150 us -> 147 us (0.980)
  waiting for transfers between devices: 38 us -> 18.8 us
  Pallas kernels: 79.7 us -> 88.8 us
  local copies, waits for them, and re-layouts: 1.78 us -> 5.03 us
  starting transfers between devices: 26.5 us -> 29 us
    all_to_all x4, waiting for transfers between devices: 36.7 us -> 8.77 us  [swap(): lax.all_to_all(v.reshape(half, state // half, v.shape[-1]), 'node', split...]
    pallas_call x2 -> x4, Pallas kernels: 6.98 us -> 16.2 us  [the longest x2 9.28 us: join_slots(): pl.pallas_call(kernel, in_specs=in_specs, out_specs=[pl.BlockSpec(memory_...]
    ppermute x0 -> x2, waiting for transfers between devices: none -> 8.72 us  [cross(): return lax.ppermute(v, 'node', across)]
    ppermute x0 -> x2, starting transfers between devices: none -> 6.12 us  [cross(): return lax.ppermute(v, 'node', across)]
    all_to_all x4, starting transfers between devices: 26.4 us -> 22.8 us  [swap(): lax.all_to_all(v.reshape(half, state // half, v.shape[-1]), 'node', split...]
    unnamed x26 -> x30, local copies, waits for them, and re-layouts: 1.07 us -> 3.54 us
  transfers between devices with their start and end apart: 5 -> 7, of which waited for: 4 -> 4; matrix products, arithmetic and copies ran while one was open for 0% -> 1% of each run, Pallas kernels for 44% -> 48%
where the time goes in v2:
time: 147 us; the launch traced here: 145 us
  Pallas kernels  88.8 us (60%)
  starting transfers between devices  29 us (20%)
  waiting for transfers between devices  18.8 us (13%)
  local copies, waits for them, and re-layouts  5.03 us (3%)
  other arithmetic  2.26 us (2%)
  between operations  1.55 us (1%)
    pallas_call x4, Pallas kernels, node_inner(): pl.pallas_call(kernel, grid=(count,), in_specs=in_specs, out_specs=[pl.Bl...  43.1 us
    all_to_all x4, starting transfers between devices, swap(): lax.all_to_all(v.reshape(half, state // half, v.shape[-1]), 'node', split...  22.8 us
    pallas_call x2, Pallas kernels, node_outer(): pl.pallas_call(functools.partial(outer_kernel, heads, head_width, aliased...  17 us
    pallas_call x2, Pallas kernels, node_states(): pl.pallas_call(functools.partial(states_kernel, heads, head_width, chunk)...  12.6 us
    pallas_call x2, Pallas kernels, join_slots(): pl.pallas_call(kernel, in_specs=in_specs, out_specs=[pl.BlockSpec(memory_...  9.28 us
    all_to_all x4, waiting for transfers between devices, swap(): lax.all_to_all(v.reshape(half, state // half, v.shape[-1]), 'node', split...  8.77 us
    ppermute x2, waiting for transfers between devices, cross(): return lax.ppermute(v, 'node', across)  8.72 us
    pallas_call x2, Pallas kernels, pack_slots(): pl.pallas_call(kernel, in_specs=in_specs, out_specs=[pl.BlockSpec(memory_...  6.89 us
  transfers between devices with their start and end apart: 7, of which 4 were waited for; matrix products, arithmetic and copies ran while one was open for 1% of the time, Pallas kernels for 48%

profile of v2, /device:TPU:0, one launch (start us, length us, event | category | flops | bytes accessed | tf_op | source)
XLA Modules:
  0.0 145.5 jit_solution(474737260652098010)
XLA Ops:
  0.6 6.3 %node_states.3 = (bf16[128,4224]{1,0:T(8,128)(2,1)}, f32[32,512]{1,0:T(8,128)}, f32[32,512]{1,0:T(8,128)}, bf16[512,64]{1,0:T(8,128)(2,1)}, bf16[512,64]{1,0:T(8,128)(2,1)}) custom-call(bf16[512,4096]{1,0:T(8,128)(2,1)} %x_ref.7, bf16[512,4096]{1,0:T(8,128)(2,1)} %cot_ref.7, bf16[512,128]{1,0:T(8,128)(2,1)} %b_ref.7, bf16[512,128]{1,0:T(8,128)(2,1)} %c_ref.7, ...), custom_call_target="tpu_custom_call" | custom-call | flops 536870912 | bytes 5242880 | tf_op jit(solution)/shard_map/node_states/pallas_call | solution.py:113
  6.9 6.2 %all-to-all-start = ((bf16[8,16,4224]{2,1,0:T(8,128)(2,1)}), bf16[8,16,4224]{2,1,0:T(8,128)(2,1)S(1)}, u32[]{:S(2)}, u32[]{:S(2)}) async-start(bf16[8,16,4224]{2,1,0:T(8,128)(2,1)} %bitcast.18), calls=%async_computation | async-start | bytes 2162688 | tf_op jit(solution)/shard_map/all_to_all | solution.py:652
  13.1 6.3 %node_states.2 = (bf16[128,4224]{1,0:T(8,128)(2,1)}, f32[32,512]{1,0:T(8,128)}, f32[32,512]{1,0:T(8,128)}, bf16[512,64]{1,0:T(8,128)(2,1)}, bf16[512,64]{1,0:T(8,128)(2,1)}) custom-call(bf16[512,4096]{1,0:T(8,128)(2,1)} %x_ref.7, bf16[512,4096]{1,0:T(8,128)(2,1)} %cot_ref.7, bf16[512,128]{1,0:T(8,128)(2,1)} %b_ref.7, bf16[512,128]{1,0:T(8,128)(2,1)} %c_ref.7, ...), custom_call_target="tpu_custom_call" | custom-call | flops 536870912 | bytes 5242880 | tf_op jit(solution)/shard_map/node_states/pallas_call | solution.py:113
  19.4 8.8 %all-to-all-done.refs_1_ = bf16[8,16,4224]{2,1,0:T(8,128)(2,1)S(1)} async-done(((bf16[8,16,4224]{2,1,0:T(8,128)(2,1)}), bf16[8,16,4224]{2,1,0:T(8,128)(2,1)S(1)}, u32[]{:S(2)}, u32[]{:S(2)}) %all-to-all-start) | async-done | bytes 1081376 | tf_op jit(solution)/shard_map/all_to_all | solution.py:652
  28.2 3.6 %all-to-all-start.1 = ((bf16[8,16,4224]{2,1,0:T(8,128)(2,1)}), bf16[8,16,4224]{2,1,0:T(8,128)(2,1)S(1)}, u32[]{:S(2)}, u32[]{:S(2)}) async-start(bf16[8,16,4224]{2,1,0:T(8,128)(2,1)} %bitcast.17), calls=%async_computation.1 | async-start | bytes 2162688 | tf_op jit(solution)/shard_map/all_to_all | solution.py:652
  31.8 0.1 fusion.5
  31.9 0.7 convert_reduce_fusion
  33.2 10.8 %node_inner.4 = (bf16[512,4096]{1,0:T(8,128)(2,1)}, bf16[512,4096]{1,0:T(8,128)(2,1)}, f32[512,128]{1,0:T(8,128)}, f32[512,128]{1,0:T(8,128)}) custom-call(f32[32,512]{1,0:T(8,128)} %get-tuple-element.60.after_ref.refs_4_, bf16[512,4096]{1,0:T(8,128)(2,1)} %x_ref.7, bf16[512,4096]{1,0:T(8,128)(2,1)} %cot_ref.7, bf16[512,128]{1,0:T(8,128)(2,1)} %b_ref.7, ...), custom_call_target="tpu_custom_call" | custom-call | flops 6442450944 | bytes 6291456 | tf_op jit(solution)/shard_map/node_inner/pallas_call | solution.py:253
  44.0 3.4 %pack_slots.2 = (bf16[6,16,2176]{2,1,0:T(8,128)(2,1)}, bf16[6,16,2176]{2,1,0:T(8,128)(2,1)S(1)}) custom-call(f32[512,128]{1,0:T(8,128)} %get-tuple-element.63.after_ref, s32[16]{0:T(128)} %refs_0_.14, bf16[8,16,4224]{2,1,0:T(8,128)(2,1)} %copy-done.1), custom_call_target="tpu_custom_call" | custom-call | flops 5242880 | bytes 2097152 | tf_op jit(solution)/shard_map/pack_slots/pallas_call | solution.py:396
  47.5 2.6 %collective-permute-start.2 = (bf16[6,16,2176]{2,1,0:T(8,128)(2,1)}, bf16[6,16,2176]{2,1,0:T(8,128)(2,1)S(1)}, u32[]{:S(2)}, u32[]{:S(2)}) collective-permute-start(bf16[6,16,2176]{2,1,0:T(8,128)(2,1)} %get-tuple-element.71), channel_id=1, source_target_pairs={{0,16},{2,18},{4,20},{6,22},{8,24},{10,26},{12,28},{14,30},{16,0},... | collective-permute-start | bytes 1253384 | tf_op jit(solution)/shard_map/ppermute | solution.py:662
  50.1 10.8 %node_inner.5 = (bf16[512,4096]{1,0:T(8,128)(2,1)}, bf16[512,4096]{1,0:T(8,128)(2,1)}, f32[512,128]{1,0:T(8,128)}, f32[512,128]{1,0:T(8,128)}) custom-call(bf16[6,16,2176]{2,1,0:T(8,128)(2,1)S(1)} %get-tuple-element.65.after_ref, bf16[512,4096]{1,0:T(8,128)(2,1)} %x_ref.7, bf16[512,4096]{1,0:T(8,128)(2,1)} %cot_ref.7, ...), custom_call_target="tpu_custom_call", output_to_operand_aliasing={{0}: (7, {}), {1}: (8, {})} | custom-call | flops 6442450944 | bytes 6291456 | tf_op jit(solution)/shard_map/node_inner/pallas_call | solution.py:253
  60.9 1.0 copy-done
  61.9 3.5 %pack_slots.3 = (bf16[6,16,2176]{2,1,0:T(8,128)(2,1)}, bf16[6,16,2176]{2,1,0:T(8,128)(2,1)S(1)}) custom-call(f32[512,128]{1,0:T(8,128)} %get-tuple-element.68.after_ref, s32[16]{0:T(128)} %refs_0_.14, bf16[8,16,4224]{2,1,0:T(8,128)(2,1)} %copy-done), custom_call_target="tpu_custom_call" | custom-call | flops 5242880 | bytes 2097152 | tf_op jit(solution)/shard_map/pack_slots/pallas_call | solution.py:396
  65.3 0.8 conditional.1
  65.3 0.8 copy.22
  66.1 2.4 %collective-permute-done.2.refs_2_ = bf16[6,16,2176]{2,1,0:T(8,128)(2,1)S(1)} collective-permute-done((bf16[6,16,2176]{2,1,0:T(8,128)(2,1)}, bf16[6,16,2176]{2,1,0:T(8,128)(2,1)S(1)}, u32[]{:S(2)}, u32[]{:S(2)}) %collective-permute-start.2) | collective-permute-done | bytes 417824 | tf_op jit(solution)/shard_map/ppermute | solution.py:662
  68.5 0.7 copy-done.7
  69.3 4.6 %join_slots.2 = (bf16[8,16,4096]{2,1,0:T(8,128)(2,1)}, f32[8,128]{1,0:T(8,128)}) custom-call(bf16[6,16,2176]{2,1,0:T(8,128)(2,1)S(1)} %get-tuple-element.70.after_ref, s32[16]{0:T(128)} %refs_0_.14, bf16[8,16,4224]{2,1,0:T(8,128)(2,1)} %copy-done.1, bf16[6,16,2176]{2,1,0:T(8,128)(2,1)} %copy-done.7, bf16[6,16,2176]{2,1,0:T(8,128)(2,1)S(1)} %get-tuple-element.72.refs_3_), custom_call_target="tpu_custom_call" | custom-call | flops 5242880 | bytes 2097152 | tf_op jit(solution)/shard_map/join_slots/pallas_call | solution.py:508
  73.8 4.2 %all-to-all-start.3 = ((bf16[8,16,4096]{2,1,0:T(8,128)(2,1)}), bf16[8,16,4096]{2,1,0:T(8,128)(2,1)S(1)}, u32[]{:S(2)}, u32[]{:S(2)}) async-start(bf16[8,16,4096]{2,1,0:T(8,128)(2,1)} %get-tuple-element.88), calls=%async_computation.3 | async-start | bytes 2097152 | tf_op jit(solution)/shard_map/all_to_all | solution.py:652
  78.0 3.5 %collective-permute-start.3 = (bf16[6,16,2176]{2,1,0:T(8,128)(2,1)S(1)}, bf16[6,16,2176]{2,1,0:T(8,128)(2,1)S(1)}, u32[]{:S(2)}, u32[]{:S(2)}) collective-permute-start(bf16[6,16,2176]{2,1,0:T(8,128)(2,1)S(1)} %copy-done.14), channel_id=1, source_target_pairs={{0,16},{2,18},{4,20},{6,22},{8,24},{10,26},{12,28},{14,30},{16,0},... | collective-permute-start | bytes 1253384 | tf_op jit(solution)/shard_map/ppermute | solution.py:662
  81.5 10.8 %node_inner.6 = (bf16[512,4096]{1,0:T(8,128)(2,1)}, bf16[512,4096]{1,0:T(8,128)(2,1)}, f32[512,128]{1,0:T(8,128)}, f32[512,128]{1,0:T(8,128)}) custom-call(f32[8,128]{1,0:T(8,128)} %get-tuple-element.73.after_ref, bf16[512,4096]{1,0:T(8,128)(2,1)} %x_ref.7, bf16[512,4096]{1,0:T(8,128)(2,1)} %cot_ref.7, ...), custom_call_target="tpu_custom_call", output_to_operand_aliasing={{0}: (7, {}), {1}: (8, {})} | custom-call | flops 6442450944 | bytes 6291456 | tf_op jit(solution)/shard_map/node_inner/pallas_call | solution.py:253
  92.3 6.3 %collective-permute-done.3.refs_2_ = bf16[6,16,2176]{2,1,0:T(8,128)(2,1)S(1)} collective-permute-done((bf16[6,16,2176]{2,1,0:T(8,128)(2,1)S(1)}, bf16[6,16,2176]{2,1,0:T(8,128)(2,1)S(1)}, u32[]{:S(2)}, u32[]{:S(2)}) %collective-permute-start.3) | collective-permute-done | bytes 417824 | tf_op jit(solution)/shard_map/ppermute | solution.py:662
  98.6 0.8 copy-done.8
  99.3 4.7 %join_slots.3 = (bf16[8,16,4096]{2,1,0:T(8,128)(2,1)}, f32[8,128]{1,0:T(8,128)}) custom-call(f32[512,128]{1,0:T(8,128)} %get-tuple-element.77.after_ref, s32[16]{0:T(128)} %refs_0_.14, bf16[8,16,4224]{2,1,0:T(8,128)(2,1)} %copy-done, bf16[6,16,2176]{2,1,0:T(8,128)(2,1)} %copy-done.8, bf16[6,16,2176]{2,1,0:T(8,128)(2,1)} %get-tuple-element.79.refs_3_), custom_call_target="tpu_custom_call" | custom-call | flops 5242880 | bytes 2097152 | tf_op jit(solution)/shard_map/join_slots/pallas_call | solution.py:508
  104.1 8.9 %all-to-all-start.2 = ((bf16[8,16,4096]{2,1,0:T(8,128)(2,1)}), bf16[8,16,4096]{2,1,0:T(8,128)(2,1)S(1)}, u32[]{:S(2)}, u32[]{:S(2)}) async-start(bf16[8,16,4096]{2,1,0:T(8,128)(2,1)} %get-tuple-element.80), calls=%async_computation.2 | async-start | bytes 2097152 | tf_op jit(solution)/shard_map/all_to_all | solution.py:652
  112.9 10.8 %node_inner.7 = (bf16[512,4096]{1,0:T(8,128)(2,1)}, bf16[512,4096]{1,0:T(8,128)(2,1)}, f32[512,128]{1,0:T(8,128)}, f32[512,128]{1,0:T(8,128)}) custom-call(f32[8,128]{1,0:T(8,128)} %get-tuple-element.81.after_ref, bf16[512,4096]{1,0:T(8,128)(2,1)} %x_ref.7, bf16[512,4096]{1,0:T(8,128)(2,1)} %cot_ref.7, ...), custom_call_target="tpu_custom_call", output_to_operand_aliasing={{0}: (7, {}), {1}: (8, {})} | custom-call | flops 6442450944 | bytes 6291456 | tf_op jit(solution)/shard_map/node_inner/pallas_call | solution.py:253
  123.7 8.4 %node_outer.2 = (bf16[512,4096]{1,0:T(8,128)(2,1)}, bf16[512,4096]{1,0:T(8,128)(2,1)}, f32[512,128]{1,0:T(8,128)}, f32[512,128]{1,0:T(8,128)}) custom-call(bf16[512,4096]{1,0:T(8,128)(2,1)} %x_ref.7, bf16[512,4096]{1,0:T(8,128)(2,1)} %cot_ref.7, bf16[512,128]{1,0:T(8,128)(2,1)} %b_ref.7, bf16[512,128]{1,0:T(8,128)(2,1)} %c_ref.7, ...), custom_call_target="tpu_custom_call" | custom-call | flops 1073741824 | bytes 16777216 | tf_op jit(solution)/shard_map/node_outer/pallas_call | solution.py:601
  132.2 1.0 copy-done.3
  133.2 8.5 %node_outer.3 = (bf16[512,4096]{1,0:T(8,128)(2,1)}, bf16[512,4096]{1,0:T(8,128)(2,1)}, f32[512,128]{1,0:T(8,128)}, f32[512,128]{1,0:T(8,128)}) custom-call(bf16[512,4096]{1,0:T(8,128)(2,1)} %x_ref.7, bf16[512,4096]{1,0:T(8,128)(2,1)} %cot_ref.7, bf16[512,128]{1,0:T(8,128)(2,1)} %b_ref.7, ...), custom_call_target="tpu_custom_call", output_to_operand_aliasing={{0}: (10, {}), {1}: (11, {})} | custom-call | flops 1073741824 | bytes 16777216 | tf_op jit(solution)/shard_map/node_outer/pallas_call | solution.py:601
  141.9 1.4 add_bitcast_fusion
  143.4 1.3 collective-permute-done.4
  144.8 0.7 slice_bitcast_fusion
  (33 shorter events, 0.2 us)
Async XLA Ops:
  6.9 21.3 %all-to-all-start = ((bf16[8,16,4224]{2,1,0:T(8,128)(2,1)}), bf16[8,16,4224]{2,1,0:T(8,128)(2,1)S(1)}, u32[]{:S(2)}, u32[]{:S(2)}) async-start(bf16[8,16,4224]{2,1,0:T(8,128)(2,1)} %bitcast.18), calls=%async_computation | async-start | bytes 2162688 | tf_op jit(solution)/shard_map/all_to_all | solution.py:652
  13.1 18.6 %copy-start.13 = (s32[16]{0:T(128)S(1)}, s32[16]{0:T(128)}, u32[]{:S(2)}) copy-start(s32[16]{0:T(128)} %refs_0_.14) | copy-start | bytes 196
  28.2 15.9 %copy-start.1 = (bf16[8,16,4224]{2,1,0:T(8,128)(2,1)}, bf16[8,16,4224]{2,1,0:T(8,128)(2,1)S(1)}, u32[]{:S(2)}) copy-start(bf16[8,16,4224]{2,1,0:T(8,128)(2,1)S(1)} %all-to-all-done.refs_1_) | copy-start | bytes 3244036
  28.2 32.7 %all-to-all-start.1 = ((bf16[8,16,4224]{2,1,0:T(8,128)(2,1)}), bf16[8,16,4224]{2,1,0:T(8,128)(2,1)S(1)}, u32[]{:S(2)}, u32[]{:S(2)}) async-start(bf16[8,16,4224]{2,1,0:T(8,128)(2,1)} %bitcast.17), calls=%async_computation.1 | async-start | bytes 2162688 | tf_op jit(solution)/shard_map/all_to_all | solution.py:652
  47.5 21.0 %collective-permute-start.2 = (bf16[6,16,2176]{2,1,0:T(8,128)(2,1)}, bf16[6,16,2176]{2,1,0:T(8,128)(2,1)S(1)}, u32[]{:S(2)}, u32[]{:S(2)}) collective-permute-start(bf16[6,16,2176]{2,1,0:T(8,128)(2,1)} %get-tuple-element.71), channel_id=1, source_target_pairs={{0,16},{2,18},{4,20},{6,22},{8,24},{10,26},{12,28},{14,30},{16,0},... | collective-permute-start | bytes 1253384 | tf_op jit(solution)/shard_map/ppermute | solution.py:662
  60.9 1.0 copy-start
  65.3 12.7 %copy-start.14 = (bf16[6,16,2176]{2,1,0:T(8,128)(2,1)S(1)}, bf16[6,16,2176]{2,1,0:T(8,128)(2,1)}, u32[]{:S(2)}) copy-start(bf16[6,16,2176]{2,1,0:T(8,128)(2,1)} %get-tuple-element.78) | copy-start | bytes 1253380
  68.5 0.8 copy-start.7
  73.8 30.2 %all-to-all-start.3 = ((bf16[8,16,4096]{2,1,0:T(8,128)(2,1)}), bf16[8,16,4096]{2,1,0:T(8,128)(2,1)S(1)}, u32[]{:S(2)}, u32[]{:S(2)}) async-start(bf16[8,16,4096]{2,1,0:T(8,128)(2,1)} %get-tuple-element.88), calls=%async_computation.3 | async-start | bytes 2097152 | tf_op jit(solution)/shard_map/all_to_all | solution.py:652
  78.0 20.6 %collective-permute-start.3 = (bf16[6,16,2176]{2,1,0:T(8,128)(2,1)S(1)}, bf16[6,16,2176]{2,1,0:T(8,128)(2,1)S(1)}, u32[]{:S(2)}, u32[]{:S(2)}) collective-permute-start(bf16[6,16,2176]{2,1,0:T(8,128)(2,1)S(1)} %copy-done.14), channel_id=1, source_target_pairs={{0,16},{2,18},{4,20},{6,22},{8,24},{10,26},{12,28},{14,30},{16,0},... | collective-permute-start | bytes 1253384 | tf_op jit(solution)/shard_map/ppermute | solution.py:662
  98.6 0.8 copy-start.8
  104.1 19.7 %copy-start.2 = (bf16[8,16,4096]{2,1,0:T(8,128)(2,1)}, bf16[8,16,4096]{2,1,0:T(8,128)(2,1)S(1)}, u32[]{:S(2)}) copy-start(bf16[8,16,4096]{2,1,0:T(8,128)(2,1)S(1)} %all-to-all-done.3) | copy-start | bytes 3145732
  104.1 28.1 %all-to-all-start.2 = ((bf16[8,16,4096]{2,1,0:T(8,128)(2,1)}), bf16[8,16,4096]{2,1,0:T(8,128)(2,1)S(1)}, u32[]{:S(2)}, u32[]{:S(2)}) async-start(bf16[8,16,4096]{2,1,0:T(8,128)(2,1)} %get-tuple-element.80), calls=%async_computation.2 | async-start | bytes 2097152 | tf_op jit(solution)/shard_map/all_to_all | solution.py:652
  132.2 1.0 copy-start.3
  133.2 8.6 %copy-start.4 = (f32[512,128]{1,0:T(8,128)S(1)}, f32[512,128]{1,0:T(8,128)}, u32[]{:S(2)}) copy-start(f32[512,128]{1,0:T(8,128)} %get-tuple-element.63.after_ref) | copy-start | bytes 786436
  133.2 8.6 %copy-start.5 = (f32[512,128]{1,0:T(8,128)S(1)}, f32[512,128]{1,0:T(8,128)}, u32[]{:S(2)}) copy-start(f32[512,128]{1,0:T(8,128)} %get-tuple-element.68.after_ref) | copy-start | bytes 786436
  133.2 8.6 %copy-start.6 = (f32[512,128]{1,0:T(8,128)S(1)}, f32[512,128]{1,0:T(8,128)}, u32[]{:S(2)}) copy-start(f32[512,128]{1,0:T(8,128)} %get-tuple-element.77.after_ref) | copy-start | bytes 786436
  133.2 8.6 %copy-start.9 = (f32[512,128]{1,0:T(8,128)S(1)}, f32[512,128]{1,0:T(8,128)}, u32[]{:S(2)}) copy-start(f32[512,128]{1,0:T(8,128)} %get-tuple-element.93) | copy-start | bytes 786436
  133.2 8.6 %copy-start.10 = (f32[512,128]{1,0:T(8,128)S(1)}, f32[512,128]{1,0:T(8,128)}, u32[]{:S(2)}) copy-start(f32[512,128]{1,0:T(8,128)} %get-tuple-element.94) | copy-start | bytes 786436
  133.2 8.6 %copy-start.11 = (f32[512,128]{1,0:T(8,128)S(1)}, f32[512,128]{1,0:T(8,128)}, u32[]{:S(2)}) copy-start(f32[512,128]{1,0:T(8,128)} %get-tuple-element.95) | copy-start | bytes 786436
  133.2 8.6 %copy-start.12 = (f32[512,128]{1,0:T(8,128)S(1)}, f32[512,128]{1,0:T(8,128)}, u32[]{:S(2)}) copy-start(f32[512,128]{1,0:T(8,128)} %get-tuple-element.99) | copy-start | bytes 786436
  143.3 1.4 collective-permute-start.4

commit v3 on v2

--- a/solution.py
+++ b/solution.py
@@ -13,6 +13,8 @@
 CHUNKS = 2
 PARTS = 2
 
+LOG2E = 1.0 / math.log(2.0)
+
 f32 = jnp.float32
 bf16 = jnp.bfloat16
 NN = (((1,), (0,)), ((), ()))
@@ -39,10 +41,22 @@
     return high, (v - high.astype(f32)).astype(bf16)
 
 
-def spread_matrix(rows, heads, width, head_width, offset):
-    row = lax.broadcasted_iota(jnp.int32, (rows, width), 0) % heads
-    lane = (lax.broadcasted_iota(jnp.int32, (rows, width), 1) + offset) // head_width
+def spread_matrix(rows, width, head_width):
+    row = lax.broadcasted_iota(jnp.int32, (rows, width), 0)
+    lane = lax.broadcasted_iota(jnp.int32, (rows, width), 1) // head_width
     return (row == lane).astype(bf16)
+
+
+def head_lanes(columns, first, head_width):
+    lane = lax.broadcasted_iota(jnp.int32, columns.shape, 1) // head_width + first
+    return jnp.take_along_axis(columns, lane, axis=1)
+
+
+def pad_lanes(v):
+    gap = LANES - v.shape[0]
+    if gap:
+        v = jnp.concatenate([v, jnp.zeros((gap, v.shape[1]), v.dtype)], axis=0)
+    return v.T
 
 
 def states_kernel(
@@ -60,6 +74,7 @@
     src_ref,
     grow_ref,
     tail_ref,
+    gram_ref,
     bt_ref,
     ct_ref,
 ):
@@ -67,6 +82,7 @@
     length = step_ref.shape[1]
     index = pl.program_id(0)
     width = heads * head_width
+    pack = LANES // head_width
 
     @pl.when(index == 0)
     def _():
@@ -81,27 +97,33 @@
         second, third = split_two(rest)
         cumulative = mm(third, upper) + mm(second, upper) + mm(first, upper)
         last = cumulative[:, length - 1 :]
-        low_ref[...] = cumulative
-        src_ref[...] = cumulative - jnp.log(step)
-        growth = jnp.exp(cumulative)
-        tail = jnp.exp(last - cumulative) * step
-        grow_ref[...] = jnp.concatenate(split_two(growth.T), axis=1)
-        tail_ref[...] = jnp.concatenate(split_two(tail.T), axis=1)
+        low_ref[...] = pad_lanes(cumulative * LOG2E)
+        src_ref[...] = (cumulative - jnp.log(step)) * LOG2E
+        grow_ref[...] = pad_lanes(jnp.exp(cumulative))
+        tail_ref[...] = pad_lanes(jnp.exp(last - cumulative) * step)
         bt_ref[...] = b_ref[...].T
         ct_ref[...] = c_ref[...].T
         total = jnp.exp(jnp.broadcast_to(last, (heads, send_ref.shape[0])))
-        pad = jnp.zeros((LANES - heads, send_ref.shape[0]), f32)
-        totals = jnp.concatenate([total, pad], axis=0).T
-        send_ref[:, 2 * width :] = totals.astype(bf16)
-
-    spread = spread_matrix(2 * heads, heads, block, head_width, index * block)
-    tail_wide = mm(tail_ref[...], spread)
-    grow_wide = mm(grow_ref[...], spread)
-    tailed = (tail_wide * x_ref[...].astype(f32)).astype(bf16)
-    emitted = (grow_wide * cot_ref[...].astype(f32)).astype(bf16)
+        send_ref[:, 2 * width :] = pad_lanes(total).astype(bf16)
+        gram_ref[...] = mm(c_ref[...], b_ref[...], NT).astype(bf16)
+
+    grow = grow_ref[...]
+    tail = tail_ref[...]
+    parts = range(block // LANES)
+    tailed = []
+    emitted = []
+    for q in parts:
+        lanes = slice(q * LANES, (q + 1) * LANES)
+        first = (index * (block // LANES) + q) * pack
+        tail_wide = head_lanes(tail, first, head_width)
+        grow_wide = head_lanes(grow, first, head_width)
+        tailed.append((tail_wide * x_ref[:, lanes].astype(f32)).astype(bf16))
+        emitted.append((grow_wide * cot_ref[:, lanes].astype(f32)).astype(bf16))
     at = pl.multiple_of(index * block, block)
-    send_ref[:, pl.ds(at, block)] = mm(bt_ref[...], tailed).astype(bf16)
-    send_ref[:, pl.ds(at + width, block)] = mm(ct_ref[...], emitted).astype(bf16)
+    send_ref[:, pl.ds(at, block)] = mm(bt_ref[...], jnp.concatenate(tailed, axis=1)).astype(bf16)
+    send_ref[:, pl.ds(at + width, block)] = mm(
+        ct_ref[...], jnp.concatenate(emitted, axis=1)
+    ).astype(bf16)
 
 
 def node_states(x, cot, b, c, step, rate, chunk, heads, head_width):
@@ -123,17 +145,19 @@
         ],
         out_specs=[
             pl.BlockSpec((state, 2 * width + LANES), whole),
+            pl.BlockSpec((length, LANES), whole),
             pl.BlockSpec((heads, length), whole),
-            pl.BlockSpec((heads, length), whole),
-            pl.BlockSpec((length, 2 * heads), whole),
-            pl.BlockSpec((length, 2 * heads), whole),
+            pl.BlockSpec((length, LANES), whole),
+            pl.BlockSpec((length, LANES), whole),
+            pl.BlockSpec((length, length), whole),
         ],
         out_shape=[
             jax.ShapeDtypeStruct((state, 2 * width + LANES), bf16),
+            jax.ShapeDtypeStruct((length, LANES), f32),
             jax.ShapeDtypeStruct((heads, length), f32),
-            jax.ShapeDtypeStruct((heads, length), f32),
-            jax.ShapeDtypeStruct((length, 2 * heads), bf16),
-            jax.ShapeDtypeStruct((length, 2 * heads), bf16),
+            jax.ShapeDtypeStruct((length, LANES), f32),
+            jax.ShapeDtypeStruct((length, LANES), f32),
+            jax.ShapeDtypeStruct((length, length), bf16),
         ],
         scratch_shapes=[pltpu.VMEM((state, length), bf16), pltpu.VMEM((state, length), bf16)],
         name="node_states",
@@ -146,7 +170,6 @@
 
 
 def inner_kernel(
-    heads,
     head_width,
     first,
     aliased,
@@ -154,23 +177,24 @@
     cot_ref,
     b_ref,
     c_ref,
+    gram_ref,
     low_ref,
     src_ref,
     *refs,
 ):
     if aliased:
         refs = refs[2:]
-    out_ref, grad_ref, gc_ref, gb_ref, gram_ref, mixed_ref, wa_ref, wb_ref = refs
+    out_ref, grad_ref, gc_ref, gb_ref, mixed_ref, turned_ref, wa_ref, wb_ref = refs
     length = x_ref.shape[0]
     index = pl.program_id(0)
     pack = LANES // head_width
-    blocks = length // LANES
-    half = length // 2
+    pairs = x_ref.shape[1] // LANES
+    wide = 2 * LANES
+    tiles = length // wide
     weights = (wa_ref, wb_ref)
 
     @pl.when(index == 0)
     def _():
-        gram_ref[...] = mm(c_ref[...], b_ref[...], NT)
         mixed_ref[...] = jnp.zeros_like(mixed_ref)
         for ref in weights:
             ref[...] = jnp.zeros_like(ref)
@@ -179,68 +203,93 @@
     causal = lax.broadcasted_iota(jnp.int32, (LANES, LANES), 0) >= lax.broadcasted_iota(
         jnp.int32, (LANES, LANES), 1
     )
-    x = x_ref[...]
-    cot = cot_ref[...]
-    cots = [jnp.where(lane == a, cot, jnp.zeros_like(cot)) for a in range(pack)]
-    place = (first + index) * pack
-    columns = [
-        jnp.broadcast_to(low_ref[pl.ds(place + a, 1), :], (LANES, length)).T for a in range(pack)
-    ]
-    sources = [src_ref[pl.ds(place + a, 1), :] for a in range(pack)]
-    for i in range(blocks):
-        rows = slice(i * LANES, (i + 1) * LANES)
-        until = (i + 1) * LANES
-        scores = [mm(cots[a][rows], x[:until], NT) for a in range(pack)]
-        for j in range(i + 1):
-            cols = slice(j * LANES, (j + 1) * LANES)
-            gram = gram_ref[rows, cols]
-            mixed = mixed_ref[rows, cols]
-            for a in range(pack):
-                differ = columns[a][rows] - sources[a][:, cols]
-                if i == j:
-                    differ = jnp.where(causal, differ, -jnp.inf)
-                decay = jnp.exp(differ)
-                weights[a][rows, cols] = (decay * gram).astype(bf16)
-                mixed = mixed + decay * scores[a][:, cols]
-            mixed_ref[rows, cols] = mixed
-    cot_turned = cot.T
-    turned = []
-    for a in range(pack):
-        w = weights[a]
-        top = mm(w[:half, :half], x[:half])
-        bottom = mm(w[half:, :], x)
-        both = jnp.concatenate([top, bottom], axis=0)
-        out = both if a == 0 else jnp.where(lane == a, both, out)
-        part = cot_turned[a * head_width : (a + 1) * head_width]
-        left = mm(part, w[:, :half])
-        right = mm(part[:, half:], w[half:, half:])
-        turned.append(jnp.concatenate([left, right], axis=1))
-    out_ref[...] = out.astype(out_ref.dtype)
-    grad_ref[...] = jnp.concatenate(turned, axis=0).T.astype(grad_ref.dtype)
+    xs = [x_ref[:, q * LANES : (q + 1) * LANES] for q in range(pairs)]
+    turned_cots = [cot_ref[:, q * LANES : (q + 1) * LANES].T for q in range(pairs)]
+    low = low_ref[...]
+
+    def decays(h):
+        q, a = h // pack, h % pack
+        w = weights[h % 2]
+        cot = cot_ref[:, q * LANES : (q + 1) * LANES]
+        cot = jnp.where(lane == a, cot, jnp.zeros_like(cot))
+        place = (first + index * pairs + q) * pack + a
+        column = head_lanes(low, place, LANES)
+        source = src_ref[pl.ds(place, 1), :]
+        for tile in range(tiles):
+            scores = mm(cot[tile * wide :], xs[q][tile * wide : (tile + 1) * wide], NT)
+            for i in range(2 * tile, 2 * tiles):
+                rows = slice(i * LANES, (i + 1) * LANES)
+                here = slice((i - 2 * tile) * LANES, (i - 2 * tile + 1) * LANES)
+                for j in range(2 * tile, min(2 * tile + 1, i) + 1):
+                    cols = slice(j * LANES, (j + 1) * LANES)
+                    side = slice((j - 2 * tile) * LANES, (j - 2 * tile + 1) * LANES)
+                    differ = column[rows] - source[:, cols]
+                    if i == j:
+                        differ = jnp.where(causal, differ, -jnp.inf)
+                    decay = jnp.exp2(differ)
+                    w[rows, cols] = decay.astype(bf16) * gram_ref[rows, cols]
+                    mixed_ref[rows, cols] += decay * scores[here, side]
+                yield
+
+    def products(h):
+        q, a = h // pack, h % pack
+        w = weights[h % 2]
+        x = xs[q]
+        part = turned_cots[q][a * head_width : (a + 1) * head_width]
+        mine = slice(q * LANES + a * head_width, q * LANES + (a + 1) * head_width)
+        own = slice(a * head_width, (a + 1) * head_width)
+        for tile in range(tiles):
+            rows = slice(tile * wide, (tile + 1) * wide)
+            found = mm(w[rows, : (tile + 1) * wide], x[: (tile + 1) * wide])
+            out_ref[rows, mine] = found[:, own].astype(bf16)
+            yield
+            found = mm(part[:, tile * wide :], w[tile * wide :, rows])
+            turned_ref[mine, rows] = found.astype(bf16)
+            yield
+
+    def finish(q):
+        lanes = slice(q * LANES, (q + 1) * LANES)
+        grad_ref[:, lanes] = turned_ref[lanes, :].T
+
+    before = None
+    for h in range(pairs * pack):
+        for _ in decays(h):
+            if before is not None:
+                next(before, None)
+        if before is not None:
+            for _ in before:
+                pass
+            if h % pack == 0:
+                finish(h // pack - 1)
+        before = products(h)
+    for _ in before:
+        pass
+    finish(pairs - 1)
 
     @pl.when(index == pl.num_programs(0) - 1)
     def _():
-        high, low = split_two(mixed_ref[...])
-        gc_ref[...] = mm(high, b_ref[...]) + mm(low, b_ref[...])
-        high, low = split_two(mixed_ref[...].T)
-        gb_ref[...] = mm(high, c_ref[...]) + mm(low, c_ref[...])
-
-
-def node_inner(x, cot, b, c, low, src, prior, after, chunk, part, parts, heads, head_width):
+        mixed = mixed_ref[...].astype(bf16)
+        gc_ref[...] = mm(mixed, b_ref[...])
+        gb_ref[...] = mm(mixed.T, c_ref[...])
+
+
+def node_inner(x, cot, b, c, gram, low, src, prior, after, chunk, part, parts, heads, head_width):
     length, state = b.shape
     width = heads * head_width
-    count = width // LANES // parts
+    block = min(width // parts, 2 * LANES)
+    count = width // block // parts
     offset = (chunk * parts + part) * count
     whole = lambda i: (0, 0)
     place = lambda i: (0, offset + i)
     aliased = prior is not None
-    operands = [x, cot, b, c, low, src]
+    operands = [x, cot, b, c, gram, low, src]
     in_specs = [
-        pl.BlockSpec((length, LANES), place),
-        pl.BlockSpec((length, LANES), place),
+        pl.BlockSpec((length, block), place),
+        pl.BlockSpec((length, block), place),
         pl.BlockSpec((length, state), whole),
         pl.BlockSpec((length, state), whole),
-        pl.BlockSpec((heads, length), whole),
+        pl.BlockSpec((length, length), whole),
+        pl.BlockSpec((length, LANES), whole),
         pl.BlockSpec((heads, length), whole),
     ]
     aliases = {}
@@ -248,15 +297,15 @@
         aliases = {len(operands): 0, len(operands) + 1: 1}
         operands += list(prior)
         in_specs += [pl.BlockSpec(memory_space=pl.ANY)] * 2
-    kernel = functools.partial(inner_kernel, heads, head_width, part * count, aliased)
+    kernel = functools.partial(inner_kernel, head_width, part * count * block // LANES, aliased)
     kernel, in_specs, operands, aliases = ordered(kernel, in_specs, operands, after, aliases)
     return pl.pallas_call(
         kernel,
         grid=(count,),
         in_specs=in_specs,
         out_specs=[
-            pl.BlockSpec((length, LANES), place),
-            pl.BlockSpec((length, LANES), place),
+            pl.BlockSpec((length, block), place),
+            pl.BlockSpec((length, block), place),
             pl.BlockSpec((length, state), whole),
             pl.BlockSpec((length, state), whole),
         ],
@@ -268,15 +317,15 @@
         ],
         scratch_shapes=[
             pltpu.VMEM((length, length), f32),
-            pltpu.VMEM((length, length), f32),
+            pltpu.VMEM((block, length), bf16),
             pltpu.VMEM((length, length), bf16),
             pltpu.VMEM((length, length), bf16),
         ],
         input_output_aliases=aliases,
         name="node_inner",
         cost_estimate=pl.CostEstimate(
-            flops=24 * length * length * count * LANES,
-            bytes_accessed=12 * length * count * LANES,
+            flops=24 * length * length * count * block,
+            bytes_accessed=12 * length * count * block,
             transcendentals=length * length * heads // parts,
         ),
     )(*operands)
@@ -309,11 +358,9 @@
 
 
 def widen(narrow, heads, head_width):
-    count, rows = narrow.shape[:2]
-    width = heads * head_width
-    flat = narrow.astype(f32).reshape(count * rows, LANES).astype(bf16)
-    spread = spread_matrix(LANES, LANES, width, head_width, 0)
-    return mm(flat, spread).reshape(count, rows, width)
+    count = narrow.shape[0]
+    flat = jnp.concatenate([narrow[n, :1].astype(f32) for n in range(count)], axis=0)
+    return mm(flat.astype(bf16), spread_matrix(LANES, heads * head_width, head_width))
 
 
 def pack_kernel(
@@ -350,13 +397,13 @@
                 slot_ref[slot] = slot_ref[slot] + flow
 
             if level < LEVELS - 1:
-                flow = flow * jnp.where(live, decay_ref[spot(up)], 1.0)
+                flow = flow * jnp.where(live, decay_ref[pl.ds(spot(up), 1)], 1.0)
             at = jnp.where(live, up, at)
 
         @pl.when(rank_ref[node] >= 0)
         def _():
             total = recv_ref[m, :, :width].astype(f32)
-            factor = decay_ref[m]
+            factor = decay_ref[pl.ds(m, 1)]
             chain = recv_ref[m, :, 2 * width :].astype(f32)
             at = node
             live = jnp.bool_(True)
@@ -365,7 +412,7 @@
                 live = jnp.logical_and(jnp.logical_and(live, up >= 0), inside(up))
                 where = spot(up)
                 total = total + jnp.where(live, factor * recv_ref[where, :, :width].astype(f32), 0.0)
-                factor = factor * jnp.where(live, decay_ref[where], 1.0)
+                factor = factor * jnp.where(live, decay_ref[pl.ds(where, 1)], 1.0)
                 chain = chain * jnp.where(live, recv_ref[where, :, 2 * width :].astype(f32), 1.0)
                 at = jnp.where(live, up, at)
             slot_ref[rank_ref[node]] = total
@@ -402,7 +449,7 @@
             jax.ShapeDtypeStruct((more, rows, width + LANES), bf16),
         ],
         scratch_shapes=[
-            pltpu.VMEM((half, rows, width), f32),
+            pltpu.VMEM((half, width), f32),
             pltpu.VMEM((main + more, rows, width), f32),
             pltpu.VMEM((main + more, rows, LANES), f32),
             pltpu.SMEM((nodes,), jnp.int32),
@@ -467,7 +514,7 @@
                 value = jnp.where(live, value, 0.0)
                 start = start + (value if factor is None else factor * value)
             if level < LEVELS - 1:
-                step = jnp.where(near, decay_ref[where], chain_ref[slot])
+                step = jnp.where(near, decay_ref[pl.ds(where, 1)], chain_ref[pl.ds(slot, 1)])
                 flow = flow * step
                 factor = step if factor is None else factor * step
                 top = jnp.maximum(up, 0)
@@ -489,7 +536,7 @@
         def _():
             extra = slot_ref[rank_ref[node]]
             back_ref[m] = back_ref[m] + extra
-            climb(node, extra * decay_ref[m], None)
+            climb(node, extra * decay_ref[pl.ds(m, 1)], None)
 
         return carry
 
@@ -514,9 +561,9 @@
             jax.ShapeDtypeStruct((8, LANES), f32),
         ],
         scratch_shapes=[
-            pltpu.VMEM((half, rows, width), f32),
+            pltpu.VMEM((half, width), f32),
             pltpu.VMEM((slots, rows, width), f32),
-            pltpu.VMEM((slots, rows, width), f32),
+            pltpu.VMEM((slots, width), f32),
             pltpu.VMEM((half, rows, width), f32),
             pltpu.SMEM((nodes,), jnp.int32),
         ],
@@ -548,9 +595,12 @@
     out_ref, gx_ref, gc_ref, gb_ref = refs[2:] if aliased else refs
     block = x_ref.shape[1]
     index = pl.program_id(0)
-    spread = spread_matrix(2 * heads, heads, block, head_width, index * block)
-    grow_wide = mm(grow_ref[...], spread)
-    tail_wide = mm(tail_ref[...], spread)
+    pack = LANES // head_width
+    firsts = [(index * (block // LANES) + q) * pack for q in range(block // LANES)]
+    grow = grow_ref[...]
+    tail = tail_ref[...]
+    grow_wide = jnp.concatenate([head_lanes(grow, v, head_width) for v in firsts], axis=1)
+    tail_wide = jnp.concatenate([head_lanes(tail, v, head_width) for v in firsts], axis=1)
     start = start_ref[...]
     back = back_ref[...]
     out_ref[...] = (inner_ref[...].astype(f32) + grow_wide * mm(c_ref[...], start)).astype(bf16)
@@ -586,8 +636,8 @@
         pl.BlockSpec((length, block), place),
         pl.BlockSpec((length, state), whole),
         pl.BlockSpec((length, state), whole),
-        pl.BlockSpec((length, 2 * heads), whole),
-        pl.BlockSpec((length, 2 * heads), whole),
+        pl.BlockSpec((length, LANES), whole),
+        pl.BlockSpec((length, LANES), whole),
         pl.BlockSpec((state, block), spot),
         pl.BlockSpec((state, block), lambda i: (0, count + i)),
         pl.BlockSpec((length, block), place),
@@ -678,7 +728,7 @@
 
     def inner_part(prior, token, k, part):
         *prior, gc, gb = node_inner(
-            *shared, made[k][1], made[k][2], prior, token, k, part, PARTS, *sizes
+            *shared, made[0][5], made[k][1], made[k][2], prior, token, k, part, PARTS, *sizes
         )
         grads_found.append((gb, gc))
         return prior, gc

time: 147 us -> 143 us (0.973)
  Pallas kernels: 88.8 us -> 82 us
  waiting for transfers between devices: 18.8 us -> 22.5 us
    pallas_call x4, Pallas kernels: 43.1 us -> 35 us  [node_inner(): pl.pallas_call(kernel, grid=(count,), in_specs=in_specs, out_specs=[pl.Bl...]
    ppermute x2, waiting for transfers between devices: 8.72 us -> 13.2 us  [cross(): return lax.ppermute(v, 'node', across)]
    pallas_call x2, Pallas kernels: 12.6 us -> 14.1 us  [node_states(): pl.pallas_call(functools.partial(states_kernel, heads, head_width, chunk)...]
  transfers between devices with their start and end apart: 7 -> 7, of which waited for: 4 -> 4; matrix products, arithmetic and copies ran while one was open for 1% -> 1% of each run, Pallas kernels for 48% -> 44%
where the time goes in v3:
time: 143 us; the launch traced here: 142 us
  Pallas kernels  82 us (57%)
  starting transfers between devices  28.6 us (20%)
  waiting for transfers between devices  22.5 us (16%)
  local copies, waits for them, and re-layouts  5.05 us (4%)
  other arithmetic  2.22 us (2%)
  between operations  1.51 us (1%)
    pallas_call x4, Pallas kernels, node_inner(): pl.pallas_call(kernel, grid=(count,), in_specs=in_specs, out_specs=[pl.Bl...  35 us
    all_to_all x4, starting transfers between devices, swap(): lax.all_to_all(v.reshape(half, state // half, v.shape[-1]), 'node', split...  22.6 us
    pallas_call x2, Pallas kernels, node_outer(): pl.pallas_call(functools.partial(outer_kernel, heads, head_width, aliased...  17.6 us
    pallas_call x2, Pallas kernels, node_states(): pl.pallas_call(functools.partial(states_kernel, heads, head_width, chunk)...  14.1 us
    ppermute x2, waiting for transfers between devices, cross(): return lax.ppermute(v, 'node', across)  13.2 us
    pallas_call x2, Pallas kernels, join_slots(): pl.pallas_call(kernel, in_specs=in_specs, out_specs=[pl.BlockSpec(memory_...  8.78 us
    all_to_all x4, waiting for transfers between devices, swap(): lax.all_to_all(v.reshape(half, state // half, v.shape[-1]), 'node', split...  8.01 us
    pallas_call x2, Pallas kernels, pack_slots(): pl.pallas_call(kernel, in_specs=in_specs, out_specs=[pl.BlockSpec(memory_...  6.65 us
  transfers between devices with their start and end apart: 7, of which 4 were waited for; matrix products, arithmetic and copies ran while one was open for 1% of the time, Pallas kernels for 44%

profile of v3, /device:TPU:0, one launch (start us, length us, event | category | flops | bytes accessed | tf_op | source)
XLA Modules:
  0.0 141.9 jit_solution(12806309443629467243)
XLA Ops:
  0.6 7.0 %node_states.3 = (bf16[128,4224]{1,0:T(8,128)(2,1)}, f32[512,128]{1,0:T(8,128)}, f32[32,512]{1,0:T(8,128)}, f32[512,128]{1,0:T(8,128)}, f32[512,128]{1,0:T(8,128)}, /*index=5*/bf16[512,512]{1,0:T(8,128)(2,1)}) custom-call(bf16[512,4096]{1,0:T(8,128)(2,1)} %x_ref.7, bf16[512,4096]{1,0:T(8,128)(2,1)} %cot_ref.7, bf16[512,128]{1,0:T(8,128)(2,1)} %b_ref.7, ...), custom_call_target="tpu_custom_call" | custom-call | flops 536870912 | bytes 5242880 | tf_op jit(solution)/shard_map/node_states/pallas_call | solution.py:135
  7.7 6.2 %all-to-all-start = ((bf16[8,16,4224]{2,1,0:T(8,128)(2,1)}), bf16[8,16,4224]{2,1,0:T(8,128)(2,1)S(1)}, u32[]{:S(2)}, u32[]{:S(2)}) async-start(bf16[8,16,4224]{2,1,0:T(8,128)(2,1)} %bitcast.18), calls=%async_computation | async-start | bytes 2162688 | tf_op jit(solution)/shard_map/all_to_all | solution.py:702
  13.9 7.0 %node_states.2 = (bf16[128,4224]{1,0:T(8,128)(2,1)}, f32[512,128]{1,0:T(8,128)}, f32[32,512]{1,0:T(8,128)}, f32[512,128]{1,0:T(8,128)}, f32[512,128]{1,0:T(8,128)}, /*index=5*/bf16[512,512]{1,0:T(8,128)(2,1)}) custom-call(bf16[512,4096]{1,0:T(8,128)(2,1)} %x_ref.7, bf16[512,4096]{1,0:T(8,128)(2,1)} %cot_ref.7, bf16[512,128]{1,0:T(8,128)(2,1)} %b_ref.7, ...), custom_call_target="tpu_custom_call" | custom-call | flops 536870912 | bytes 5242880 | tf_op jit(solution)/shard_map/node_states/pallas_call | solution.py:135
  20.9 8.0 %all-to-all-done.refs_1_ = bf16[8,16,4224]{2,1,0:T(8,128)(2,1)S(1)} async-done(((bf16[8,16,4224]{2,1,0:T(8,128)(2,1)}), bf16[8,16,4224]{2,1,0:T(8,128)(2,1)S(1)}, u32[]{:S(2)}, u32[]{:S(2)}) %all-to-all-start) | async-done | bytes 1081376 | tf_op jit(solution)/shard_map/all_to_all | solution.py:702
  28.9 3.6 %all-to-all-start.1 = ((bf16[8,16,4224]{2,1,0:T(8,128)(2,1)}), bf16[8,16,4224]{2,1,0:T(8,128)(2,1)S(1)}, u32[]{:S(2)}, u32[]{:S(2)}) async-start(bf16[8,16,4224]{2,1,0:T(8,128)(2,1)} %bitcast.17), calls=%async_computation.1 | async-start | bytes 2162688 | tf_op jit(solution)/shard_map/all_to_all | solution.py:702
  32.5 0.1 fusion.5
  32.6 0.7 convert_reduce_fusion
  33.9 8.8 %node_inner.4 = (bf16[512,4096]{1,0:T(8,128)(2,1)}, bf16[512,4096]{1,0:T(8,128)(2,1)}, f32[512,128]{1,0:T(8,128)}, f32[512,128]{1,0:T(8,128)}) custom-call(f32[512,128]{1,0:T(8,128)} %get-tuple-element.61.after_ref.refs_5_, bf16[512,4096]{1,0:T(8,128)(2,1)} %x_ref.7, bf16[512,4096]{1,0:T(8,128)(2,1)} %cot_ref.7, bf16[512,128]{1,0:T(8,128)(2,1)} %b_ref.7, ...), custom_call_target="tpu_custom_call" | custom-call | flops 6442450944 | bytes 6291456 | tf_op jit(solution)/shard_map/node_inner/pallas_call | solution.py:302
  42.7 3.3 %pack_slots.2 = (bf16[6,16,2176]{2,1,0:T(8,128)(2,1)}, bf16[6,16,2176]{2,1,0:T(8,128)(2,1)S(1)}) custom-call(f32[512,128]{1,0:T(8,128)} %get-tuple-element.65.after_ref, s32[16]{0:T(128)} %refs_0_.14, bf16[8,16,4224]{2,1,0:T(8,128)(2,1)} %copy-done.1), custom_call_target="tpu_custom_call" | custom-call | flops 5242880 | bytes 2097152 | tf_op jit(solution)/shard_map/pack_slots/pallas_call | solution.py:443
  46.0 2.6 %collective-permute-start.2 = (bf16[6,16,2176]{2,1,0:T(8,128)(2,1)}, bf16[6,16,2176]{2,1,0:T(8,128)(2,1)S(1)}, u32[]{:S(2)}, u32[]{:S(2)}) collective-permute-start(bf16[6,16,2176]{2,1,0:T(8,128)(2,1)} %get-tuple-element.73), channel_id=1, source_target_pairs={{0,16},{2,18},{4,20},{6,22},{8,24},{10,26},{12,28},{14,30},{16,0},... | collective-permute-start | bytes 1253384 | tf_op jit(solution)/shard_map/ppermute | solution.py:712
  48.6 8.8 %node_inner.5 = (bf16[512,4096]{1,0:T(8,128)(2,1)}, bf16[512,4096]{1,0:T(8,128)(2,1)}, f32[512,128]{1,0:T(8,128)}, f32[512,128]{1,0:T(8,128)}) custom-call(bf16[6,16,2176]{2,1,0:T(8,128)(2,1)S(1)} %get-tuple-element.67.after_ref, bf16[512,4096]{1,0:T(8,128)(2,1)} %x_ref.7, bf16[512,4096]{1,0:T(8,128)(2,1)} %cot_ref.7, ...), custom_call_target="tpu_custom_call", output_to_operand_aliasing={{0}: (8, {}), {1}: (9, {})} | custom-call | flops 6442450944 | bytes 6291456 | tf_op jit(solution)/shard_map/node_inner/pallas_call | solution.py:302
  57.4 1.0 copy-done
  58.4 3.3 %pack_slots.3 = (bf16[6,16,2176]{2,1,0:T(8,128)(2,1)}, bf16[6,16,2176]{2,1,0:T(8,128)(2,1)S(1)}) custom-call(f32[512,128]{1,0:T(8,128)} %get-tuple-element.70.after_ref, s32[16]{0:T(128)} %refs_0_.14, bf16[8,16,4224]{2,1,0:T(8,128)(2,1)} %copy-done), custom_call_target="tpu_custom_call" | custom-call | flops 5242880 | bytes 2097152 | tf_op jit(solution)/shard_map/pack_slots/pallas_call | solution.py:443
  61.7 0.8 conditional.1
  61.7 0.8 copy.22
  62.5 4.6 %collective-permute-done.2.refs_2_ = bf16[6,16,2176]{2,1,0:T(8,128)(2,1)S(1)} collective-permute-done((bf16[6,16,2176]{2,1,0:T(8,128)(2,1)}, bf16[6,16,2176]{2,1,0:T(8,128)(2,1)S(1)}, u32[]{:S(2)}, u32[]{:S(2)}) %collective-permute-start.2) | collective-permute-done | bytes 417824 | tf_op jit(solution)/shard_map/ppermute | solution.py:712
  67.1 0.8 copy-done.7
  67.9 4.3 %join_slots.2 = (bf16[8,16,4096]{2,1,0:T(8,128)(2,1)}, f32[8,128]{1,0:T(8,128)}) custom-call(bf16[6,16,2176]{2,1,0:T(8,128)(2,1)S(1)} %get-tuple-element.72.after_ref, s32[16]{0:T(128)} %refs_0_.14, bf16[8,16,4224]{2,1,0:T(8,128)(2,1)} %copy-done.1, bf16[6,16,2176]{2,1,0:T(8,128)(2,1)} %copy-done.7, bf16[6,16,2176]{2,1,0:T(8,128)(2,1)S(1)} %get-tuple-element.74.refs_3_), custom_call_target="tpu_custom_call" | custom-call | flops 5242880 | bytes 2097152 | tf_op jit(solution)/shard_map/join_slots/pallas_call | solution.py:555
  72.2 4.1 %all-to-all-start.3 = ((bf16[8,16,4096]{2,1,0:T(8,128)(2,1)}), bf16[8,16,4096]{2,1,0:T(8,128)(2,1)S(1)}, u32[]{:S(2)}, u32[]{:S(2)}) async-start(bf16[8,16,4096]{2,1,0:T(8,128)(2,1)} %get-tuple-element.90), calls=%async_computation.3 | async-start | bytes 2097152 | tf_op jit(solution)/shard_map/all_to_all | solution.py:702
  76.3 3.3 %collective-permute-start.3 = (bf16[6,16,2176]{2,1,0:T(8,128)(2,1)S(1)}, bf16[6,16,2176]{2,1,0:T(8,128)(2,1)S(1)}, u32[]{:S(2)}, u32[]{:S(2)}) collective-permute-start(bf16[6,16,2176]{2,1,0:T(8,128)(2,1)S(1)} %copy-done.14), channel_id=1, source_target_pairs={{0,16},{2,18},{4,20},{6,22},{8,24},{10,26},{12,28},{14,30},{16,0},... | collective-permute-start | bytes 1253384 | tf_op jit(solution)/shard_map/ppermute | solution.py:712
  79.6 8.7 %node_inner.6 = (bf16[512,4096]{1,0:T(8,128)(2,1)}, bf16[512,4096]{1,0:T(8,128)(2,1)}, f32[512,128]{1,0:T(8,128)}, f32[512,128]{1,0:T(8,128)}) custom-call(f32[8,128]{1,0:T(8,128)} %get-tuple-element.75.after_ref, bf16[512,4096]{1,0:T(8,128)(2,1)} %x_ref.7, bf16[512,4096]{1,0:T(8,128)(2,1)} %cot_ref.7, ...), custom_call_target="tpu_custom_call", output_to_operand_aliasing={{0}: (8, {}), {1}: (9, {})} | custom-call | flops 6442450944 | bytes 6291456 | tf_op jit(solution)/shard_map/node_inner/pallas_call | solution.py:302
  88.3 8.6 %collective-permute-done.3.refs_2_ = bf16[6,16,2176]{2,1,0:T(8,128)(2,1)S(1)} collective-permute-done((bf16[6,16,2176]{2,1,0:T(8,128)(2,1)S(1)}, bf16[6,16,2176]{2,1,0:T(8,128)(2,1)S(1)}, u32[]{:S(2)}, u32[]{:S(2)}) %collective-permute-start.3) | collective-permute-done | bytes 417824 | tf_op jit(solution)/shard_map/ppermute | solution.py:712
  96.9 0.8 copy-done.8
  97.6 4.5 %join_slots.3 = (bf16[8,16,4096]{2,1,0:T(8,128)(2,1)}, f32[8,128]{1,0:T(8,128)}) custom-call(f32[512,128]{1,0:T(8,128)} %get-tuple-element.79.after_ref, s32[16]{0:T(128)} %refs_0_.14, bf16[8,16,4224]{2,1,0:T(8,128)(2,1)} %copy-done, bf16[6,16,2176]{2,1,0:T(8,128)(2,1)} %copy-done.8, bf16[6,16,2176]{2,1,0:T(8,128)(2,1)} %get-tuple-element.81.refs_3_), custom_call_target="tpu_custom_call" | custom-call | flops 5242880 | bytes 2097152 | tf_op jit(solution)/shard_map/join_slots/pallas_call | solution.py:555
  102.1 8.7 %all-to-all-start.2 = ((bf16[8,16,4096]{2,1,0:T(8,128)(2,1)}), bf16[8,16,4096]{2,1,0:T(8,128)(2,1)S(1)}, u32[]{:S(2)}, u32[]{:S(2)}) async-start(bf16[8,16,4096]{2,1,0:T(8,128)(2,1)} %get-tuple-element.82), calls=%async_computation.2 | async-start | bytes 2097152 | tf_op jit(solution)/shard_map/all_to_all | solution.py:702
  110.8 8.7 %node_inner.7 = (bf16[512,4096]{1,0:T(8,128)(2,1)}, bf16[512,4096]{1,0:T(8,128)(2,1)}, f32[512,128]{1,0:T(8,128)}, f32[512,128]{1,0:T(8,128)}) custom-call(f32[8,128]{1,0:T(8,128)} %get-tuple-element.83.after_ref, bf16[512,4096]{1,0:T(8,128)(2,1)} %x_ref.7, bf16[512,4096]{1,0:T(8,128)(2,1)} %cot_ref.7, ...), custom_call_target="tpu_custom_call", output_to_operand_aliasing={{0}: (8, {}), {1}: (9, {})} | custom-call | flops 6442450944 | bytes 6291456 | tf_op jit(solution)/shard_map/node_inner/pallas_call | solution.py:302
  119.5 8.7 %node_outer.2 = (bf16[512,4096]{1,0:T(8,128)(2,1)}, bf16[512,4096]{1,0:T(8,128)(2,1)}, f32[512,128]{1,0:T(8,128)}, f32[512,128]{1,0:T(8,128)}) custom-call(bf16[512,4096]{1,0:T(8,128)(2,1)} %x_ref.7, bf16[512,4096]{1,0:T(8,128)(2,1)} %cot_ref.7, bf16[512,128]{1,0:T(8,128)(2,1)} %b_ref.7, bf16[512,128]{1,0:T(8,128)(2,1)} %c_ref.7, ...), custom_call_target="tpu_custom_call" | custom-call | flops 1073741824 | bytes 16777216 | tf_op jit(solution)/shard_map/node_outer/pallas_call | solution.py:651
  128.3 1.0 copy-done.3
  129.4 8.9 %node_outer.3 = (bf16[512,4096]{1,0:T(8,128)(2,1)}, bf16[512,4096]{1,0:T(8,128)(2,1)}, f32[512,128]{1,0:T(8,128)}, f32[512,128]{1,0:T(8,128)}) custom-call(bf16[512,4096]{1,0:T(8,128)(2,1)} %x_ref.7, bf16[512,4096]{1,0:T(8,128)(2,1)} %cot_ref.7, bf16[512,128]{1,0:T(8,128)(2,1)} %b_ref.7, ...), custom_call_target="tpu_custom_call", output_to_operand_aliasing={{0}: (10, {}), {1}: (11, {})} | custom-call | flops 1073741824 | bytes 16777216 | tf_op jit(solution)/shard_map/node_outer/pallas_call | solution.py:651
  138.3 1.4 add_bitcast_fusion
  139.8 1.3 collective-permute-done.4
  141.2 0.7 slice_bitcast_fusion
  (33 shorter events, 0.2 us)
Async XLA Ops:
  7.7 21.3 %all-to-all-start = ((bf16[8,16,4224]{2,1,0:T(8,128)(2,1)}), bf16[8,16,4224]{2,1,0:T(8,128)(2,1)S(1)}, u32[]{:S(2)}, u32[]{:S(2)}) async-start(bf16[8,16,4224]{2,1,0:T(8,128)(2,1)} %bitcast.18), calls=%async_computation | async-start | bytes 2162688 | tf_op jit(solution)/shard_map/all_to_all | solution.py:702
  13.9 18.6 %copy-start.13 = (s32[16]{0:T(128)S(1)}, s32[16]{0:T(128)}, u32[]{:S(2)}) copy-start(s32[16]{0:T(128)} %refs_0_.14) | copy-start | bytes 196
  28.9 13.8 %copy-start.1 = (bf16[8,16,4224]{2,1,0:T(8,128)(2,1)}, bf16[8,16,4224]{2,1,0:T(8,128)(2,1)S(1)}, u32[]{:S(2)}) copy-start(bf16[8,16,4224]{2,1,0:T(8,128)(2,1)S(1)} %all-to-all-done.refs_1_) | copy-start | bytes 3244036
  28.9 28.5 %all-to-all-start.1 = ((bf16[8,16,4224]{2,1,0:T(8,128)(2,1)}), bf16[8,16,4224]{2,1,0:T(8,128)(2,1)S(1)}, u32[]{:S(2)}, u32[]{:S(2)}) async-start(bf16[8,16,4224]{2,1,0:T(8,128)(2,1)} %bitcast.17), calls=%async_computation.1 | async-start | bytes 2162688 | tf_op jit(solution)/shard_map/all_to_all | solution.py:702
  46.0 21.0 %collective-permute-start.2 = (bf16[6,16,2176]{2,1,0:T(8,128)(2,1)}, bf16[6,16,2176]{2,1,0:T(8,128)(2,1)S(1)}, u32[]{:S(2)}, u32[]{:S(2)}) collective-permute-start(bf16[6,16,2176]{2,1,0:T(8,128)(2,1)} %get-tuple-element.73), channel_id=1, source_target_pairs={{0,16},{2,18},{4,20},{6,22},{8,24},{10,26},{12,28},{14,30},{16,0},... | collective-permute-start | bytes 1253384 | tf_op jit(solution)/shard_map/ppermute | solution.py:712
  57.4 1.0 copy-start
  61.7 14.6 %copy-start.14 = (bf16[6,16,2176]{2,1,0:T(8,128)(2,1)S(1)}, bf16[6,16,2176]{2,1,0:T(8,128)(2,1)}, u32[]{:S(2)}) copy-start(bf16[6,16,2176]{2,1,0:T(8,128)(2,1)} %get-tuple-element.80) | copy-start | bytes 1253380
  67.1 0.8 copy-start.7
  72.2 30.0 %all-to-all-start.3 = ((bf16[8,16,4096]{2,1,0:T(8,128)(2,1)}), bf16[8,16,4096]{2,1,0:T(8,128)(2,1)S(1)}, u32[]{:S(2)}, u32[]{:S(2)}) async-start(bf16[8,16,4096]{2,1,0:T(8,128)(2,1)} %get-tuple-element.90), calls=%async_computation.3 | async-start | bytes 2097152 | tf_op jit(solution)/shard_map/all_to_all | solution.py:702
  76.3 20.6 %collective-permute-start.3 = (bf16[6,16,2176]{2,1,0:T(8,128)(2,1)S(1)}, bf16[6,16,2176]{2,1,0:T(8,128)(2,1)S(1)}, u32[]{:S(2)}, u32[]{:S(2)}) collective-permute-start(bf16[6,16,2176]{2,1,0:T(8,128)(2,1)S(1)} %copy-done.14), channel_id=1, source_target_pairs={{0,16},{2,18},{4,20},{6,22},{8,24},{10,26},{12,28},{14,30},{16,0},... | collective-permute-start | bytes 1253384 | tf_op jit(solution)/shard_map/ppermute | solution.py:712
  96.9 0.8 copy-start.8
  102.1 17.4 %copy-start.2 = (bf16[8,16,4096]{2,1,0:T(8,128)(2,1)}, bf16[8,16,4096]{2,1,0:T(8,128)(2,1)S(1)}, u32[]{:S(2)}) copy-start(bf16[8,16,4096]{2,1,0:T(8,128)(2,1)S(1)} %all-to-all-done.3) | copy-start | bytes 3145732
  102.1 26.2 %all-to-all-start.2 = ((bf16[8,16,4096]{2,1,0:T(8,128)(2,1)}), bf16[8,16,4096]{2,1,0:T(8,128)(2,1)S(1)}, u32[]{:S(2)}, u32[]{:S(2)}) async-start(bf16[8,16,4096]{2,1,0:T(8,128)(2,1)} %get-tuple-element.82), calls=%async_computation.2 | async-start | bytes 2097152 | tf_op jit(solution)/shard_map/all_to_all | solution.py:702
  128.3 1.0 copy-start.3
  129.3 8.9 %copy-start.4 = (f32[512,128]{1,0:T(8,128)S(1)}, f32[512,128]{1,0:T(8,128)}, u32[]{:S(2)}) copy-start(f32[512,128]{1,0:T(8,128)} %get-tuple-element.65.after_ref) | copy-start | bytes 786436
  129.3 8.9 %copy-start.5 = (f32[512,128]{1,0:T(8,128)S(1)}, f32[512,128]{1,0:T(8,128)}, u32[]{:S(2)}) copy-start(f32[512,128]{1,0:T(8,128)} %get-tuple-element.70.after_ref) | copy-start | bytes 786436
  129.3 8.9 %copy-start.6 = (f32[512,128]{1,0:T(8,128)S(1)}, f32[512,128]{1,0:T(8,128)}, u32[]{:S(2)}) copy-start(f32[512,128]{1,0:T(8,128)} %get-tuple-element.79.after_ref) | copy-start | bytes 786436
  129.3 8.9 %copy-start.9 = (f32[512,128]{1,0:T(8,128)S(1)}, f32[512,128]{1,0:T(8,128)}, u32[]{:S(2)}) copy-start(f32[512,128]{1,0:T(8,128)} %get-tuple-element.95) | copy-start | bytes 786436
  129.3 8.9 %copy-start.10 = (f32[512,128]{1,0:T(8,128)S(1)}, f32[512,128]{1,0:T(8,128)}, u32[]{:S(2)}) copy-start(f32[512,128]{1,0:T(8,128)} %get-tuple-element.96) | copy-start | bytes 786436
  129.3 8.9 %copy-start.11 = (f32[512,128]{1,0:T(8,128)S(1)}, f32[512,128]{1,0:T(8,128)}, u32[]{:S(2)}) copy-start(f32[512,128]{1,0:T(8,128)} %get-tuple-element.97) | copy-start | bytes 786436
  129.3 8.9 %copy-start.12 = (f32[512,128]{1,0:T(8,128)S(1)}, f32[512,128]{1,0:T(8,128)}, u32[]{:S(2)}) copy-start(f32[512,128]{1,0:T(8,128)} %get-tuple-element.101) | copy-start | bytes 786436
  139.7 1.4 collective-permute-start.4

commit v4 on v3

--- a/solution.py
+++ b/solution.py
@@ -8,7 +8,9 @@
 from jax.experimental.pallas import tpu as pltpu
 from jax.sharding import PartitionSpec as P
 
+
 LEVELS = 3
+VMEM_BYTES = 24 << 20
 LANES = 128
 CHUNKS = 2
 PARTS = 2
@@ -41,9 +43,9 @@
     return high, (v - high.astype(f32)).astype(bf16)
 
 
-def spread_matrix(rows, width, head_width):
+def spread_matrix(rows, width, head_width, offset=0):
     row = lax.broadcasted_iota(jnp.int32, (rows, width), 0)
-    lane = lax.broadcasted_iota(jnp.int32, (rows, width), 1) // head_width
+    lane = (lax.broadcasted_iota(jnp.int32, (rows, width), 1) + offset) // head_width
     return (row == lane).astype(bf16)
 
 
@@ -82,7 +84,6 @@
     length = step_ref.shape[1]
     index = pl.program_id(0)
     width = heads * head_width
-    pack = LANES // head_width
 
     @pl.when(index == 0)
     def _():
@@ -99,31 +100,20 @@
         last = cumulative[:, length - 1 :]
         low_ref[...] = pad_lanes(cumulative * LOG2E)
         src_ref[...] = (cumulative - jnp.log(step)) * LOG2E
-        grow_ref[...] = pad_lanes(jnp.exp(cumulative))
-        tail_ref[...] = pad_lanes(jnp.exp(last - cumulative) * step)
+        grow_ref[...] = pad_lanes(jnp.exp(cumulative)).astype(bf16)
+        tail_ref[...] = pad_lanes(jnp.exp(last - cumulative) * step).astype(bf16)
         bt_ref[...] = b_ref[...].T
         ct_ref[...] = c_ref[...].T
         total = jnp.exp(jnp.broadcast_to(last, (heads, send_ref.shape[0])))
         send_ref[:, 2 * width :] = pad_lanes(total).astype(bf16)
         gram_ref[...] = mm(c_ref[...], b_ref[...], NT).astype(bf16)
 
-    grow = grow_ref[...]
-    tail = tail_ref[...]
-    parts = range(block // LANES)
-    tailed = []
-    emitted = []
-    for q in parts:
-        lanes = slice(q * LANES, (q + 1) * LANES)
-        first = (index * (block // LANES) + q) * pack
-        tail_wide = head_lanes(tail, first, head_width)
-        grow_wide = head_lanes(grow, first, head_width)
-        tailed.append((tail_wide * x_ref[:, lanes].astype(f32)).astype(bf16))
-        emitted.append((grow_wide * cot_ref[:, lanes].astype(f32)).astype(bf16))
+    spread = spread_matrix(LANES, block, head_width, index * block)
+    tailed = mm(tail_ref[...], spread).astype(bf16) * x_ref[...]
+    emitted = mm(grow_ref[...], spread).astype(bf16) * cot_ref[...]
     at = pl.multiple_of(index * block, block)
-    send_ref[:, pl.ds(at, block)] = mm(bt_ref[...], jnp.concatenate(tailed, axis=1)).astype(bf16)
-    send_ref[:, pl.ds(at + width, block)] = mm(
-        ct_ref[...], jnp.concatenate(emitted, axis=1)
-    ).astype(bf16)
+    send_ref[:, pl.ds(at, block)] = mm(bt_ref[...], tailed).astype(bf16)
+    send_ref[:, pl.ds(at + width, block)] = mm(ct_ref[...], emitted).astype(bf16)
 
 
 def node_states(x, cot, b, c, step, rate, chunk, heads, head_width):
@@ -155,8 +145,8 @@
             jax.ShapeDtypeStruct((state, 2 * width + LANES), bf16),
             jax.ShapeDtypeStruct((length, LANES), f32),
             jax.ShapeDtypeStruct((heads, length), f32),
-            jax.ShapeDtypeStruct((length, LANES), f32),
-            jax.ShapeDtypeStruct((length, LANES), f32),
+            jax.ShapeDtypeStruct((length, LANES), bf16),
+            jax.ShapeDtypeStruct((length, LANES), bf16),
             jax.ShapeDtypeStruct((length, length), bf16),
         ],
         scratch_shapes=[pltpu.VMEM((state, length), bf16), pltpu.VMEM((state, length), bf16)],
@@ -177,14 +167,14 @@
     cot_ref,
     b_ref,
     c_ref,
-    gram_ref,
+    given_ref,
     low_ref,
     src_ref,
     *refs,
 ):
     if aliased:
         refs = refs[2:]
-    out_ref, grad_ref, gc_ref, gb_ref, mixed_ref, turned_ref, wa_ref, wb_ref = refs
+    out_ref, grad_ref, gc_ref, gb_ref, mixed_ref, turned_ref, wa_ref, wb_ref, gram_ref = refs
     length = x_ref.shape[0]
     index = pl.program_id(0)
     pack = LANES // head_width
@@ -195,6 +185,7 @@
 
     @pl.when(index == 0)
     def _():
+        gram_ref[...] = given_ref[...]
         mixed_ref[...] = jnp.zeros_like(mixed_ref)
         for ref in weights:
             ref[...] = jnp.zeros_like(ref)
@@ -320,6 +311,7 @@
             pltpu.VMEM((block, length), bf16),
             pltpu.VMEM((length, length), bf16),
             pltpu.VMEM((length, length), bf16),
+            pltpu.VMEM((length, length), bf16),
         ],
         input_output_aliases=aliases,
         name="node_inner",
@@ -407,7 +399,7 @@
             chain = recv_ref[m, :, 2 * width :].astype(f32)
             at = node
             live = jnp.bool_(True)
-            for level in range(LEVELS - 1):
+            for _ in range(LEVELS - 1):
                 up = parents_ref[at]
                 live = jnp.logical_and(jnp.logical_and(live, up >= 0), inside(up))
                 where = spot(up)
@@ -454,6 +446,7 @@
             pltpu.VMEM((main + more, rows, LANES), f32),
             pltpu.SMEM((nodes,), jnp.int32),
         ],
+        compiler_params=pltpu.CompilerParams(vmem_limit_bytes=VMEM_BYTES),
         name="pack_slots",
         cost_estimate=pl.CostEstimate(
             flops=20 * half * rows * width,
@@ -479,7 +472,6 @@
     rank_ref,
 ):
     half = recv_ref.shape[0]
-    nodes = rank_ref.shape[0]
     width = heads * head_width
     main = main_ref.shape[0]
     base = lax.axis_index("node") // half * half
@@ -567,6 +559,7 @@
             pltpu.VMEM((half, rows, width), f32),
             pltpu.SMEM((nodes,), jnp.int32),
         ],
+        compiler_params=pltpu.CompilerParams(vmem_limit_bytes=VMEM_BYTES),
         name="join_slots",
         cost_estimate=pl.CostEstimate(
             flops=20 * half * rows * width,
@@ -577,9 +570,9 @@
 
 
 def outer_kernel(
-    heads,
     head_width,
-    aliased,
+    extras,
+    final,
     x_ref,
     cot_ref,
     b_ref,
@@ -592,36 +585,49 @@
     grad_ref,
     *refs,
 ):
-    out_ref, gx_ref, gc_ref, gb_ref = refs[2:] if aliased else refs
+    added = refs[: 2 * extras]
+    refs = refs[2 * extras :]
+    if not final:
+        out_ref, gx_ref, gc_ref, gb_ref = refs
+    else:
+        out_ref, gx_ref, own_ref = refs[2:5]
+        pieces = refs[5:-2]
+        gc_ref, gb_ref = refs[-2:]
     block = x_ref.shape[1]
     index = pl.program_id(0)
-    pack = LANES // head_width
-    firsts = [(index * (block // LANES) + q) * pack for q in range(block // LANES)]
-    grow = grow_ref[...]
-    tail = tail_ref[...]
-    grow_wide = jnp.concatenate([head_lanes(grow, v, head_width) for v in firsts], axis=1)
-    tail_wide = jnp.concatenate([head_lanes(tail, v, head_width) for v in firsts], axis=1)
+
+    @pl.when(index == 0)
+    def _():
+        gc_ref[...] = sum(ref[...] for ref in added[:extras])
+        gb_ref[...] = sum(ref[...] for ref in added[extras:])
+
+    spread = spread_matrix(LANES, block, head_width, index * block)
+    grow_wide = mm(grow_ref[...], spread)
+    tail_wide = mm(tail_ref[...], spread)
     start = start_ref[...]
     back = back_ref[...]
     out_ref[...] = (inner_ref[...].astype(f32) + grow_wide * mm(c_ref[...], start)).astype(bf16)
     gx_ref[...] = (grad_ref[...].astype(f32) + tail_wide * mm(b_ref[...], back)).astype(bf16)
-    emitted = (grow_wide * cot_ref[...].astype(f32)).astype(bf16)
-    tailed = (tail_wide * x_ref[...].astype(f32)).astype(bf16)
-    gc = mm(emitted, start, NT)
-    gb = mm(tailed, back, NT)
-
-    @pl.when(index == 0)
-    def _():
-        gc_ref[...] = gc
-        gb_ref[...] = gb
-
-    @pl.when(index > 0)
-    def _():
-        gc_ref[...] += gc
-        gb_ref[...] += gb
-
-
-def node_outer(x, cot, b, c, grow, tail, states, inner, grad, prior, chunk, heads, head_width):
+    gc_ref[...] += mm(grow_wide.astype(bf16) * cot_ref[...], start, NT)
+    gb_ref[...] += mm(tail_wide.astype(bf16) * x_ref[...], back, NT)
+
+    if final:
+
+        @pl.when(index == pl.num_programs(0) - 1)
+        def _():
+            size = len(pieces) + 1
+            me = lax.axis_index("head")
+            rows = own_ref.shape[1]
+            for shift in range(size):
+                at = pl.multiple_of(lax.rem(me + shift, size) * rows, rows)
+                for n, ref in enumerate((gb_ref, gc_ref)):
+                    if shift == 0:
+                        own_ref[n] = ref[pl.ds(at, rows)]
+                    else:
+                        pieces[shift - 1][n] = ref[pl.ds(at, rows)].astype(bf16)
+
+
+def node_outer(x, cot, b, c, grow, tail, states, inner, grad, found, prior, chunk, heads, head_width):
     length, state = b.shape
     width = heads * head_width
     block = min(width, 4 * LANES)
@@ -629,7 +635,7 @@
     whole = lambda i: (0, 0)
     spot = lambda i: (0, i)
     place = lambda i: (0, chunk * count + i)
-    aliased = prior is not None
+    final = prior is not None
     operands = [x, cot, b, c, grow, tail, states, states, inner, grad]
     in_specs = [
         pl.BlockSpec((length, block), place),
@@ -643,51 +649,53 @@
         pl.BlockSpec((length, block), place),
         pl.BlockSpec((length, block), place),
     ]
+    operands += [v[1] for v in found] + [v[0] for v in found]
+    in_specs += [pl.BlockSpec((length, state), whole)] * (2 * len(found))
+    out_specs = [pl.BlockSpec((length, block), place)] * 2
+    out_shape = [jax.ShapeDtypeStruct(x.shape, bf16)] * 2
+    grads = jax.ShapeDtypeStruct((length, state), f32)
+    scratch = []
     aliases = {}
-    if aliased:
+    if final:
         aliases = {len(operands): 0, len(operands) + 1: 1}
         operands += list(prior)
         in_specs += [pl.BlockSpec(memory_space=pl.ANY)] * 2
+        size = lax.axis_size("head")
+        kept = (2, length // size, state)
+        cube = lambda i: (0, 0, 0)
+        out_specs += [pl.BlockSpec(kept, cube)] * size
+        out_shape += [jax.ShapeDtypeStruct(kept, f32)]
+        out_shape += [jax.ShapeDtypeStruct(kept, bf16)] * (size - 1)
+        scratch = [pltpu.VMEM((length, state), f32)] * 2
+    else:
+        out_specs += [pl.BlockSpec((length, state), whole)] * 2
+        out_shape += [grads] * 2
     return pl.pallas_call(
-        functools.partial(outer_kernel, heads, head_width, aliased),
+        functools.partial(outer_kernel, head_width, len(found), final),
         grid=(count,),
         in_specs=in_specs,
-        out_specs=[
-            pl.BlockSpec((length, block), place),
-            pl.BlockSpec((length, block), place),
-            pl.BlockSpec((length, state), whole),
-            pl.BlockSpec((length, state), whole),
-        ],
-        out_shape=[
-            jax.ShapeDtypeStruct(x.shape, bf16),
-            jax.ShapeDtypeStruct(x.shape, bf16),
-            jax.ShapeDtypeStruct((length, state), f32),
-            jax.ShapeDtypeStruct((length, state), f32),
-        ],
+        out_specs=out_specs,
+        out_shape=out_shape,
+        scratch_shapes=scratch,
         input_output_aliases=aliases,
         name="node_outer",
         cost_estimate=pl.CostEstimate(
             flops=8 * length * state * width,
-            bytes_accessed=16 * length * width,
+            bytes_accessed=12 * length * width,
             transcendentals=0,
         ),
     )(*operands)
 
 
-def scatter_sum(parts):
+def scatter_sum(own, pieces):
     size = lax.axis_size("head")
-    me = lax.axis_index("head")
-    rows = parts.shape[1] // size
-    total = lax.dynamic_slice_in_dim(parts, me * rows, rows, axis=1)
-    for shift in range(1, size):
-        target = (me + shift) % size
-        piece = lax.dynamic_slice_in_dim(parts, target * rows, rows, axis=1).astype(bf16)
-        moved = lax.ppermute(piece, "head", [(i, (i + shift) % size) for i in range(size)])
-        total = total + moved.astype(f32)
-    return total
-
-
-def on_device(inputs, b_matrix, c_matrix, step_size, decay_rate, parents, cotangent):
+    for shift, piece in enumerate(pieces, 1):
+        pairs = [(i, (i + shift) % size) for i in range(size)]
+        own = own + lax.ppermute(piece, "head", pairs).astype(f32)
+    return own
+
+
+def one_device(inputs, b_matrix, c_matrix, step_size, decay_rate, parents, cotangent):
     state = b_matrix.shape[1]
     head_count = step_size.shape[0]
     head_width = inputs.shape[1] // head_count
@@ -722,7 +730,7 @@
     sizes = (heads, head_width)
     made = [node_states(*shared, step_size, rate, k, *sizes) for k in range(CHUNKS)]
     received = [swap(made[k][0]) for k in range(CHUNKS)]
-    grads_found = []
+    found = []
     prior = None
     token = made[CHUNKS - 1][1]
 
@@ -730,7 +738,7 @@
         *prior, gc, gb = node_inner(
             *shared, made[0][5], made[k][1], made[k][2], prior, token, k, part, PARTS, *sizes
         )
-        grads_found.append((gb, gc))
+        found.append((gb, gc))
         return prior, gc
 
     todo = [(k, part) for k in range(CHUNKS) for part in range(PARTS)]
@@ -756,19 +764,19 @@
     inner = prior
     prior = None
     for k in range(CHUNKS):
-        *prior, gc, gb = node_outer(
-            *shared, made[k][3], made[k][4], states[k], *inner, prior, k, *sizes
+        result = node_outer(
+            *shared, made[k][3], made[k][4], states[k], *inner, found, prior, k, *sizes
         )
-        grads_found.append((gb, gc))
-    grad_b = sum(g[0] for g in grads_found)
-    grad_c = sum(g[1] for g in grads_found)
-    grads = scatter_sum(jnp.stack([grad_b, grad_c]))
+        prior = result[:2]
+        if k == 0:
+            found = [(result[3], result[2])]
+    grads = scatter_sum(result[2], result[3:])
     return prior[0], prior[1], grads[0], grads[1]
 
 
 def solution(mesh):
     return jax.shard_map(
-        on_device,
+        one_device,
         mesh=mesh,
         in_specs=(
             P("node", "head"),

time: 143 us -> 178 us (1.24)
  waiting for transfers between devices: 22.5 us -> 56.4 us
  Pallas kernels: 82 us -> 77.4 us
  starting transfers between devices: 28.6 us -> 32.5 us
  local copies, waits for them, and re-layouts: 5.05 us -> 7.33 us
    ppermute x2 -> x4, waiting for transfers between devices: 13.2 us -> 46 us  [cross(): return lax.ppermute(v, 'node', across)]
    ppermute x2 -> x4, starting transfers between devices: 5.89 us -> 9.42 us  [cross(): return lax.ppermute(v, 'node', across)]
    unnamed x30 -> x18, local copies, waits for them, and re-layouts: 3.57 us -> 5.86 us
    pallas_call x2, Pallas kernels: 6.65 us -> 4.42 us  [pack_slots(): pl.pallas_call(kernel, in_specs=in_specs, out_specs=[pl.BlockSpec(memory_...]
  transfers between devices with their start and end apart: 7 -> 9, of which waited for: 4 -> 5; matrix products, arithmetic and copies ran while one was open for 1% -> 1% of each run, Pallas kernels for 44% -> 33%
where the time goes in v4:
time: 178 us; the launch traced here: 177 us
  Pallas kernels  77.4 us (43%)
  waiting for transfers between devices  56.4 us (32%)
  starting transfers between devices  32.5 us (18%)
  local copies, waits for them, and re-layouts  7.33 us (4%)
    ppermute x4, waiting for transfers between devices, cross(): return lax.ppermute(v, 'node', across)  46 us
    pallas_call x4, Pallas kernels, node_inner(): pl.pallas_call(kernel, grid=(count,), in_specs=in_specs, out_specs=[pl.Bl...  35.2 us
    all_to_all x4, starting transfers between devices, swap(): lax.all_to_all(v.reshape(half, state // half, v.shape[-1]), 'node', split...  23 us
    pallas_call x2, Pallas kernels, node_outer(): pl.pallas_call(functools.partial(outer_kernel, head_width, len(found), fi...  17.7 us
    pallas_call x2, Pallas kernels, node_states(): pl.pallas_call(functools.partial(states_kernel, heads, head_width, chunk)...  12.3 us
    ppermute x4, starting transfers between devices, cross(): return lax.ppermute(v, 'node', across)  9.42 us
    all_to_all x4, waiting for transfers between devices, swap(): lax.all_to_all(v.reshape(half, state // half, v.shape[-1]), 'node', split...  8.87 us
    pallas_call x2, Pallas kernels, join_slots(): pl.pallas_call(kernel, in_specs=in_specs, out_specs=[pl.BlockSpec(memory_...  7.72 us
  transfers between devices with their start and end apart: 9, of which 5 were waited for; matrix products, arithmetic and copies ran while one was open for 1% of the time, Pallas kernels for 33%

profile of v4, /device:TPU:0, one launch (start us, length us, event | category | flops | bytes accessed | tf_op | source)
XLA Modules:
  0.0 176.7 jit_solution(12578227532028198635)
XLA Ops:
  0.6 6.2 %node_states.3 = (bf16[128,4224]{1,0:T(8,128)(2,1)}, f32[512,128]{1,0:T(8,128)}, f32[32,512]{1,0:T(8,128)}, bf16[512,128]{1,0:T(8,128)(2,1)}, bf16[512,128]{1,0:T(8,128)(2,1)}, /*index=5*/bf16[512,512]{1,0:T(8,128)(2,1)}) custom-call(bf16[512,4096]{1,0:T(8,128)(2,1)} %x_ref.7, bf16[512,4096]{1,0:T(8,128)(2,1)} %cot_ref.7, bf16[512,128]{1,0:T(8,128)(2,1)} %b_ref.7, ...), custom_call_target="tpu_custom_call" | custom-call | flops 536870912 | bytes 5242880 | tf_op jit(solution)/shard_map/node_states/pallas_call | solution.py:125
  6.8 6.2 %all-to-all-start = ((bf16[8,16,4224]{2,1,0:T(8,128)(2,1)}), bf16[8,16,4224]{2,1,0:T(8,128)(2,1)S(1)}, u32[]{:S(2)}, u32[]{:S(2)}) async-start(bf16[8,16,4224]{2,1,0:T(8,128)(2,1)} %bitcast.14), calls=%async_computation | async-start | bytes 2162688 | tf_op jit(solution)/shard_map/all_to_all | solution.py:710
  13.0 6.2 %node_states.2 = (bf16[128,4224]{1,0:T(8,128)(2,1)}, f32[512,128]{1,0:T(8,128)}, f32[32,512]{1,0:T(8,128)}, bf16[512,128]{1,0:T(8,128)(2,1)}, bf16[512,128]{1,0:T(8,128)(2,1)}, /*index=5*/bf16[512,512]{1,0:T(8,128)(2,1)}) custom-call(bf16[512,4096]{1,0:T(8,128)(2,1)} %x_ref.7, bf16[512,4096]{1,0:T(8,128)(2,1)} %cot_ref.7, bf16[512,128]{1,0:T(8,128)(2,1)} %b_ref.7, ...), custom_call_target="tpu_custom_call" | custom-call | flops 536870912 | bytes 5242880 | tf_op jit(solution)/shard_map/node_states/pallas_call | solution.py:125
  19.2 8.9 %all-to-all-done.refs_1_ = bf16[8,16,4224]{2,1,0:T(8,128)(2,1)S(1)} async-done(((bf16[8,16,4224]{2,1,0:T(8,128)(2,1)}), bf16[8,16,4224]{2,1,0:T(8,128)(2,1)S(1)}, u32[]{:S(2)}, u32[]{:S(2)}) %all-to-all-start) | async-done | bytes 1081376 | tf_op jit(solution)/shard_map/all_to_all | solution.py:710
  28.1 3.6 %all-to-all-start.1 = ((bf16[8,16,4224]{2,1,0:T(8,128)(2,1)}), bf16[8,16,4224]{2,1,0:T(8,128)(2,1)S(1)}, u32[]{:S(2)}, u32[]{:S(2)}) async-start(bf16[8,16,4224]{2,1,0:T(8,128)(2,1)} %bitcast.13), calls=%async_computation.1 | async-start | bytes 2162688 | tf_op jit(solution)/shard_map/all_to_all | solution.py:710
  33.0 8.8 %node_inner.4 = (bf16[512,4096]{1,0:T(8,128)(2,1)}, bf16[512,4096]{1,0:T(8,128)(2,1)}, f32[512,128]{1,0:T(8,128)}, f32[512,128]{1,0:T(8,128)}) custom-call(f32[512,128]{1,0:T(8,128)} %get-tuple-element.61.after_ref.refs_5_, bf16[512,4096]{1,0:T(8,128)(2,1)} %x_ref.7, bf16[512,4096]{1,0:T(8,128)(2,1)} %cot_ref.7, bf16[512,128]{1,0:T(8,128)(2,1)} %b_ref.7, ...), custom_call_target="tpu_custom_call" | custom-call | flops 6442450944 | bytes 6291456 | tf_op jit(solution)/shard_map/node_inner/pallas_call | solution.py:293
  41.9 0.9 copy-done
  42.8 2.6 %pack_slots.2 = (bf16[6,16,2176]{2,1,0:T(8,128)(2,1)S(1)}, bf16[6,16,2176]{2,1,0:T(8,128)(2,1)}) custom-call(f32[512,128]{1,0:T(8,128)S(1)} %copy-done, s32[16]{0:T(128)S(1)} %copy-done.3, bf16[8,16,4224]{2,1,0:T(8,128)(2,1)S(1)} %all-to-all-done.refs_1_), custom_call_target="tpu_custom_call" | custom-call | flops 5242880 | bytes 2097152 | tf_op jit(solution)/shard_map/pack_slots/pallas_call | solution.py:435
  45.4 2.7 %collective-permute-start.2 = (bf16[6,16,2176]{2,1,0:T(8,128)(2,1)S(1)}, bf16[6,16,2176]{2,1,0:T(8,128)(2,1)S(1)}, u32[]{:S(2)}, u32[]{:S(2)}) collective-permute-start(bf16[6,16,2176]{2,1,0:T(8,128)(2,1)S(1)} %get-tuple-element.73), channel_id=1, source_target_pairs={{0,16},{2,18},{4,20},{6,22},{8,24},{10,26},{12,28},{14,30},{16,0},... | collective-permute-start | bytes 1253384 | tf_op jit(solution)/shard_map/ppermute | solution.py:720
  48.1 8.8 %node_inner.5 = (bf16[512,4096]{1,0:T(8,128)(2,1)}, bf16[512,4096]{1,0:T(8,128)(2,1)}, f32[512,128]{1,0:T(8,128)}, f32[512,128]{1,0:T(8,128)}) custom-call(bf16[6,16,2176]{2,1,0:T(8,128)(2,1)} %get-tuple-element.67.after_ref, bf16[512,4096]{1,0:T(8,128)(2,1)} %x_ref.7, bf16[512,4096]{1,0:T(8,128)(2,1)} %cot_ref.7, ...), custom_call_target="tpu_custom_call", output_to_operand_aliasing={{0}: (8, {}), {1}: (9, {})} | custom-call | flops 6442450944 | bytes 6291456 | tf_op jit(solution)/shard_map/node_inner/pallas_call | solution.py:293
  56.9 0.9 copy-done.1
  57.8 1.8 %pack_slots.3 = (bf16[6,16,2176]{2,1,0:T(8,128)(2,1)S(1)}, bf16[6,16,2176]{2,1,0:T(8,128)(2,1)S(1)}) custom-call(f32[512,128]{1,0:T(8,128)S(1)} %copy-done.1, s32[16]{0:T(128)S(1)} %copy-done.3, bf16[8,16,4224]{2,1,0:T(8,128)(2,1)S(1)} %all-to-all-done.1.refs_1_), custom_call_target="tpu_custom_call" | custom-call | flops 5242880 | bytes 2097152 | tf_op jit(solution)/shard_map/pack_slots/pallas_call | solution.py:435
  59.7 0.8 copy-done.8
  60.5 41.7 %conditional.1 = (bf16[6,16,2176]{2,1,0:T(8,128)(2,1)}, bf16[6,16,2176]{2,1,0:T(8,128)(2,1)}) conditional(s32[]{:T(128)} %convert_element_type.10, (bf16[6,16,2176]{2,1,0:T(8,128)(2,1)}, bf16[6,16,2176]{2,1,0:T(8,128)(2,1)S(1)}) %tuple.15, (bf16[6,16,2176]{2,1,0:T(8,128)(2,1)}, bf16[6,16,2176]{2,1,0:T(8,128)(2,1)S(1)}) %tuple.15), branch_computations={%region_2.0_spmd, %region_3.0_spmd} | conditional | bytes 4178016 | solution.py:751
  60.8 2.6 %collective-permute-start.1 = (bf16[6,16,2176]{2,1,0:T(8,128)(2,1)S(1)}, bf16[6,16,2176]{2,1,0:T(8,128)(2,1)}, u32[]{:S(2)}, u32[]{:S(2)}) collective-permute-start(bf16[6,16,2176]{2,1,0:T(8,128)(2,1)S(1)} %get-tuple-element.9), channel_id=1, source_target_pairs={{0,16},{2,18},{4,20},{6,22},{8,24},{10,26},{12,28},{14,30},{16,0},... | collective-permute-start | bytes 1253384 | tf_op jit(solution)/shard_map/cond/branch_1_fun/ppermute | solution.py:720
  63.4 31.0 %collective-permute-done = bf16[6,16,2176]{2,1,0:T(8,128)(2,1)S(1)} collective-permute-done((bf16[6,16,2176]{2,1,0:T(8,128)(2,1)}, bf16[6,16,2176]{2,1,0:T(8,128)(2,1)S(1)}, u32[]{:S(2)}, u32[]{:S(2)}) %collective-permute-start) | collective-permute-done | bytes 417824 | tf_op jit(solution)/shard_map/cond/branch_1_fun/ppermute | solution.py:720
  94.4 0.8 copy.23
  95.2 7.0 %collective-permute-done.1 = bf16[6,16,2176]{2,1,0:T(8,128)(2,1)} collective-permute-done((bf16[6,16,2176]{2,1,0:T(8,128)(2,1)S(1)}, bf16[6,16,2176]{2,1,0:T(8,128)(2,1)}, u32[]{:S(2)}, u32[]{:S(2)}) %collective-permute-start.1) | collective-permute-done | bytes 417824 | tf_op jit(solution)/shard_map/cond/branch_1_fun/ppermute | solution.py:720
  102.2 3.8 %join_slots.2 = (bf16[8,16,4096]{2,1,0:T(8,128)(2,1)}, f32[8,128]{1,0:T(8,128)S(1)}) custom-call(bf16[6,16,2176]{2,1,0:T(8,128)(2,1)} %copy-done.8, s32[16]{0:T(128)S(1)} %copy-done.3, bf16[8,16,4224]{2,1,0:T(8,128)(2,1)S(1)} %all-to-all-done.refs_1_, bf16[6,16,2176]{2,1,0:T(8,128)(2,1)S(1)} %collective-permute-done.2.refs_2_, ...), custom_call_target="tpu_custom_call" | custom-call | flops 5242880 | bytes 2097152 | tf_op jit(solution)/shard_map/join_slots/pallas_call | solution.py:547
  106.6 4.0 %all-to-all-start.3 = ((bf16[8,16,4096]{2,1,0:T(8,128)(2,1)}), bf16[8,16,4096]{2,1,0:T(8,128)(2,1)S(1)}, u32[]{:S(2)}, u32[]{:S(2)}) async-start(bf16[8,16,4096]{2,1,0:T(8,128)(2,1)} %get-tuple-element.90), calls=%async_computation.3 | async-start | bytes 2097152 | tf_op jit(solution)/shard_map/all_to_all | solution.py:710
  110.6 3.8 %collective-permute-start.3 = (bf16[6,16,2176]{2,1,0:T(8,128)(2,1)S(1)}, bf16[6,16,2176]{2,1,0:T(8,128)(2,1)S(1)}, u32[]{:S(2)}, u32[]{:S(2)}) collective-permute-start(bf16[6,16,2176]{2,1,0:T(8,128)(2,1)S(1)} %get-tuple-element.80), channel_id=1, source_target_pairs={{0,16},{2,18},{4,20},{6,22},{8,24},{10,26},{12,28},{14,30},{16,0},... | collective-permute-start | bytes 1253384 | tf_op jit(solution)/shard_map/ppermute | solution.py:720
  114.4 8.8 %node_inner.6 = (bf16[512,4096]{1,0:T(8,128)(2,1)}, bf16[512,4096]{1,0:T(8,128)(2,1)}, f32[512,128]{1,0:T(8,128)}, f32[512,128]{1,0:T(8,128)}) custom-call(f32[8,128]{1,0:T(8,128)} %copy-done.5, bf16[512,4096]{1,0:T(8,128)(2,1)} %x_ref.7, bf16[512,4096]{1,0:T(8,128)(2,1)} %cot_ref.7, ...), custom_call_target="tpu_custom_call", output_to_operand_aliasing={{0}: (8, {}), {1}: (9, {})} | custom-call | flops 6442450944 | bytes 6291456 | tf_op jit(solution)/shard_map/node_inner/pallas_call | solution.py:293
  123.2 8.0 %collective-permute-done.3.refs_2_ = bf16[6,16,2176]{2,1,0:T(8,128)(2,1)S(1)} collective-permute-done((bf16[6,16,2176]{2,1,0:T(8,128)(2,1)S(1)}, bf16[6,16,2176]{2,1,0:T(8,128)(2,1)S(1)}, u32[]{:S(2)}, u32[]{:S(2)}) %collective-permute-start.3) | collective-permute-done | bytes 417824 | tf_op jit(solution)/shard_map/ppermute | solution.py:720
  131.2 0.9 copy-done.2
  132.1 3.9 %join_slots.3 = (bf16[8,16,4096]{2,1,0:T(8,128)(2,1)}, f32[8,128]{1,0:T(8,128)S(1)}) custom-call(f32[512,128]{1,0:T(8,128)S(1)} %copy-done.2, s32[16]{0:T(128)S(1)} %copy-done.3, bf16[8,16,4224]{2,1,0:T(8,128)(2,1)S(1)} %all-to-all-done.1.refs_1_, bf16[6,16,2176]{2,1,0:T(8,128)(2,1)S(1)} %collective-permute-done.3.refs_2_, ...), custom_call_target="tpu_custom_call" | custom-call | flops 5242880 | bytes 2097152 | tf_op jit(solution)/shard_map/join_slots/pallas_call | solution.py:547
  136.6 9.3 %all-to-all-start.2 = ((bf16[8,16,4096]{2,1,0:T(8,128)(2,1)}), bf16[8,16,4096]{2,1,0:T(8,128)(2,1)S(1)}, u32[]{:S(2)}, u32[]{:S(2)}) async-start(bf16[8,16,4096]{2,1,0:T(8,128)(2,1)} %get-tuple-element.82), calls=%async_computation.2 | async-start | bytes 2097152 | tf_op jit(solution)/shard_map/all_to_all | solution.py:710
  145.9 8.8 %node_inner.7 = (bf16[512,4096]{1,0:T(8,128)(2,1)}, bf16[512,4096]{1,0:T(8,128)(2,1)}, f32[512,128]{1,0:T(8,128)}, f32[512,128]{1,0:T(8,128)}) custom-call(f32[8,128]{1,0:T(8,128)} %copy-done.4, bf16[512,4096]{1,0:T(8,128)(2,1)} %x_ref.7, bf16[512,4096]{1,0:T(8,128)(2,1)} %cot_ref.7, ...), custom_call_target="tpu_custom_call", output_to_operand_aliasing={{0}: (8, {}), {1}: (9, {})} | custom-call | flops 6442450944 | bytes 6291456 | tf_op jit(solution)/shard_map/node_inner/pallas_call | solution.py:293
  154.7 8.9 %node_outer.2 = (bf16[512,4096]{1,0:T(8,128)(2,1)}, bf16[512,4096]{1,0:T(8,128)(2,1)}, f32[512,128]{1,0:T(8,128)}, f32[512,128]{1,0:T(8,128)}) custom-call(bf16[512,4096]{1,0:T(8,128)(2,1)} %x_ref.7, bf16[512,4096]{1,0:T(8,128)(2,1)} %cot_ref.7, bf16[512,128]{1,0:T(8,128)(2,1)} %b_ref.7, bf16[512,128]{1,0:T(8,128)(2,1)} %c_ref.7, ...), custom_call_target="tpu_custom_call" | custom-call | flops 1073741824 | bytes 12582912 | tf_op jit(solution)/shard_map/node_outer/pallas_call | solution.py:673
  163.6 1.0 copy-done.6
  164.7 8.8 %node_outer.3 = (bf16[512,4096]{1,0:T(8,128)(2,1)}, bf16[512,4096]{1,0:T(8,128)(2,1)}, f32[2,256,128]{2,1,0:T(8,128)}, bf16[2,256,128]{2,1,0:T(8,128)(2,1)}) custom-call(bf16[512,4096]{1,0:T(8,128)(2,1)} %x_ref.7, bf16[512,4096]{1,0:T(8,128)(2,1)} %cot_ref.7, bf16[512,128]{1,0:T(8,128)(2,1)} %b_ref.7, ...), custom_call_target="tpu_custom_call", output_to_operand_aliasing={{0}: (12, {}), {1}: (13, {})} | custom-call | flops 1073741824 | bytes 12582912 | tf_op jit(solution)/shard_map/node_outer/pallas_call | solution.py:673
  173.5 1.5 collective-permute-done.4
  175.0 1.0 convert_add_fusion
  (23 shorter events, 3.1 us)
Async XLA Ops:
  6.8 21.3 %all-to-all-start = ((bf16[8,16,4224]{2,1,0:T(8,128)(2,1)}), bf16[8,16,4224]{2,1,0:T(8,128)(2,1)S(1)}, u32[]{:S(2)}, u32[]{:S(2)}) async-start(bf16[8,16,4224]{2,1,0:T(8,128)(2,1)} %bitcast.14), calls=%async_computation | async-start | bytes 2162688 | tf_op jit(solution)/shard_map/all_to_all | solution.py:710
  13.0 18.6 %copy-start.3 = (s32[16]{0:T(128)S(1)}, s32[16]{0:T(128)}, u32[]{:S(2)}) copy-start(s32[16]{0:T(128)} %refs_0_.14) | copy-start | bytes 196
  28.1 28.8 %all-to-all-start.1 = ((bf16[8,16,4224]{2,1,0:T(8,128)(2,1)}), bf16[8,16,4224]{2,1,0:T(8,128)(2,1)S(1)}, u32[]{:S(2)}, u32[]{:S(2)}) async-start(bf16[8,16,4224]{2,1,0:T(8,128)(2,1)} %bitcast.13), calls=%async_computation.1 | async-start | bytes 2162688 | tf_op jit(solution)/shard_map/all_to_all | solution.py:710
  41.9 1.0 copy-start
  45.4 56.8 %collective-permute-start.2 = (bf16[6,16,2176]{2,1,0:T(8,128)(2,1)S(1)}, bf16[6,16,2176]{2,1,0:T(8,128)(2,1)S(1)}, u32[]{:S(2)}, u32[]{:S(2)}) collective-permute-start(bf16[6,16,2176]{2,1,0:T(8,128)(2,1)S(1)} %get-tuple-element.73), channel_id=1, source_target_pairs={{0,16},{2,18},{4,20},{6,22},{8,24},{10,26},{12,28},{14,30},{16,0},... | collective-permute-start | bytes 1253384 | tf_op jit(solution)/shard_map/ppermute | solution.py:720
  56.9 1.0 copy-start.1
  59.7 0.8 copy-start.8
  60.5 33.9 %collective-permute-start = (bf16[6,16,2176]{2,1,0:T(8,128)(2,1)}, bf16[6,16,2176]{2,1,0:T(8,128)(2,1)S(1)}, u32[]{:S(2)}, u32[]{:S(2)}) collective-permute-start(bf16[6,16,2176]{2,1,0:T(8,128)(2,1)} %get-tuple-element.8), channel_id=1, source_target_pairs={{0,16},{2,18},{4,20},{6,22},{8,24},{10,26},{12,28},{14,30},{16,0},... | collective-permute-start | bytes 1253384 | tf_op jit(solution)/shard_map/cond/branch_1_fun/ppermute | solution.py:720
  60.8 41.4 %collective-permute-start.1 = (bf16[6,16,2176]{2,1,0:T(8,128)(2,1)S(1)}, bf16[6,16,2176]{2,1,0:T(8,128)(2,1)}, u32[]{:S(2)}, u32[]{:S(2)}) collective-permute-start(bf16[6,16,2176]{2,1,0:T(8,128)(2,1)S(1)} %get-tuple-element.9), channel_id=1, source_target_pairs={{0,16},{2,18},{4,20},{6,22},{8,24},{10,26},{12,28},{14,30},{16,0},... | collective-permute-start | bytes 1253384 | tf_op jit(solution)/shard_map/cond/branch_1_fun/ppermute | solution.py:720
  106.0 0.6 copy-start.5
  106.6 30.0 %all-to-all-start.3 = ((bf16[8,16,4096]{2,1,0:T(8,128)(2,1)}), bf16[8,16,4096]{2,1,0:T(8,128)(2,1)S(1)}, u32[]{:S(2)}, u32[]{:S(2)}) async-start(bf16[8,16,4096]{2,1,0:T(8,128)(2,1)} %get-tuple-element.90), calls=%async_computation.3 | async-start | bytes 2097152 | tf_op jit(solution)/shard_map/all_to_all | solution.py:710
  110.6 20.6 %collective-permute-start.3 = (bf16[6,16,2176]{2,1,0:T(8,128)(2,1)S(1)}, bf16[6,16,2176]{2,1,0:T(8,128)(2,1)S(1)}, u32[]{:S(2)}, u32[]{:S(2)}) collective-permute-start(bf16[6,16,2176]{2,1,0:T(8,128)(2,1)S(1)} %get-tuple-element.80), channel_id=1, source_target_pairs={{0,16},{2,18},{4,20},{6,22},{8,24},{10,26},{12,28},{14,30},{16,0},... | collective-permute-start | bytes 1253384 | tf_op jit(solution)/shard_map/ppermute | solution.py:720
  131.2 0.9 copy-start.2
  136.0 0.6 copy-start.4
  136.6 18.1 %copy-start.7 = (bf16[8,16,4096]{2,1,0:T(8,128)(2,1)}, bf16[8,16,4096]{2,1,0:T(8,128)(2,1)S(1)}, u32[]{:S(2)}) copy-start(bf16[8,16,4096]{2,1,0:T(8,128)(2,1)S(1)} %all-to-all-done.3) | copy-start | bytes 3145732
  136.6 27.0 %all-to-all-start.2 = ((bf16[8,16,4096]{2,1,0:T(8,128)(2,1)}), bf16[8,16,4096]{2,1,0:T(8,128)(2,1)S(1)}, u32[]{:S(2)}, u32[]{:S(2)}) async-start(bf16[8,16,4096]{2,1,0:T(8,128)(2,1)} %get-tuple-element.82), calls=%async_computation.2 | async-start | bytes 2097152 | tf_op jit(solution)/shard_map/all_to_all | solution.py:710
  163.6 1.0 copy-start.6
  173.4 1.6 collective-permute-start.4

commit v5 on v4

--- a/solution.py
+++ b/solution.py
@@ -25,17 +25,6 @@
 
 def mm(a, b, dims=NN):
     return lax.dot_general(a, b, dims, preferred_element_type=f32)
-
-
-def ordered(kernel, in_specs, operands, after, aliases=None):
-    if after is None:
-        return kernel, in_specs, operands, aliases or {}
-
-    def body(after_ref, *refs):
-        kernel(*refs)
-
-    shifted = {key + 1: value for key, value in (aliases or {}).items()}
-    return body, [pl.BlockSpec(memory_space=pl.ANY)] + in_specs, [after] + operands, shifted
 
 
 def split_two(v):
@@ -264,7 +253,7 @@
         gb_ref[...] = mm(mixed.T, c_ref[...])
 
 
-def node_inner(x, cot, b, c, gram, low, src, prior, after, chunk, part, parts, heads, head_width):
+def node_inner(x, cot, b, c, gram, low, src, prior, chunk, part, parts, heads, head_width):
     length, state = b.shape
     width = heads * head_width
     block = min(width // parts, 2 * LANES)
@@ -289,7 +278,6 @@
         operands += list(prior)
         in_specs += [pl.BlockSpec(memory_space=pl.ANY)] * 2
     kernel = functools.partial(inner_kernel, head_width, part * count * block // LANES, aliased)
-    kernel, in_specs, operands, aliases = ordered(kernel, in_specs, operands, after, aliases)
     return pl.pallas_call(
         kernel,
         grid=(count,),
@@ -425,13 +413,13 @@
     return most // 2, most - most // 2
 
 
-def pack_slots(parents, recv, after, nodes, heads, head_width):
+def pack_slots(parents, recv, nodes, heads, head_width):
     half, rows, _ = recv.shape
     width = heads * head_width
     main, more = slot_counts(nodes)
     in_specs = [pl.BlockSpec(memory_space=pltpu.SMEM), pl.BlockSpec(memory_space=pltpu.VMEM)]
     kernel = functools.partial(pack_kernel, heads, head_width)
-    kernel, in_specs, operands, _ = ordered(kernel, in_specs, [parents, recv], after)
+    operands = [parents, recv]
     return pl.pallas_call(
         kernel,
         in_specs=in_specs,
@@ -464,7 +452,6 @@
     main_ref,
     more_ref,
     out_ref,
-    token_ref,
     decay_ref,
     slot_ref,
     chain_ref,
@@ -534,24 +521,20 @@
 
     lax.fori_loop(0, half, visit, 0)
     out_ref[:, :, width:] = back_ref[...].astype(bf16)
-    token_ref[...] = jnp.zeros_like(token_ref)
-
-
-def join_slots(parents, recv, main, more, after, nodes, heads, head_width):
+
+
+def join_slots(parents, recv, main, more, nodes, heads, head_width):
     half, rows, _ = recv.shape
     width = heads * head_width
     in_specs = [pl.BlockSpec(memory_space=pltpu.SMEM)] + [pl.BlockSpec(memory_space=pltpu.VMEM)] * 3
     kernel = functools.partial(join_kernel, heads, head_width)
-    kernel, in_specs, operands, _ = ordered(kernel, in_specs, [parents, recv, main, more], after)
+    operands = [parents, recv, main, more]
     slots = main.shape[0] + more.shape[0]
     return pl.pallas_call(
         kernel,
         in_specs=in_specs,
-        out_specs=[pl.BlockSpec(memory_space=pltpu.VMEM)] * 2,
-        out_shape=[
-            jax.ShapeDtypeStruct((half, rows, 2 * width), bf16),
-            jax.ShapeDtypeStruct((8, LANES), f32),
-        ],
+        out_specs=pl.BlockSpec(memory_space=pltpu.VMEM),
+        out_shape=jax.ShapeDtypeStruct((half, rows, 2 * width), bf16),
         scratch_shapes=[
             pltpu.VMEM((half, width), f32),
             pltpu.VMEM((slots, rows, width), f32),
@@ -627,7 +610,9 @@
                         pieces[shift - 1][n] = ref[pl.ds(at, rows)].astype(bf16)
 
 
-def node_outer(x, cot, b, c, grow, tail, states, inner, grad, found, prior, chunk, heads, head_width):
+def node_outer(
+    x, cot, b, c, grow, tail, states, inner, grad, found, prior, chunk, heads, head_width
+):
     length, state = b.shape
     width = heads * head_width
     block = min(width, 4 * LANES)
@@ -670,8 +655,9 @@
     else:
         out_specs += [pl.BlockSpec((length, state), whole)] * 2
         out_shape += [grads] * 2
+    kernel = functools.partial(outer_kernel, head_width, len(found), final)
     return pl.pallas_call(
-        functools.partial(outer_kernel, head_width, len(found), final),
+        kernel,
         grid=(count,),
         in_specs=in_specs,
         out_specs=out_specs,
@@ -728,26 +714,23 @@
 
     shared = (inputs, cotangent, b_matrix, c_matrix)
     sizes = (heads, head_width)
-    made = [node_states(*shared, step_size, rate, k, *sizes) for k in range(CHUNKS)]
+    made = []
+    for k in range(CHUNKS):
+        made.append(node_states(*shared, step_size, rate, k, *sizes))
     received = [swap(made[k][0]) for k in range(CHUNKS)]
     found = []
     prior = None
-    token = made[CHUNKS - 1][1]
-
-    def inner_part(prior, token, k, part):
-        *prior, gc, gb = node_inner(
-            *shared, made[0][5], made[k][1], made[k][2], prior, token, k, part, PARTS, *sizes
-        )
-        found.append((gb, gc))
-        return prior, gc
-
-    todo = [(k, part) for k in range(CHUNKS) for part in range(PARTS)]
+    for k in range(CHUNKS):
+        for part in range(PARTS):
+            *prior, gc, gb = node_inner(
+                *shared, made[0][5], made[k][1], made[k][2], prior, k, part, PARTS, *sizes
+            )
+            found.append((gb, gc))
+    inner = prior
     packed = []
     for k in range(CHUNKS):
-        prior, token = inner_part(prior, token, *todo.pop(0))
-        main, more = pack_slots(parents, received[k], token, nodes, *sizes)
+        main, more = pack_slots(parents, received[k], nodes, *sizes)
         packed.append((main, more, cross(main)))
-        token = more
     others = lax.cond(
         crowded,
         lambda vs: tuple(cross(v) for v in vs),
@@ -756,12 +739,8 @@
     )
     states = []
     for k in range(CHUNKS):
-        joined, token = join_slots(
-            parents, received[k], packed[k][2], others[k], token, nodes, *sizes
-        )
+        joined = join_slots(parents, received[k], packed[k][2], others[k], nodes, *sizes)
         states.append(swap(joined).reshape(state, -1))
-        prior, token = inner_part(prior, token, *todo.pop(0))
-    inner = prior
     prior = None
     for k in range(CHUNKS):
         result = node_outer(

time: 178 us -> 182 us (1.022)
  waiting for transfers between devices: 56.4 us -> 70.4 us
  starting transfers between devices: 32.5 us -> 26.9 us
  local copies, waits for them, and re-layouts: 7.33 us -> 3.29 us
    all_to_all x4, waiting for transfers between devices: 8.87 us -> 25.3 us  [swap(): lax.all_to_all(v.reshape(half, state // half, v.shape[-1]), 'node', split...]
    unnamed x18 -> x8, local copies, waits for them, and re-layouts: 5.86 us -> 1.05 us
    all_to_all x4, starting transfers between devices: 23 us -> 19.5 us  [swap(): lax.all_to_all(v.reshape(half, state // half, v.shape[-1]), 'node', split...]
    ppermute x4, waiting for transfers between devices: 46 us -> 43.5 us  [cross(): return lax.ppermute(v, 'node', across)]
    ppermute x4, starting transfers between devices: 9.42 us -> 7.36 us  [cross(): return lax.ppermute(v, 'node', across)]
  transfers between devices with their start and end apart: 9 -> 9, of which waited for: 5 -> 6; matrix products, arithmetic and copies ran while one was open for 1% -> 1% of each run, Pallas kernels for 33% -> 32%
where the time goes in v5:
time: 182 us; the launch traced here: 181 us
  Pallas kernels  77.5 us (43%)
  waiting for transfers between devices  70.4 us (39%)
  starting transfers between devices  26.9 us (15%)
  local copies, waits for them, and re-layouts  3.29 us (2%)
    ppermute x4, waiting for transfers between devices, cross(): return lax.ppermute(v, 'node', across)  43.5 us
    pallas_call x4, Pallas kernels, node_inner(): pl.pallas_call(kernel, grid=(count,), in_specs=in_specs, out_specs=[pl.Bl...  35.1 us
    all_to_all x4, waiting for transfers between devices, swap(): lax.all_to_all(v.reshape(half, state // half, v.shape[-1]), 'node', split...  25.3 us
    all_to_all x4, starting transfers between devices, swap(): lax.all_to_all(v.reshape(half, state // half, v.shape[-1]), 'node', split...  19.5 us
    pallas_call x2, Pallas kernels, node_outer(): pl.pallas_call(kernel, grid=(count,), in_specs=in_specs, out_specs=out_sp...  17.7 us
    pallas_call x2, Pallas kernels, node_states(): pl.pallas_call(functools.partial(states_kernel, heads, head_width, chunk)...  12.3 us
    ppermute x4, starting transfers between devices, cross(): return lax.ppermute(v, 'node', across)  7.36 us
    pallas_call x2, Pallas kernels, join_slots(): pl.pallas_call(kernel, in_specs=in_specs, out_specs=pl.BlockSpec(memory_s...  7.26 us
  transfers between devices with their start and end apart: 9, of which 6 were waited for; matrix products, arithmetic and copies ran while one was open for 1% of the time, Pallas kernels for 32%

profile of v5, /device:TPU:0, one launch (start us, length us, event | category | flops | bytes accessed | tf_op | source)
XLA Modules:
  0.0 181.3 jit_solution(9124045034204028774)
XLA Ops:
  0.6 6.2 %node_states.3 = (bf16[128,4224]{1,0:T(8,128)(2,1)}, f32[512,128]{1,0:T(8,128)}, f32[32,512]{1,0:T(8,128)}, bf16[512,128]{1,0:T(8,128)(2,1)}, bf16[512,128]{1,0:T(8,128)(2,1)}, /*index=5*/bf16[512,512]{1,0:T(8,128)(2,1)}) custom-call(bf16[512,4096]{1,0:T(8,128)(2,1)} %x_ref.15, bf16[512,4096]{1,0:T(8,128)(2,1)} %cot_ref.15, bf16[512,128]{1,0:T(8,128)(2,1)} %b_ref.15, ...), custom_call_target="tpu_custom_call" | custom-call | flops 536870912 | bytes 5242880 | tf_op jit(solution)/shard_map/node_states/pallas_call | solution.py:114
  6.8 6.2 %all-to-all-start.1 = ((bf16[8,16,4224]{2,1,0:T(8,128)(2,1)}), bf16[8,16,4224]{2,1,0:T(8,128)(2,1)S(1)}, u32[]{:S(2)}, u32[]{:S(2)}) async-start(bf16[8,16,4224]{2,1,0:T(8,128)(2,1)} %bitcast.14), calls=%async_computation.1 | async-start | bytes 2162688 | tf_op jit(solution)/shard_map/all_to_all | solution.py:696
  13.0 6.2 %node_states.2 = (bf16[128,4224]{1,0:T(8,128)(2,1)}, f32[512,128]{1,0:T(8,128)}, f32[32,512]{1,0:T(8,128)}, bf16[512,128]{1,0:T(8,128)(2,1)}, bf16[512,128]{1,0:T(8,128)(2,1)}, /*index=5*/bf16[512,512]{1,0:T(8,128)(2,1)}) custom-call(bf16[512,4096]{1,0:T(8,128)(2,1)} %x_ref.15, bf16[512,4096]{1,0:T(8,128)(2,1)} %cot_ref.15, bf16[512,128]{1,0:T(8,128)(2,1)} %b_ref.15, ...), custom_call_target="tpu_custom_call" | custom-call | flops 536870912 | bytes 5242880 | tf_op jit(solution)/shard_map/node_states/pallas_call | solution.py:114
  19.2 8.9 %all-to-all-done.1.recv_ref = bf16[8,16,4224]{2,1,0:T(8,128)(2,1)S(1)} async-done(((bf16[8,16,4224]{2,1,0:T(8,128)(2,1)}), bf16[8,16,4224]{2,1,0:T(8,128)(2,1)S(1)}, u32[]{:S(2)}, u32[]{:S(2)}) %all-to-all-start.1) | async-done | bytes 1081376 | tf_op jit(solution)/shard_map/all_to_all | solution.py:696
  28.1 3.6 %all-to-all-start = ((bf16[8,16,4224]{2,1,0:T(8,128)(2,1)}), bf16[8,16,4224]{2,1,0:T(8,128)(2,1)S(1)}, u32[]{:S(2)}, u32[]{:S(2)}) async-start(bf16[8,16,4224]{2,1,0:T(8,128)(2,1)} %bitcast.13), calls=%async_computation | async-start | bytes 2162688 | tf_op jit(solution)/shard_map/all_to_all | solution.py:696
  31.7 2.6 %pack_slots.3 = (bf16[6,16,2176]{2,1,0:T(8,128)(2,1)S(1)}, bf16[6,16,2176]{2,1,0:T(8,128)(2,1)}) custom-call(s32[16]{0:T(128)S(1)} %copy-done, bf16[8,16,4224]{2,1,0:T(8,128)(2,1)S(1)} %all-to-all-done.1.recv_ref), custom_call_target="tpu_custom_call" | custom-call | flops 5242880 | bytes 2097152 | tf_op jit(solution)/shard_map/pack_slots/pallas_call | solution.py:423
  34.2 2.7 %collective-permute-start.3 = (bf16[6,16,2176]{2,1,0:T(8,128)(2,1)S(1)}, bf16[6,16,2176]{2,1,0:T(8,128)(2,1)S(1)}, u32[]{:S(2)}, u32[]{:S(2)}) collective-permute-start(bf16[6,16,2176]{2,1,0:T(8,128)(2,1)S(1)} %get-tuple-element.78), channel_id=1, source_target_pairs={{0,16},{2,18},{4,20},{6,22},{8,24},{10,26},{12,28},{14,30},{16,0},... | collective-permute-start | bytes 1253384 | tf_op jit(solution)/shard_map/ppermute | solution.py:706
  37.0 0.6 convert_reduce_fusion
  38.3 16.5 %all-to-all-done.recv_ref = bf16[8,16,4224]{2,1,0:T(8,128)(2,1)S(1)} async-done(((bf16[8,16,4224]{2,1,0:T(8,128)(2,1)}), bf16[8,16,4224]{2,1,0:T(8,128)(2,1)S(1)}, u32[]{:S(2)}, u32[]{:S(2)}) %all-to-all-start) | async-done | bytes 1081376 | tf_op jit(solution)/shard_map/all_to_all | solution.py:696
  54.8 2.6 %pack_slots.2 = (bf16[6,16,2176]{2,1,0:T(8,128)(2,1)S(1)}, bf16[6,16,2176]{2,1,0:T(8,128)(2,1)}) custom-call(s32[16]{0:T(128)S(1)} %copy-done, bf16[8,16,4224]{2,1,0:T(8,128)(2,1)S(1)} %all-to-all-done.recv_ref), custom_call_target="tpu_custom_call" | custom-call | flops 5242880 | bytes 2097152 | tf_op jit(solution)/shard_map/pack_slots/pallas_call | solution.py:423
  57.4 37.7 %conditional.1 = ((bf16[6,16,2176]{2,1,0:T(8,128)(2,1)}, bf16[6,16,2176]{2,1,0:T(8,128)(2,1)})) conditional(s32[]{:T(128)} %convert_element_type.10, (bf16[6,16,2176]{2,1,0:T(8,128)(2,1)}, bf16[6,16,2176]{2,1,0:T(8,128)(2,1)}) %tuple.15, (bf16[6,16,2176]{2,1,0:T(8,128)(2,1)}, bf16[6,16,2176]{2,1,0:T(8,128)(2,1)}) %tuple.15), branch_computations={%region_2.0_spmd, %region_3.0_spmd} | conditional | bytes 5013608 | solution.py:734
  57.4 2.9 %collective-permute-start.1 = (bf16[6,16,2176]{2,1,0:T(8,128)(2,1)}, bf16[6,16,2176]{2,1,0:T(8,128)(2,1)S(1)}, u32[]{:S(2)}, u32[]{:S(2)}) collective-permute-start(bf16[6,16,2176]{2,1,0:T(8,128)(2,1)} %get-tuple-element.9), channel_id=1, source_target_pairs={{0,16},{2,18},{4,20},{6,22},{8,24},{10,26},{12,28},{14,30},{16,0},... | collective-permute-start | bytes 1253384 | tf_op jit(solution)/shard_map/cond/branch_1_fun/ppermute | solution.py:706
  60.3 25.2 %collective-permute-done = bf16[6,16,2176]{2,1,0:T(8,128)(2,1)S(1)} collective-permute-done((bf16[6,16,2176]{2,1,0:T(8,128)(2,1)}, bf16[6,16,2176]{2,1,0:T(8,128)(2,1)S(1)}, u32[]{:S(2)}, u32[]{:S(2)}) %collective-permute-start) | collective-permute-done | bytes 417824 | tf_op jit(solution)/shard_map/cond/branch_1_fun/ppermute | solution.py:706
  85.5 0.8 copy.21
  86.2 8.1 %collective-permute-done.1 = bf16[6,16,2176]{2,1,0:T(8,128)(2,1)S(1)} collective-permute-done((bf16[6,16,2176]{2,1,0:T(8,128)(2,1)}, bf16[6,16,2176]{2,1,0:T(8,128)(2,1)S(1)}, u32[]{:S(2)}, u32[]{:S(2)}) %collective-permute-start.1) | collective-permute-done | bytes 417824 | tf_op jit(solution)/shard_map/cond/branch_1_fun/ppermute | solution.py:706
  94.3 0.8 copy.22
  95.1 3.8 %join_slots.3 = bf16[8,16,4096]{2,1,0:T(8,128)(2,1)} custom-call(s32[16]{0:T(128)S(1)} %copy-done, bf16[8,16,4224]{2,1,0:T(8,128)(2,1)S(1)} %all-to-all-done.1.recv_ref, bf16[6,16,2176]{2,1,0:T(8,128)(2,1)S(1)} %collective-permute-done.3.main_ref, bf16[6,16,2176]{2,1,0:T(8,128)(2,1)} %get-tuple-element.79.more_ref), custom_call_target="tpu_custom_call" | custom-call | flops 5242880 | bytes 2097152 | tf_op jit(solution)/shard_map/join_slots/pallas_call | solution.py:533
  98.9 3.6 %all-to-all-start.3 = ((bf16[8,16,4096]{2,1,0:T(8,128)(2,1)}), bf16[8,16,4096]{2,1,0:T(8,128)(2,1)S(1)}, u32[]{:S(2)}, u32[]{:S(2)}) async-start(bf16[8,16,4096]{2,1,0:T(8,128)(2,1)} %join_slots.3), calls=%async_computation.3 | async-start | bytes 2097152 | tf_op jit(solution)/shard_map/all_to_all | solution.py:696
  102.5 1.7 collective-permute-start.2
  104.3 8.8 %node_inner.4 = (bf16[512,4096]{1,0:T(8,128)(2,1)}, bf16[512,4096]{1,0:T(8,128)(2,1)}, f32[512,128]{1,0:T(8,128)}, f32[512,128]{1,0:T(8,128)}) custom-call(bf16[512,4096]{1,0:T(8,128)(2,1)} %x_ref.15, bf16[512,4096]{1,0:T(8,128)(2,1)} %cot_ref.15, bf16[512,128]{1,0:T(8,128)(2,1)} %b_ref.15, bf16[512,128]{1,0:T(8,128)(2,1)} %c_ref.15, ...), custom_call_target="tpu_custom_call" | custom-call | flops 6442450944 | bytes 6291456 | tf_op jit(solution)/shard_map/node_inner/pallas_call | solution.py:281
  113.1 10.3 %collective-permute-done.2.main_ref = bf16[6,16,2176]{2,1,0:T(8,128)(2,1)S(1)} collective-permute-done((bf16[6,16,2176]{2,1,0:T(8,128)(2,1)S(1)}, bf16[6,16,2176]{2,1,0:T(8,128)(2,1)S(1)}, u32[]{:S(2)}, u32[]{:S(2)}) %collective-permute-start.2) | collective-permute-done | bytes 417824 | tf_op jit(solution)/shard_map/ppermute | solution.py:706
  123.3 3.4 %join_slots.2 = bf16[8,16,4096]{2,1,0:T(8,128)(2,1)} custom-call(s32[16]{0:T(128)S(1)} %copy-done, bf16[8,16,4224]{2,1,0:T(8,128)(2,1)S(1)} %all-to-all-done.recv_ref, bf16[6,16,2176]{2,1,0:T(8,128)(2,1)S(1)} %collective-permute-done.2.main_ref, bf16[6,16,2176]{2,1,0:T(8,128)(2,1)S(1)} %copy-done.3), custom_call_target="tpu_custom_call" | custom-call | flops 5242880 | bytes 2097152 | tf_op jit(solution)/shard_map/join_slots/pallas_call | solution.py:533
  126.8 6.1 %all-to-all-start.2 = ((bf16[8,16,4096]{2,1,0:T(8,128)(2,1)}), bf16[8,16,4096]{2,1,0:T(8,128)(2,1)S(1)}, u32[]{:S(2)}, u32[]{:S(2)}) async-start(bf16[8,16,4096]{2,1,0:T(8,128)(2,1)} %join_slots.2), calls=%async_computation.2 | async-start | bytes 2097152 | tf_op jit(solution)/shard_map/all_to_all | solution.py:696
  132.9 8.8 %node_inner.5 = (bf16[512,4096]{1,0:T(8,128)(2,1)}, bf16[512,4096]{1,0:T(8,128)(2,1)}, f32[512,128]{1,0:T(8,128)}, f32[512,128]{1,0:T(8,128)}) custom-call(bf16[512,4096]{1,0:T(8,128)(2,1)} %x_ref.15, bf16[512,4096]{1,0:T(8,128)(2,1)} %cot_ref.15, bf16[512,128]{1,0:T(8,128)(2,1)} %b_ref.15, ...), custom_call_target="tpu_custom_call", output_to_operand_aliasing={{0}: (7, {}), {1}: (8, {})} | custom-call | flops 6442450944 | bytes 6291456 | tf_op jit(solution)/shard_map/node_inner/pallas_call | solution.py:281
  141.7 8.8 %node_inner.6 = (bf16[512,4096]{1,0:T(8,128)(2,1)}, bf16[512,4096]{1,0:T(8,128)(2,1)}, f32[512,128]{1,0:T(8,128)}, f32[512,128]{1,0:T(8,128)}) custom-call(bf16[512,4096]{1,0:T(8,128)(2,1)} %x_ref.15, bf16[512,4096]{1,0:T(8,128)(2,1)} %cot_ref.15, bf16[512,128]{1,0:T(8,128)(2,1)} %b_ref.15, ...), custom_call_target="tpu_custom_call", output_to_operand_aliasing={{0}: (7, {}), {1}: (8, {})} | custom-call | flops 6442450944 | bytes 6291456 | tf_op jit(solution)/shard_map/node_inner/pallas_call | solution.py:281
  150.4 8.8 %node_inner.7 = (bf16[512,4096]{1,0:T(8,128)(2,1)}, bf16[512,4096]{1,0:T(8,128)(2,1)}, f32[512,128]{1,0:T(8,128)}, f32[512,128]{1,0:T(8,128)}) custom-call(bf16[512,4096]{1,0:T(8,128)(2,1)} %x_ref.15, bf16[512,4096]{1,0:T(8,128)(2,1)} %cot_ref.15, bf16[512,128]{1,0:T(8,128)(2,1)} %b_ref.15, ...), custom_call_target="tpu_custom_call", output_to_operand_aliasing={{0}: (7, {}), {1}: (8, {})} | custom-call | flops 6442450944 | bytes 6291456 | tf_op jit(solution)/shard_map/node_inner/pallas_call | solution.py:281
  159.2 8.9 %node_outer.2 = (bf16[512,4096]{1,0:T(8,128)(2,1)}, bf16[512,4096]{1,0:T(8,128)(2,1)}, f32[512,128]{1,0:T(8,128)}, f32[512,128]{1,0:T(8,128)}) custom-call(bf16[512,4096]{1,0:T(8,128)(2,1)} %x_ref.15, bf16[512,4096]{1,0:T(8,128)(2,1)} %cot_ref.15, bf16[512,128]{1,0:T(8,128)(2,1)} %b_ref.15, bf16[512,128]{1,0:T(8,128)(2,1)} %c_ref.15, ...), custom_call_target="tpu_custom_call" | custom-call | flops 1073741824 | bytes 12582912 | tf_op jit(solution)/shard_map/node_outer/pallas_call | solution.py:659
  168.1 1.0 copy-done.1
  169.2 8.8 %node_outer.3 = (bf16[512,4096]{1,0:T(8,128)(2,1)}, bf16[512,4096]{1,0:T(8,128)(2,1)}, f32[2,256,128]{2,1,0:T(8,128)}, bf16[2,256,128]{2,1,0:T(8,128)(2,1)}) custom-call(bf16[512,4096]{1,0:T(8,128)(2,1)} %x_ref.15, bf16[512,4096]{1,0:T(8,128)(2,1)} %cot_ref.15, bf16[512,128]{1,0:T(8,128)(2,1)} %b_ref.15, ...), custom_call_target="tpu_custom_call", output_to_operand_aliasing={{0}: (12, {}), {1}: (13, {})} | custom-call | flops 1073741824 | bytes 12582912 | tf_op jit(solution)/shard_map/node_outer/pallas_call | solution.py:659
  178.0 1.5 collective-permute-done.4
  179.6 1.0 convert_add_fusion
  180.6 0.7 slice_bitcast_fusion
  (14 shorter events, 0.2 us)
Async XLA Ops:
  6.8 21.3 %all-to-all-start.1 = ((bf16[8,16,4224]{2,1,0:T(8,128)(2,1)}), bf16[8,16,4224]{2,1,0:T(8,128)(2,1)S(1)}, u32[]{:S(2)}, u32[]{:S(2)}) async-start(bf16[8,16,4224]{2,1,0:T(8,128)(2,1)} %bitcast.14), calls=%async_computation.1 | async-start | bytes 2162688 | tf_op jit(solution)/shard_map/all_to_all | solution.py:696
  13.0 18.6 %copy-start = (s32[16]{0:T(128)S(1)}, s32[16]{0:T(128)}, u32[]{:S(2)}) copy-start(s32[16]{0:T(128)} %parents_ref.7) | copy-start | bytes 196
  28.1 26.7 %all-to-all-start = ((bf16[8,16,4224]{2,1,0:T(8,128)(2,1)}), bf16[8,16,4224]{2,1,0:T(8,128)(2,1)S(1)}, u32[]{:S(2)}, u32[]{:S(2)}) async-start(bf16[8,16,4224]{2,1,0:T(8,128)(2,1)} %bitcast.13), calls=%async_computation | async-start | bytes 2162688 | tf_op jit(solution)/shard_map/all_to_all | solution.py:696
  34.2 60.9 %collective-permute-start.3 = (bf16[6,16,2176]{2,1,0:T(8,128)(2,1)S(1)}, bf16[6,16,2176]{2,1,0:T(8,128)(2,1)S(1)}, u32[]{:S(2)}, u32[]{:S(2)}) collective-permute-start(bf16[6,16,2176]{2,1,0:T(8,128)(2,1)S(1)} %get-tuple-element.78), channel_id=1, source_target_pairs={{0,16},{2,18},{4,20},{6,22},{8,24},{10,26},{12,28},{14,30},{16,0},... | collective-permute-start | bytes 1253384 | tf_op jit(solution)/shard_map/ppermute | solution.py:706
  57.4 28.1 %collective-permute-start = (bf16[6,16,2176]{2,1,0:T(8,128)(2,1)}, bf16[6,16,2176]{2,1,0:T(8,128)(2,1)S(1)}, u32[]{:S(2)}, u32[]{:S(2)}) collective-permute-start(bf16[6,16,2176]{2,1,0:T(8,128)(2,1)} %get-tuple-element.8), channel_id=1, source_target_pairs={{0,16},{2,18},{4,20},{6,22},{8,24},{10,26},{12,28},{14,30},{16,0},... | collective-permute-start | bytes 1253384 | tf_op jit(solution)/shard_map/cond/branch_1_fun/ppermute | solution.py:706
  57.4 37.0 %collective-permute-start.1 = (bf16[6,16,2176]{2,1,0:T(8,128)(2,1)}, bf16[6,16,2176]{2,1,0:T(8,128)(2,1)S(1)}, u32[]{:S(2)}, u32[]{:S(2)}) collective-permute-start(bf16[6,16,2176]{2,1,0:T(8,128)(2,1)} %get-tuple-element.9), channel_id=1, source_target_pairs={{0,16},{2,18},{4,20},{6,22},{8,24},{10,26},{12,28},{14,30},{16,0},... | collective-permute-start | bytes 1253384 | tf_op jit(solution)/shard_map/cond/branch_1_fun/ppermute | solution.py:706
  98.9 27.9 %all-to-all-start.3 = ((bf16[8,16,4096]{2,1,0:T(8,128)(2,1)}), bf16[8,16,4096]{2,1,0:T(8,128)(2,1)S(1)}, u32[]{:S(2)}, u32[]{:S(2)}) async-start(bf16[8,16,4096]{2,1,0:T(8,128)(2,1)} %join_slots.3), calls=%async_computation.3 | async-start | bytes 2097152 | tf_op jit(solution)/shard_map/all_to_all | solution.py:696
  102.5 20.8 %collective-permute-start.2 = (bf16[6,16,2176]{2,1,0:T(8,128)(2,1)S(1)}, bf16[6,16,2176]{2,1,0:T(8,128)(2,1)S(1)}, u32[]{:S(2)}, u32[]{:S(2)}) collective-permute-start(bf16[6,16,2176]{2,1,0:T(8,128)(2,1)S(1)} %get-tuple-element.58), channel_id=1, source_target_pairs={{0,16},{2,18},{4,20},{6,22},{8,24},{10,26},{12,28},{14,30},{16,0},... | collective-permute-start | bytes 1253384 | tf_op jit(solution)/shard_map/ppermute | solution.py:706
  104.3 19.1 %copy-start.3 = (bf16[6,16,2176]{2,1,0:T(8,128)(2,1)S(1)}, bf16[6,16,2176]{2,1,0:T(8,128)(2,1)}, u32[]{:S(2)}) copy-start(bf16[6,16,2176]{2,1,0:T(8,128)(2,1)} %get-tuple-element.62.more_ref) | copy-start | bytes 1253380
  126.8 14.9 %copy-start.2 = (bf16[8,16,4096]{2,1,0:T(8,128)(2,1)}, bf16[8,16,4096]{2,1,0:T(8,128)(2,1)S(1)}, u32[]{:S(2)}) copy-start(bf16[8,16,4096]{2,1,0:T(8,128)(2,1)S(1)} %all-to-all-done.3) | copy-start | bytes 3145732
  126.8 41.3 %all-to-all-start.2 = ((bf16[8,16,4096]{2,1,0:T(8,128)(2,1)}), bf16[8,16,4096]{2,1,0:T(8,128)(2,1)S(1)}, u32[]{:S(2)}, u32[]{:S(2)}) async-start(bf16[8,16,4096]{2,1,0:T(8,128)(2,1)} %join_slots.2), calls=%async_computation.2 | async-start | bytes 2097152 | tf_op jit(solution)/shard_map/all_to_all | solution.py:696
  168.1 1.0 copy-start.1
  177.9 1.6 collective-permute-start.4

commit v6 on v5

--- a/solution.py
+++ b/solution.py
@@ -12,6 +12,7 @@
 LEVELS = 3
 VMEM_BYTES = 24 << 20
 LANES = 128
+SUBLANES = 8
 CHUNKS = 2
 PARTS = 2
 
@@ -48,6 +49,11 @@
     if gap:
         v = jnp.concatenate([v, jnp.zeros((gap, v.shape[1]), v.dtype)], axis=0)
     return v.T
+
+
+def half_steps(step_ref, spread):
+    steps = mm(step_ref[...], spread)
+    return steps[:1], steps[SUBLANES : SUBLANES + 1]
 
 
 def states_kernel(
@@ -66,11 +72,14 @@
     grow_ref,
     tail_ref,
     gram_ref,
+    keep_ref,
+    step_out_ref,
     bt_ref,
     ct_ref,
 ):
     block = x_ref.shape[1]
     length = step_ref.shape[1]
+    middle = length // 2
     index = pl.program_id(0)
     width = heads * head_width
 
@@ -87,22 +96,37 @@
         second, third = split_two(rest)
         cumulative = mm(third, upper) + mm(second, upper) + mm(first, upper)
         last = cumulative[:, length - 1 :]
+        mid = cumulative[:, middle - 1 : middle]
+        late = lax.broadcasted_iota(jnp.int32, cumulative.shape, 1) >= middle
         low_ref[...] = pad_lanes(cumulative * LOG2E)
         src_ref[...] = (cumulative - jnp.log(step)) * LOG2E
-        grow_ref[...] = pad_lanes(jnp.exp(cumulative)).astype(bf16)
-        tail_ref[...] = pad_lanes(jnp.exp(last - cumulative) * step).astype(bf16)
+        grow_ref[...] = pad_lanes(jnp.exp(cumulative - jnp.where(late, mid, 0.0))).astype(bf16)
+        tail = jnp.exp(jnp.where(late, last, mid) - cumulative) * step
+        tail_ref[...] = pad_lanes(tail).astype(bf16)
         bt_ref[...] = b_ref[...].T
         ct_ref[...] = c_ref[...].T
         total = jnp.exp(jnp.broadcast_to(last, (heads, send_ref.shape[0])))
         send_ref[:, 2 * width :] = pad_lanes(total).astype(bf16)
-        gram_ref[...] = mm(c_ref[...], b_ref[...], NT).astype(bf16)
+        each = (heads, SUBLANES)
+        steps = [jnp.broadcast_to(mid, each), jnp.broadcast_to(last - mid, each)]
+        step_out_ref[...] = pad_lanes(jnp.exp(jnp.concatenate(steps, axis=1))).astype(bf16)
+        for rows in (slice(0, middle), slice(middle, length)):
+            gram_ref[rows] = mm(c_ref[rows], b_ref[rows], NT).astype(bf16)
 
     spread = spread_matrix(LANES, block, head_width, index * block)
     tailed = mm(tail_ref[...], spread).astype(bf16) * x_ref[...]
     emitted = mm(grow_ref[...], spread).astype(bf16) * cot_ref[...]
-    at = pl.multiple_of(index * block, block)
-    send_ref[:, pl.ds(at, block)] = mm(bt_ref[...], tailed).astype(bf16)
-    send_ref[:, pl.ds(at + width, block)] = mm(ct_ref[...], emitted).astype(bf16)
+    early_step, late_step = half_steps(step_out_ref, spread)
+    early_state = mm(bt_ref[:, :middle], tailed[:middle])
+    late_state = mm(bt_ref[:, middle:], tailed[middle:])
+    early_seed = mm(ct_ref[:, :middle], emitted[:middle])
+    late_seed = mm(ct_ref[:, middle:], emitted[middle:])
+    here = pl.ds(pl.multiple_of(index * block, block), block)
+    there = pl.ds(pl.multiple_of(index * block + width, LANES), block)
+    send_ref[:, here] = (late_step * early_state + late_state).astype(bf16)
+    send_ref[:, there] = (early_seed + early_step * late_seed).astype(bf16)
+    keep_ref[:, here] = early_state.astype(bf16)
+    keep_ref[:, there] = late_seed.astype(bf16)
 
 
 def node_states(x, cot, b, c, step, rate, chunk, heads, head_width):
@@ -128,7 +152,9 @@
             pl.BlockSpec((heads, length), whole),
             pl.BlockSpec((length, LANES), whole),
             pl.BlockSpec((length, LANES), whole),
-            pl.BlockSpec((length, length), whole),
+            pl.BlockSpec((length, length // 2), whole),
+            pl.BlockSpec((state, 2 * width), whole),
+            pl.BlockSpec((2 * SUBLANES, LANES), whole),
         ],
         out_shape=[
             jax.ShapeDtypeStruct((state, 2 * width + LANES), bf16),
@@ -136,7 +162,9 @@
             jax.ShapeDtypeStruct((heads, length), f32),
             jax.ShapeDtypeStruct((length, LANES), bf16),
             jax.ShapeDtypeStruct((length, LANES), bf16),
-            jax.ShapeDtypeStruct((length, length), bf16),
+            jax.ShapeDtypeStruct((length, length // 2), bf16),
+            jax.ShapeDtypeStruct((state, 2 * width), bf16),
+            jax.ShapeDtypeStruct((2 * SUBLANES, LANES), bf16),
         ],
         scratch_shapes=[pltpu.VMEM((state, length), bf16), pltpu.VMEM((state, length), bf16)],
         name="node_states",
@@ -168,8 +196,8 @@
     index = pl.program_id(0)
     pack = LANES // head_width
     pairs = x_ref.shape[1] // LANES
-    wide = 2 * LANES
-    tiles = length // wide
+    wide = length // 2
+    blocks = wide // LANES
     weights = (wa_ref, wb_ref)
 
     @pl.when(index == 0)
@@ -183,6 +211,7 @@
     causal = lax.broadcasted_iota(jnp.int32, (LANES, LANES), 0) >= lax.broadcasted_iota(
         jnp.int32, (LANES, LANES), 1
     )
+    halves = (slice(0, wide), slice(wide, length))
     xs = [x_ref[:, q * LANES : (q + 1) * LANES] for q in range(pairs)]
     turned_cots = [cot_ref[:, q * LANES : (q + 1) * LANES].T for q in range(pairs)]
     low = low_ref[...]
@@ -195,36 +224,31 @@
         place = (first + index * pairs + q) * pack + a
         column = head_lanes(low, place, LANES)
         source = src_ref[pl.ds(place, 1), :]
-        for tile in range(tiles):
-            scores = mm(cot[tile * wide :], xs[q][tile * wide : (tile + 1) * wide], NT)
-            for i in range(2 * tile, 2 * tiles):
-                rows = slice(i * LANES, (i + 1) * LANES)
-                here = slice((i - 2 * tile) * LANES, (i - 2 * tile + 1) * LANES)
-                for j in range(2 * tile, min(2 * tile + 1, i) + 1):
+        for part in halves:
+            scores = mm(cot[part], xs[q][part], NT)
+            for i in range(blocks):
+                here = slice(i * LANES, (i + 1) * LANES)
+                rows = slice(part.start + here.start, part.start + here.stop)
+                for j in range(i + 1):
                     cols = slice(j * LANES, (j + 1) * LANES)
-                    side = slice((j - 2 * tile) * LANES, (j - 2 * tile + 1) * LANES)
-                    differ = column[rows] - source[:, cols]
+                    differ = column[rows] - source[:, part.start + cols.start : part.start + cols.stop]
                     if i == j:
                         differ = jnp.where(causal, differ, -jnp.inf)
                     decay = jnp.exp2(differ)
                     w[rows, cols] = decay.astype(bf16) * gram_ref[rows, cols]
-                    mixed_ref[rows, cols] += decay * scores[here, side]
+                    mixed_ref[rows, cols] += decay * scores[here, cols]
                 yield
 
     def products(h):
         q, a = h // pack, h % pack
         w = weights[h % 2]
-        x = xs[q]
-        part = turned_cots[q][a * head_width : (a + 1) * head_width]
+        turned = turned_cots[q][a * head_width : (a + 1) * head_width]
         mine = slice(q * LANES + a * head_width, q * LANES + (a + 1) * head_width)
         own = slice(a * head_width, (a + 1) * head_width)
-        for tile in range(tiles):
-            rows = slice(tile * wide, (tile + 1) * wide)
-            found = mm(w[rows, : (tile + 1) * wide], x[: (tile + 1) * wide])
-            out_ref[rows, mine] = found[:, own].astype(bf16)
+        for part in halves:
+            out_ref[part, mine] = mm(w[part], xs[q][part])[:, own].astype(bf16)
             yield
-            found = mm(part[:, tile * wide :], w[tile * wide :, rows])
-            turned_ref[mine, rows] = found.astype(bf16)
+            turned_ref[mine, part] = mm(turned[:, part], w[part]).astype(bf16)
             yield
 
     def finish(q):
@@ -248,9 +272,10 @@
 
     @pl.when(index == pl.num_programs(0) - 1)
     def _():
-        mixed = mixed_ref[...].astype(bf16)
-        gc_ref[...] = mm(mixed, b_ref[...])
-        gb_ref[...] = mm(mixed.T, c_ref[...])
+        for part in halves:
+            mixed = mixed_ref[part].astype(bf16)
+            gc_ref[part] = mm(mixed, b_ref[part])
+            gb_ref[part] = mm(mixed.T, c_ref[part])
 
 
 def node_inner(x, cot, b, c, gram, low, src, prior, chunk, part, parts, heads, head_width):
@@ -268,7 +293,7 @@
         pl.BlockSpec((length, block), place),
         pl.BlockSpec((length, state), whole),
         pl.BlockSpec((length, state), whole),
-        pl.BlockSpec((length, length), whole),
+        pl.BlockSpec((length, length // 2), whole),
         pl.BlockSpec((length, LANES), whole),
         pl.BlockSpec((heads, length), whole),
     ]
@@ -295,11 +320,11 @@
             jax.ShapeDtypeStruct((length, state), f32),
         ],
         scratch_shapes=[
-            pltpu.VMEM((length, length), f32),
+            pltpu.VMEM((length, length // 2), f32),
             pltpu.VMEM((block, length), bf16),
-            pltpu.VMEM((length, length), bf16),
-            pltpu.VMEM((length, length), bf16),
-            pltpu.VMEM((length, length), bf16),
+            pltpu.VMEM((length, length // 2), bf16),
+            pltpu.VMEM((length, length // 2), bf16),
+            pltpu.VMEM((length, length // 2), bf16),
         ],
         input_output_aliases=aliases,
         name="node_inner",
@@ -564,6 +589,9 @@
     tail_ref,
     start_ref,
     back_ref,
+    early_ref,
+    late_ref,
+    step_ref,
     inner_ref,
     grad_ref,
     *refs,
@@ -587,12 +615,21 @@
     spread = spread_matrix(LANES, block, head_width, index * block)
     grow_wide = mm(grow_ref[...], spread)
     tail_wide = mm(tail_ref[...], spread)
+    early_step, late_step = half_steps(step_ref, spread)
     start = start_ref[...]
     back = back_ref[...]
-    out_ref[...] = (inner_ref[...].astype(f32) + grow_wide * mm(c_ref[...], start)).astype(bf16)
-    gx_ref[...] = (grad_ref[...].astype(f32) + tail_wide * mm(b_ref[...], back)).astype(bf16)
-    gc_ref[...] += mm(grow_wide.astype(bf16) * cot_ref[...], start, NT)
-    gb_ref[...] += mm(tail_wide.astype(bf16) * x_ref[...], back, NT)
+    starts = (start, (early_step * start.astype(f32) + early_ref[...].astype(f32)).astype(bf16))
+    backs = ((late_step * back.astype(f32) + late_ref[...].astype(f32)).astype(bf16), back)
+    middle = x_ref.shape[0] // 2
+    for n, part in enumerate((slice(0, middle), slice(middle, 2 * middle))):
+        grow = grow_wide[part]
+        tail = tail_wide[part]
+        carried = grow * mm(c_ref[part], starts[n])
+        out_ref[part] = (inner_ref[part].astype(f32) + carried).astype(bf16)
+        carried = tail * mm(b_ref[part], backs[n])
+        gx_ref[part] = (grad_ref[part].astype(f32) + carried).astype(bf16)
+        gc_ref[part] += mm(grow.astype(bf16) * cot_ref[part], starts[n], NT)
+        gb_ref[part] += mm(tail.astype(bf16) * x_ref[part], backs[n], NT)
 
     if final:
 
@@ -611,7 +648,7 @@
 
 
 def node_outer(
-    x, cot, b, c, grow, tail, states, inner, grad, found, prior, chunk, heads, head_width
+    x, cot, b, c, grow, tail, states, keep, steps, inner, grad, found, prior, chunk, heads, head_width
 ):
     length, state = b.shape
     width = heads * head_width
@@ -621,7 +658,7 @@
     spot = lambda i: (0, i)
     place = lambda i: (0, chunk * count + i)
     final = prior is not None
-    operands = [x, cot, b, c, grow, tail, states, states, inner, grad]
+    operands = [x, cot, b, c, grow, tail, states, states, keep, keep, steps, inner, grad]
     in_specs = [
         pl.BlockSpec((length, block), place),
         pl.BlockSpec((length, block), place),
@@ -631,6 +668,9 @@
         pl.BlockSpec((length, LANES), whole),
         pl.BlockSpec((state, block), spot),
         pl.BlockSpec((state, block), lambda i: (0, count + i)),
+        pl.BlockSpec((state, block), spot),
+        pl.BlockSpec((state, block), lambda i: (0, count + i)),
+        pl.BlockSpec((2 * SUBLANES, LANES), whole),
         pl.BlockSpec((length, block), place),
         pl.BlockSpec((length, block), place),
     ]
@@ -744,7 +784,7 @@
     prior = None
     for k in range(CHUNKS):
         result = node_outer(
-            *shared, made[k][3], made[k][4], states[k], *inner, found, prior, k, *sizes
+            *shared, *made[k][3:5], states[k], *made[k][6:8], *inner, found, prior, k, *sizes
         )
         prior = result[:2]
         if k == 0:

time: 182 us -> 178 us (0.978)
  Pallas kernels: 77.5 us -> 72.1 us
    pallas_call x4, Pallas kernels: 35.1 us -> 27.5 us  [node_inner(): pl.pallas_call(kernel, grid=(count,), in_specs=in_specs, out_specs=[pl.Bl...]
    ppermute x4, waiting for transfers between devices: 43.5 us -> 45.5 us  [cross(): return lax.ppermute(v, 'node', across)]
  transfers between devices with their start and end apart: 9 -> 9, of which waited for: 6 -> 6; matrix products, arithmetic and copies ran while one was open for 1% -> 1% of each run, Pallas kernels for 32% -> 30%
where the time goes in v6:
time: 178 us; the launch traced here: 177 us
  Pallas kernels  72.1 us (41%)
  waiting for transfers between devices  71.8 us (40%)
  starting transfers between devices  27 us (15%)
  local copies, waits for them, and re-layouts  3.23 us (2%)
    ppermute x4, waiting for transfers between devices, cross(): return lax.ppermute(v, 'node', across)  45.5 us
    pallas_call x4, Pallas kernels, node_inner(): pl.pallas_call(kernel, grid=(count,), in_specs=in_specs, out_specs=[pl.Bl...  27.5 us
    all_to_all x4, waiting for transfers between devices, swap(): lax.all_to_all(v.reshape(half, state // half, v.shape[-1]), 'node', split...  24.8 us
    all_to_all x4, starting transfers between devices, swap(): lax.all_to_all(v.reshape(half, state // half, v.shape[-1]), 'node', split...  19.5 us
    pallas_call x2, Pallas kernels, node_outer(): pl.pallas_call(kernel, grid=(count,), in_specs=in_specs, out_specs=out_sp...  18.9 us
    pallas_call x2, Pallas kernels, node_states(): pl.pallas_call(functools.partial(states_kernel, heads, head_width, chunk)...  13.3 us
    ppermute x4, starting transfers between devices, cross(): return lax.ppermute(v, 'node', across)  7.36 us
    pallas_call x2, Pallas kernels, join_slots(): pl.pallas_call(kernel, in_specs=in_specs, out_specs=pl.BlockSpec(memory_s...  7.19 us
  transfers between devices with their start and end apart: 9, of which 6 were waited for; matrix products, arithmetic and copies ran while one was open for 1% of the time, Pallas kernels for 30%

profile of v6, /device:TPU:0, one launch (start us, length us, event | category | flops | bytes accessed | tf_op | source)
XLA Modules:
  0.0 177.2 jit_solution(5239257340362272615)
XLA Ops:
  0.6 6.7 %node_states.3 = (bf16[128,4224]{1,0:T(8,128)(2,1)}, f32[512,128]{1,0:T(8,128)}, f32[32,512]{1,0:T(8,128)}, bf16[512,128]{1,0:T(8,128)(2,1)}, bf16[512,128]{1,0:...) custom-call(bf16[512,4096]{1,0:T(8,128)(2,1)} %x_ref.15, ...), custom_call_target="tpu_custom_call" | custom-call | flops 536870912 | bytes 5242880 | tf_op jit(solution)/shard_map/node_states/pallas_call | solution.py:138
  7.3 6.2 %all-to-all-start.1 = ((bf16[8,16,4224]{2,1,0:T(8,128)(2,1)}), bf16[8,16,4224]{2,1,0:T(8,128)(2,1)S(1)}, u32[]{:S(2)}, u32[]{:S(2)}) async-start(bf16[8,16,4224]{2,1,0:T(8,128)(2,1)} %bitcast.14), calls=%async_computation.1 | async-start | bytes 2162688 | tf_op jit(solution)/shard_map/all_to_all | solution.py:736
  13.5 6.7 %node_states.2 = (bf16[128,4224]{1,0:T(8,128)(2,1)}, f32[512,128]{1,0:T(8,128)}, f32[32,512]{1,0:T(8,128)}, bf16[512,128]{1,0:T(8,128)(2,1)}, bf16[512,128]{1,0:...) custom-call(bf16[512,4096]{1,0:T(8,128)(2,1)} %x_ref.15, ...), custom_call_target="tpu_custom_call" | custom-call | flops 536870912 | bytes 5242880 | tf_op jit(solution)/shard_map/node_states/pallas_call | solution.py:138
  20.2 8.4 %all-to-all-done.1.recv_ref = bf16[8,16,4224]{2,1,0:T(8,128)(2,1)S(1)} async-done(((bf16[8,16,4224]{2,1,0:T(8,128)(2,1)}), bf16[8,16,4224]{2,1,0:T(8,128)(2,1)S(1)}, u32[]{:S(2)}, u32[]{:S(2)}) %all-to-all-start.1) | async-done | bytes 1081376 | tf_op jit(solution)/shard_map/all_to_all | solution.py:736
  28.6 3.6 %all-to-all-start = ((bf16[8,16,4224]{2,1,0:T(8,128)(2,1)}), bf16[8,16,4224]{2,1,0:T(8,128)(2,1)S(1)}, u32[]{:S(2)}, u32[]{:S(2)}) async-start(bf16[8,16,4224]{2,1,0:T(8,128)(2,1)} %bitcast.13), calls=%async_computation | async-start | bytes 2162688 | tf_op jit(solution)/shard_map/all_to_all | solution.py:736
  32.1 2.6 %pack_slots.3 = (bf16[6,16,2176]{2,1,0:T(8,128)(2,1)S(1)}, bf16[6,16,2176]{2,1,0:T(8,128)(2,1)}) custom-call(s32[16]{0:T(128)S(1)} %copy-done, bf16[8,16,4224]{2,1,0:T(8,128)(2,1)S(1)} %all-to-all-done.1.recv_ref), custom_call_target="tpu_custom_call" | custom-call | flops 5242880 | bytes 2097152 | tf_op jit(solution)/shard_map/pack_slots/pallas_call | solution.py:448
  34.7 2.7 %collective-permute-start.3 = (bf16[6,16,2176]{2,1,0:T(8,128)(2,1)S(1)}, bf16[6,16,2176]{2,1,0:T(8,128)(2,1)S(1)}, u32[]{:S(2)}, u32[]{:S(2)}) collective-permute-start(bf16[6,16,2176]{2,1,0:T(8,128)(2,1)S(1)} %get-tuple-element.84), channel_id=1, source_target_pairs={{0,16},{2,18},{4,20},{6,22},{8,24},{10,26},{12,28},{14,30},{16,0},... | collective-permute-start | bytes 1253384 | tf_op jit(solution)/shard_map/ppermute | solution.py:746
  37.5 0.6 convert_reduce_fusion
  38.8 16.5 %all-to-all-done.recv_ref = bf16[8,16,4224]{2,1,0:T(8,128)(2,1)S(1)} async-done(((bf16[8,16,4224]{2,1,0:T(8,128)(2,1)}), bf16[8,16,4224]{2,1,0:T(8,128)(2,1)S(1)}, u32[]{:S(2)}, u32[]{:S(2)}) %all-to-all-start) | async-done | bytes 1081376 | tf_op jit(solution)/shard_map/all_to_all | solution.py:736
  55.3 2.6 %pack_slots.2 = (bf16[6,16,2176]{2,1,0:T(8,128)(2,1)S(1)}, bf16[6,16,2176]{2,1,0:T(8,128)(2,1)}) custom-call(s32[16]{0:T(128)S(1)} %copy-done, bf16[8,16,4224]{2,1,0:T(8,128)(2,1)S(1)} %all-to-all-done.recv_ref), custom_call_target="tpu_custom_call" | custom-call | flops 5242880 | bytes 2097152 | tf_op jit(solution)/shard_map/pack_slots/pallas_call | solution.py:448
  57.8 37.7 %conditional.1 = ((bf16[6,16,2176]{2,1,0:T(8,128)(2,1)}, bf16[6,16,2176]{2,1,0:T(8,128)(2,1)})) conditional(s32[]{:T(128)} %convert_element_type.10, (bf16[6,16,2176]{2,1,0:T(8,128)(2,1)}, bf16[6,16,2176]{2,1,0:T(8,128)(2,1)}) %tuple.15, (bf16[6,16,2176]{2,1,0:T(8,128)(2,1)}, bf16[6,16,2176]{2,1,0:T(8,128)(2,1)}) %tuple.15), branch_computations={%region_2.0_spmd, %region_3.0_spmd} | conditional | bytes 5013608 | solution.py:774
  57.8 2.9 %collective-permute-start.1 = (bf16[6,16,2176]{2,1,0:T(8,128)(2,1)}, bf16[6,16,2176]{2,1,0:T(8,128)(2,1)S(1)}, u32[]{:S(2)}, u32[]{:S(2)}) collective-permute-start(bf16[6,16,2176]{2,1,0:T(8,128)(2,1)} %get-tuple-element.9), channel_id=1, source_target_pairs={{0,16},{2,18},{4,20},{6,22},{8,24},{10,26},{12,28},{14,30},{16,0},... | collective-permute-start | bytes 1253384 | tf_op jit(solution)/shard_map/cond/branch_1_fun/ppermute | solution.py:746
  60.8 25.2 %collective-permute-done = bf16[6,16,2176]{2,1,0:T(8,128)(2,1)S(1)} collective-permute-done((bf16[6,16,2176]{2,1,0:T(8,128)(2,1)}, bf16[6,16,2176]{2,1,0:T(8,128)(2,1)S(1)}, u32[]{:S(2)}, u32[]{:S(2)}) %collective-permute-start) | collective-permute-done | bytes 417824 | tf_op jit(solution)/shard_map/cond/branch_1_fun/ppermute | solution.py:746
  86.0 0.8 copy.21
  86.7 8.1 %collective-permute-done.1 = bf16[6,16,2176]{2,1,0:T(8,128)(2,1)S(1)} collective-permute-done((bf16[6,16,2176]{2,1,0:T(8,128)(2,1)}, bf16[6,16,2176]{2,1,0:T(8,128)(2,1)S(1)}, u32[]{:S(2)}, u32[]{:S(2)}) %collective-permute-start.1) | collective-permute-done | bytes 417824 | tf_op jit(solution)/shard_map/cond/branch_1_fun/ppermute | solution.py:746
  94.8 0.8 copy.22
  95.6 3.8 %join_slots.3 = bf16[8,16,4096]{2,1,0:T(8,128)(2,1)} custom-call(s32[16]{0:T(128)S(1)} %copy-done, bf16[8,16,4224]{2,1,0:T(8,128)(2,1)S(1)} %all-to-all-done.1.recv_ref, bf16[6,16,2176]{2,1,0:T(8,128)(2,1)S(1)} %collective-permute-done.3.main_ref, bf16[6,16,2176]{2,1,0:T(8,128)(2,1)} %get-tuple-element.85.more_ref), custom_call_target="tpu_custom_call" | custom-call | flops 5242880 | bytes 2097152 | tf_op jit(solution)/shard_map/join_slots/pallas_call | solution.py:558
  99.4 3.6 %all-to-all-start.3 = ((bf16[8,16,4096]{2,1,0:T(8,128)(2,1)}), bf16[8,16,4096]{2,1,0:T(8,128)(2,1)S(1)}, u32[]{:S(2)}, u32[]{:S(2)}) async-start(bf16[8,16,4096]{2,1,0:T(8,128)(2,1)} %join_slots.3), calls=%async_computation.3 | async-start | bytes 2097152 | tf_op jit(solution)/shard_map/all_to_all | solution.py:736
  103.0 1.7 collective-permute-start.2
  104.8 6.9 %node_inner.4 = (bf16[512,4096]{1,0:T(8,128)(2,1)}, bf16[512,4096]{1,0:T(8,128)(2,1)}, f32[512,128]{1,0:T(8,128)}, f32[512,128]{1,0:T(8,128)}) custom-call(bf16[512,4096]{1,0:T(8,128)(2,1)} %x_ref.15, bf16[512,4096]{1,0:T(8,128)(2,1)} %cot_ref.15, bf16[512,128]{1,0:T(8,128)(2,1)} %b_ref.15, bf16[512,128]{1,0:T(8,128)(2,1)} %c_ref.15, ...), custom_call_target="tpu_custom_call" | custom-call | flops 6442450944 | bytes 6291456 | tf_op jit(solution)/shard_map/node_inner/pallas_call | solution.py:306
  111.6 12.2 %collective-permute-done.2.main_ref = bf16[6,16,2176]{2,1,0:T(8,128)(2,1)S(1)} collective-permute-done((bf16[6,16,2176]{2,1,0:T(8,128)(2,1)S(1)}, bf16[6,16,2176]{2,1,0:T(8,128)(2,1)S(1)}, u32[]{:S(2)}, u32[]{:S(2)}) %collective-permute-start.2) | collective-permute-done | bytes 417824 | tf_op jit(solution)/shard_map/ppermute | solution.py:746
  123.8 3.4 %join_slots.2 = bf16[8,16,4096]{2,1,0:T(8,128)(2,1)} custom-call(s32[16]{0:T(128)S(1)} %copy-done, bf16[8,16,4224]{2,1,0:T(8,128)(2,1)S(1)} %all-to-all-done.recv_ref, bf16[6,16,2176]{2,1,0:T(8,128)(2,1)S(1)} %collective-permute-done.2.main_ref, bf16[6,16,2176]{2,1,0:T(8,128)(2,1)S(1)} %copy-done.3), custom_call_target="tpu_custom_call" | custom-call | flops 5242880 | bytes 2097152 | tf_op jit(solution)/shard_map/join_slots/pallas_call | solution.py:558
  127.2 6.1 %all-to-all-start.2 = ((bf16[8,16,4096]{2,1,0:T(8,128)(2,1)}), bf16[8,16,4096]{2,1,0:T(8,128)(2,1)S(1)}, u32[]{:S(2)}, u32[]{:S(2)}) async-start(bf16[8,16,4096]{2,1,0:T(8,128)(2,1)} %join_slots.2), calls=%async_computation.2 | async-start | bytes 2097152 | tf_op jit(solution)/shard_map/all_to_all | solution.py:736
  133.3 6.8 %node_inner.5 = (bf16[512,4096]{1,0:T(8,128)(2,1)}, bf16[512,4096]{1,0:T(8,128)(2,1)}, f32[512,128]{1,0:T(8,128)}, f32[512,128]{1,0:T(8,128)}) custom-call(bf16[512,4096]{1,0:T(8,128)(2,1)} %x_ref.15, bf16[512,4096]{1,0:T(8,128)(2,1)} %cot_ref.15, bf16[512,128]{1,0:T(8,128)(2,1)} %b_ref.15, ...), custom_call_target="tpu_custom_call", output_to_operand_aliasing={{0}: (7, {}), {1}: (8, {})} | custom-call | flops 6442450944 | bytes 6291456 | tf_op jit(solution)/shard_map/node_inner/pallas_call | solution.py:306
  140.2 6.9 %node_inner.6 = (bf16[512,4096]{1,0:T(8,128)(2,1)}, bf16[512,4096]{1,0:T(8,128)(2,1)}, f32[512,128]{1,0:T(8,128)}, f32[512,128]{1,0:T(8,128)}) custom-call(bf16[512,4096]{1,0:T(8,128)(2,1)} %x_ref.15, bf16[512,4096]{1,0:T(8,128)(2,1)} %cot_ref.15, bf16[512,128]{1,0:T(8,128)(2,1)} %b_ref.15, ...), custom_call_target="tpu_custom_call", output_to_operand_aliasing={{0}: (7, {}), {1}: (8, {})} | custom-call | flops 6442450944 | bytes 6291456 | tf_op jit(solution)/shard_map/node_inner/pallas_call | solution.py:306
  147.0 6.9 %node_inner.7 = (bf16[512,4096]{1,0:T(8,128)(2,1)}, bf16[512,4096]{1,0:T(8,128)(2,1)}, f32[512,128]{1,0:T(8,128)}, f32[512,128]{1,0:T(8,128)}) custom-call(bf16[512,4096]{1,0:T(8,128)(2,1)} %x_ref.15, bf16[512,4096]{1,0:T(8,128)(2,1)} %cot_ref.15, bf16[512,128]{1,0:T(8,128)(2,1)} %b_ref.15, ...), custom_call_target="tpu_custom_call", output_to_operand_aliasing={{0}: (7, {}), {1}: (8, {})} | custom-call | flops 6442450944 | bytes 6291456 | tf_op jit(solution)/shard_map/node_inner/pallas_call | solution.py:306
  153.9 9.6 %node_outer.2 = (bf16[512,4096]{1,0:T(8,128)(2,1)}, bf16[512,4096]{1,0:T(8,128)(2,1)}, f32[512,128]{1,0:T(8,128)}, f32[512,128]{1,0:T(8,128)}) custom-call(bf16[512,4096]{1,0:T(8,128)(2,1)} %x_ref.15, bf16[512,4096]{1,0:T(8,128)(2,1)} %cot_ref.15, bf16[512,128]{1,0:T(8,128)(2,1)} %b_ref.15, bf16[512,128]{1,0:T(8,128)(2,1)} %c_ref.15, ...), custom_call_target="tpu_custom_call" | custom-call | flops 1073741824 | bytes 12582912 | tf_op jit(solution)/shard_map/node_outer/pallas_call | solution.py:699
  163.6 1.0 copy-done.2
  164.6 9.3 %node_outer.3 = (bf16[512,4096]{1,0:T(8,128)(2,1)}, bf16[512,4096]{1,0:T(8,128)(2,1)}, f32[2,256,128]{2,1,0:T(8,128)}, bf16[2,256,128]{2,1,0:T(8,128)(2,1)}) custom-call(bf16[512,4096]{1,0:T(8,128)(2,1)} %x_ref.15, bf16[512,4096]{1,0:T(8,128)(2,1)} %cot_ref.15, bf16[512,128]{1,0:T(8,128)(2,1)} %b_ref.15, ...), custom_call_target="tpu_custom_call", output_to_operand_aliasing={{0}: (15, {}), {1}: (16, {})} | custom-call | flops 1073741824 | bytes 12582912 | tf_op jit(solution)/shard_map/node_outer/pallas_call | solution.py:699
  174.0 1.5 collective-permute-done.4
  175.5 1.0 convert_add_fusion
  176.5 0.7 slice_bitcast_fusion
  (14 shorter events, 0.2 us)
Async XLA Ops:
  7.3 21.3 %all-to-all-start.1 = ((bf16[8,16,4224]{2,1,0:T(8,128)(2,1)}), bf16[8,16,4224]{2,1,0:T(8,128)(2,1)S(1)}, u32[]{:S(2)}, u32[]{:S(2)}) async-start(bf16[8,16,4224]{2,1,0:T(8,128)(2,1)} %bitcast.14), calls=%async_computation.1 | async-start | bytes 2162688 | tf_op jit(solution)/shard_map/all_to_all | solution.py:736
  13.5 18.6 %copy-start = (s32[16]{0:T(128)S(1)}, s32[16]{0:T(128)}, u32[]{:S(2)}) copy-start(s32[16]{0:T(128)} %parents_ref.7) | copy-start | bytes 196
  28.6 26.7 %all-to-all-start = ((bf16[8,16,4224]{2,1,0:T(8,128)(2,1)}), bf16[8,16,4224]{2,1,0:T(8,128)(2,1)S(1)}, u32[]{:S(2)}, u32[]{:S(2)}) async-start(bf16[8,16,4224]{2,1,0:T(8,128)(2,1)} %bitcast.13), calls=%async_computation | async-start | bytes 2162688 | tf_op jit(solution)/shard_map/all_to_all | solution.py:736
  34.7 60.9 %collective-permute-start.3 = (bf16[6,16,2176]{2,1,0:T(8,128)(2,1)S(1)}, bf16[6,16,2176]{2,1,0:T(8,128)(2,1)S(1)}, u32[]{:S(2)}, u32[]{:S(2)}) collective-permute-start(bf16[6,16,2176]{2,1,0:T(8,128)(2,1)S(1)} %get-tuple-element.84), channel_id=1, source_target_pairs={{0,16},{2,18},{4,20},{6,22},{8,24},{10,26},{12,28},{14,30},{16,0},... | collective-permute-start | bytes 1253384 | tf_op jit(solution)/shard_map/ppermute | solution.py:746
  57.8 28.1 %collective-permute-start = (bf16[6,16,2176]{2,1,0:T(8,128)(2,1)}, bf16[6,16,2176]{2,1,0:T(8,128)(2,1)S(1)}, u32[]{:S(2)}, u32[]{:S(2)}) collective-permute-start(bf16[6,16,2176]{2,1,0:T(8,128)(2,1)} %get-tuple-element.8), channel_id=1, source_target_pairs={{0,16},{2,18},{4,20},{6,22},{8,24},{10,26},{12,28},{14,30},{16,0},... | collective-permute-start | bytes 1253384 | tf_op jit(solution)/shard_map/cond/branch_1_fun/ppermute | solution.py:746
  57.8 37.0 %collective-permute-start.1 = (bf16[6,16,2176]{2,1,0:T(8,128)(2,1)}, bf16[6,16,2176]{2,1,0:T(8,128)(2,1)S(1)}, u32[]{:S(2)}, u32[]{:S(2)}) collective-permute-start(bf16[6,16,2176]{2,1,0:T(8,128)(2,1)} %get-tuple-element.9), channel_id=1, source_target_pairs={{0,16},{2,18},{4,20},{6,22},{8,24},{10,26},{12,28},{14,30},{16,0},... | collective-permute-start | bytes 1253384 | tf_op jit(solution)/shard_map/cond/branch_1_fun/ppermute | solution.py:746
  99.4 27.8 %all-to-all-start.3 = ((bf16[8,16,4096]{2,1,0:T(8,128)(2,1)}), bf16[8,16,4096]{2,1,0:T(8,128)(2,1)S(1)}, u32[]{:S(2)}, u32[]{:S(2)}) async-start(bf16[8,16,4096]{2,1,0:T(8,128)(2,1)} %join_slots.3), calls=%async_computation.3 | async-start | bytes 2097152 | tf_op jit(solution)/shard_map/all_to_all | solution.py:736
  103.0 20.8 %collective-permute-start.2 = (bf16[6,16,2176]{2,1,0:T(8,128)(2,1)S(1)}, bf16[6,16,2176]{2,1,0:T(8,128)(2,1)S(1)}, u32[]{:S(2)}, u32[]{:S(2)}) collective-permute-start(bf16[6,16,2176]{2,1,0:T(8,128)(2,1)S(1)} %get-tuple-element.62), channel_id=1, source_target_pairs={{0,16},{2,18},{4,20},{6,22},{8,24},{10,26},{12,28},{14,30},{16,0},... | collective-permute-start | bytes 1253384 | tf_op jit(solution)/shard_map/ppermute | solution.py:746
  104.8 19.1 %copy-start.3 = (bf16[6,16,2176]{2,1,0:T(8,128)(2,1)S(1)}, bf16[6,16,2176]{2,1,0:T(8,128)(2,1)}, u32[]{:S(2)}) copy-start(bf16[6,16,2176]{2,1,0:T(8,128)(2,1)} %get-tuple-element.66.more_ref) | copy-start | bytes 1253380
  127.2 12.9 %copy-start.1 = (bf16[8,16,4096]{2,1,0:T(8,128)(2,1)}, bf16[8,16,4096]{2,1,0:T(8,128)(2,1)S(1)}, u32[]{:S(2)}) copy-start(bf16[8,16,4096]{2,1,0:T(8,128)(2,1)S(1)} %all-to-all-done.3) | copy-start | bytes 3145732
  127.2 36.4 %all-to-all-start.2 = ((bf16[8,16,4096]{2,1,0:T(8,128)(2,1)}), bf16[8,16,4096]{2,1,0:T(8,128)(2,1)S(1)}, u32[]{:S(2)}, u32[]{:S(2)}) async-start(bf16[8,16,4096]{2,1,0:T(8,128)(2,1)} %join_slots.2), calls=%async_computation.2 | async-start | bytes 2097152 | tf_op jit(solution)/shard_map/all_to_all | solution.py:736
  163.6 1.0 copy-start.2
  173.9 1.6 collective-permute-start.4

commit v7 on v6

--- a/solution.py
+++ b/solution.py
@@ -601,8 +601,9 @@
     if not final:
         out_ref, gx_ref, gc_ref, gb_ref = refs
     else:
-        out_ref, gx_ref, own_ref = refs[2:5]
-        pieces = refs[5:-2]
+        out_ref, gx_ref = refs[2:4]
+        owns = refs[4:6]
+        pieces = refs[6:-2]
         gc_ref, gb_ref = refs[-2:]
     block = x_ref.shape[1]
     index = pl.program_id(0)
@@ -637,12 +638,12 @@
         def _():
             size = len(pieces) + 1
             me = lax.axis_index("head")
-            rows = own_ref.shape[1]
+            rows = owns[0].shape[0]
             for shift in range(size):
                 at = pl.multiple_of(lax.rem(me + shift, size) * rows, rows)
                 for n, ref in enumerate((gb_ref, gc_ref)):
                     if shift == 0:
-                        own_ref[n] = ref[pl.ds(at, rows)]
+                        owns[n][...] = ref[pl.ds(at, rows)]
                     else:
                         pieces[shift - 1][n] = ref[pl.ds(at, rows)].astype(bf16)
 
@@ -688,8 +689,9 @@
         size = lax.axis_size("head")
         kept = (2, length // size, state)
         cube = lambda i: (0, 0, 0)
-        out_specs += [pl.BlockSpec(kept, cube)] * size
-        out_shape += [jax.ShapeDtypeStruct(kept, f32)]
+        out_specs += [pl.BlockSpec(kept[1:], whole)] * 2
+        out_specs += [pl.BlockSpec(kept, cube)] * (size - 1)
+        out_shape += [jax.ShapeDtypeStruct(kept[1:], f32)] * 2
         out_shape += [jax.ShapeDtypeStruct(kept, bf16)] * (size - 1)
         scratch = [pltpu.VMEM((length, state), f32)] * 2
     else:
@@ -713,12 +715,13 @@
     )(*operands)
 
 
-def scatter_sum(own, pieces):
+def scatter_sum(owns, pieces):
     size = lax.axis_size("head")
     for shift, piece in enumerate(pieces, 1):
         pairs = [(i, (i + shift) % size) for i in range(size)]
-        own = own + lax.ppermute(piece, "head", pairs).astype(f32)
-    return own
+        moved = lax.ppermute(piece, "head", pairs).astype(f32)
+        owns = [own + moved[n] for n, own in enumerate(owns)]
+    return owns
 
 
 def one_device(inputs, b_matrix, c_matrix, step_size, decay_rate, parents, cotangent):
@@ -747,7 +750,8 @@
 
     places = jnp.arange(nodes)
     child = jnp.logical_and(
-        parents[:, None] == places[None, :], (places[:, None] < half) != (places[None, :] < half)
+        parents[:, None] == places[None, :],
+        (places[:, None] < half) != (places[None, :] < half),
     )
     crossing = jnp.sum(jnp.any(child, axis=0).astype(jnp.int32))
     crowded = crossing > slot_counts(nodes)[0]
@@ -789,7 +793,7 @@
         prior = result[:2]
         if k == 0:
             found = [(result[3], result[2])]
-    grads = scatter_sum(result[2], result[3:])
+    grads = scatter_sum(result[2:4], result[4:])
     return prior[0], prior[1], grads[0], grads[1]
 
 

time: 178 us -> 178 us (level)
  transfers between devices with their start and end apart: 9 -> 9, of which waited for: 6 -> 6; matrix products, arithmetic and copies ran while one was open for 1% -> 1% of each run, Pallas kernels for 30% -> 29%
where the time goes in v7:
time: 178 us; the launch traced here: 177 us
  Pallas kernels  72.1 us (41%)
  waiting for transfers between devices  71.8 us (40%)
  starting transfers between devices  27 us (15%)
  local copies, waits for them, and re-layouts  2.52 us (1%)
  other arithmetic  2.45 us (1%)
    ppermute x4, waiting for transfers between devices, cross(): return lax.ppermute(v, 'node', across)  45.5 us
    pallas_call x4, Pallas kernels, node_inner(): pl.pallas_call(kernel, grid=(count,), in_specs=in_specs, out_specs=[pl.Bl...  27.5 us
    all_to_all x4, waiting for transfers between devices, swap(): lax.all_to_all(v.reshape(half, state // half, v.shape[-1]), 'node', split...  24.8 us
    all_to_all x4, starting transfers between devices, swap(): lax.all_to_all(v.reshape(half, state // half, v.shape[-1]), 'node', split...  19.5 us
    pallas_call x2, Pallas kernels, node_outer(): pl.pallas_call(kernel, grid=(count,), in_specs=in_specs, out_specs=out_sp...  19 us
    pallas_call x2, Pallas kernels, node_states(): pl.pallas_call(functools.partial(states_kernel, heads, head_width, chunk)...  13.3 us
    ppermute x4, starting transfers between devices, cross(): return lax.ppermute(v, 'node', across)  7.36 us
    pallas_call x2, Pallas kernels, join_slots(): pl.pallas_call(kernel, in_specs=in_specs, out_specs=pl.BlockSpec(memory_s...  7.19 us
  transfers between devices with their start and end apart: 9, of which 6 were waited for; matrix products, arithmetic and copies ran while one was open for 1% of the time, Pallas kernels for 29%

profile of v7, /device:TPU:0, one launch (start us, length us, event | category | flops | bytes accessed | tf_op | source)
XLA Modules:
  0.0 177.3 jit_solution(6236678298312226996)
XLA Ops:
  0.6 6.7 %node_states.3 = (bf16[128,4224]{1,0:T(8,128)(2,1)}, f32[512,128]{1,0:T(8,128)}, f32[32,512]{1,0:T(8,128)}, bf16[512,128]{1,0:T(8,128)(2,1)}, bf16[512,128]{1,0:...) custom-call(bf16[512,4096]{1,0:T(8,128)(2,1)} %x_ref.15, ...), custom_call_target="tpu_custom_call" | custom-call | flops 536870912 | bytes 5242880 | tf_op jit(solution)/shard_map/node_states/pallas_call | solution.py:138
  7.3 6.2 %all-to-all-start.1 = ((bf16[8,16,4224]{2,1,0:T(8,128)(2,1)}), bf16[8,16,4224]{2,1,0:T(8,128)(2,1)S(1)}, u32[]{:S(2)}, u32[]{:S(2)}) async-start(bf16[8,16,4224]{2,1,0:T(8,128)(2,1)} %bitcast.18), calls=%async_computation.1 | async-start | bytes 2162688 | tf_op jit(solution)/shard_map/all_to_all | solution.py:739
  13.5 6.7 %node_states.2 = (bf16[128,4224]{1,0:T(8,128)(2,1)}, f32[512,128]{1,0:T(8,128)}, f32[32,512]{1,0:T(8,128)}, bf16[512,128]{1,0:T(8,128)(2,1)}, bf16[512,128]{1,0:...) custom-call(bf16[512,4096]{1,0:T(8,128)(2,1)} %x_ref.15, ...), custom_call_target="tpu_custom_call" | custom-call | flops 536870912 | bytes 5242880 | tf_op jit(solution)/shard_map/node_states/pallas_call | solution.py:138
  20.2 8.4 %all-to-all-done.1.recv_ref = bf16[8,16,4224]{2,1,0:T(8,128)(2,1)S(1)} async-done(((bf16[8,16,4224]{2,1,0:T(8,128)(2,1)}), bf16[8,16,4224]{2,1,0:T(8,128)(2,1)S(1)}, u32[]{:S(2)}, u32[]{:S(2)}) %all-to-all-start.1) | async-done | bytes 1081376 | tf_op jit(solution)/shard_map/all_to_all | solution.py:739
  28.6 3.6 %all-to-all-start = ((bf16[8,16,4224]{2,1,0:T(8,128)(2,1)}), bf16[8,16,4224]{2,1,0:T(8,128)(2,1)S(1)}, u32[]{:S(2)}, u32[]{:S(2)}) async-start(bf16[8,16,4224]{2,1,0:T(8,128)(2,1)} %bitcast.17), calls=%async_computation | async-start | bytes 2162688 | tf_op jit(solution)/shard_map/all_to_all | solution.py:739
  32.1 2.6 %pack_slots.3 = (bf16[6,16,2176]{2,1,0:T(8,128)(2,1)S(1)}, bf16[6,16,2176]{2,1,0:T(8,128)(2,1)}) custom-call(s32[16]{0:T(128)S(1)} %copy-done, bf16[8,16,4224]{2,1,0:T(8,128)(2,1)S(1)} %all-to-all-done.1.recv_ref), custom_call_target="tpu_custom_call" | custom-call | flops 5242880 | bytes 2097152 | tf_op jit(solution)/shard_map/pack_slots/pallas_call | solution.py:448
  34.7 2.7 %collective-permute-start.3 = (bf16[6,16,2176]{2,1,0:T(8,128)(2,1)S(1)}, bf16[6,16,2176]{2,1,0:T(8,128)(2,1)S(1)}, u32[]{:S(2)}, u32[]{:S(2)}) collective-permute-start(bf16[6,16,2176]{2,1,0:T(8,128)(2,1)S(1)} %get-tuple-element.85), channel_id=1, source_target_pairs={{0,16},{2,18},{4,20},{6,22},{8,24},{10,26},{12,28},{14,30},{16,0},... | collective-permute-start | bytes 1253384 | tf_op jit(solution)/shard_map/ppermute | solution.py:749
  37.4 0.1 fusion.3
  37.5 0.6 convert_reduce_fusion
  38.8 16.5 %all-to-all-done.recv_ref = bf16[8,16,4224]{2,1,0:T(8,128)(2,1)S(1)} async-done(((bf16[8,16,4224]{2,1,0:T(8,128)(2,1)}), bf16[8,16,4224]{2,1,0:T(8,128)(2,1)S(1)}, u32[]{:S(2)}, u32[]{:S(2)}) %all-to-all-start) | async-done | bytes 1081376 | tf_op jit(solution)/shard_map/all_to_all | solution.py:739
  55.3 2.6 %pack_slots.2 = (bf16[6,16,2176]{2,1,0:T(8,128)(2,1)S(1)}, bf16[6,16,2176]{2,1,0:T(8,128)(2,1)}) custom-call(s32[16]{0:T(128)S(1)} %copy-done, bf16[8,16,4224]{2,1,0:T(8,128)(2,1)S(1)} %all-to-all-done.recv_ref), custom_call_target="tpu_custom_call" | custom-call | flops 5242880 | bytes 2097152 | tf_op jit(solution)/shard_map/pack_slots/pallas_call | solution.py:448
  57.8 37.7 %conditional.1 = ((bf16[6,16,2176]{2,1,0:T(8,128)(2,1)}, bf16[6,16,2176]{2,1,0:T(8,128)(2,1)})) conditional(s32[]{:T(128)} %convert_element_type.10, (bf16[6,16,2176]{2,1,0:T(8,128)(2,1)}, bf16[6,16,2176]{2,1,0:T(8,128)(2,1)}) %tuple.15, (bf16[6,16,2176]{2,1,0:T(8,128)(2,1)}, bf16[6,16,2176]{2,1,0:T(8,128)(2,1)}) %tuple.15), branch_computations={%region_2.0_spmd, %region_3.0_spmd} | conditional | bytes 5013608 | solution.py:778
  57.8 2.9 %collective-permute-start.1 = (bf16[6,16,2176]{2,1,0:T(8,128)(2,1)}, bf16[6,16,2176]{2,1,0:T(8,128)(2,1)S(1)}, u32[]{:S(2)}, u32[]{:S(2)}) collective-permute-start(bf16[6,16,2176]{2,1,0:T(8,128)(2,1)} %get-tuple-element.9), channel_id=1, source_target_pairs={{0,16},{2,18},{4,20},{6,22},{8,24},{10,26},{12,28},{14,30},{16,0},... | collective-permute-start | bytes 1253384 | tf_op jit(solution)/shard_map/cond/branch_1_fun/ppermute | solution.py:749
  60.8 25.2 %collective-permute-done = bf16[6,16,2176]{2,1,0:T(8,128)(2,1)S(1)} collective-permute-done((bf16[6,16,2176]{2,1,0:T(8,128)(2,1)}, bf16[6,16,2176]{2,1,0:T(8,128)(2,1)S(1)}, u32[]{:S(2)}, u32[]{:S(2)}) %collective-permute-start) | collective-permute-done | bytes 417824 | tf_op jit(solution)/shard_map/cond/branch_1_fun/ppermute | solution.py:749
  86.0 0.8 copy.21
  86.7 8.1 %collective-permute-done.1 = bf16[6,16,2176]{2,1,0:T(8,128)(2,1)S(1)} collective-permute-done((bf16[6,16,2176]{2,1,0:T(8,128)(2,1)}, bf16[6,16,2176]{2,1,0:T(8,128)(2,1)S(1)}, u32[]{:S(2)}, u32[]{:S(2)}) %collective-permute-start.1) | collective-permute-done | bytes 417824 | tf_op jit(solution)/shard_map/cond/branch_1_fun/ppermute | solution.py:749
  94.8 0.8 copy.22
  95.6 3.8 %join_slots.3 = bf16[8,16,4096]{2,1,0:T(8,128)(2,1)} custom-call(s32[16]{0:T(128)S(1)} %copy-done, bf16[8,16,4224]{2,1,0:T(8,128)(2,1)S(1)} %all-to-all-done.1.recv_ref, bf16[6,16,2176]{2,1,0:T(8,128)(2,1)S(1)} %collective-permute-done.3.main_ref, bf16[6,16,2176]{2,1,0:T(8,128)(2,1)} %get-tuple-element.86.more_ref), custom_call_target="tpu_custom_call" | custom-call | flops 5242880 | bytes 2097152 | tf_op jit(solution)/shard_map/join_slots/pallas_call | solution.py:558
  99.4 3.6 %all-to-all-start.3 = ((bf16[8,16,4096]{2,1,0:T(8,128)(2,1)}), bf16[8,16,4096]{2,1,0:T(8,128)(2,1)S(1)}, u32[]{:S(2)}, u32[]{:S(2)}) async-start(bf16[8,16,4096]{2,1,0:T(8,128)(2,1)} %join_slots.3), calls=%async_computation.3 | async-start | bytes 2097152 | tf_op jit(solution)/shard_map/all_to_all | solution.py:739
  103.0 1.7 collective-permute-start.2
  104.8 6.9 %node_inner.4 = (bf16[512,4096]{1,0:T(8,128)(2,1)}, bf16[512,4096]{1,0:T(8,128)(2,1)}, f32[512,128]{1,0:T(8,128)}, f32[512,128]{1,0:T(8,128)}) custom-call(bf16[512,4096]{1,0:T(8,128)(2,1)} %x_ref.15, bf16[512,4096]{1,0:T(8,128)(2,1)} %cot_ref.15, bf16[512,128]{1,0:T(8,128)(2,1)} %b_ref.15, bf16[512,128]{1,0:T(8,128)(2,1)} %c_ref.15, ...), custom_call_target="tpu_custom_call" | custom-call | flops 6442450944 | bytes 6291456 | tf_op jit(solution)/shard_map/node_inner/pallas_call | solution.py:306
  111.6 12.2 %collective-permute-done.2.main_ref = bf16[6,16,2176]{2,1,0:T(8,128)(2,1)S(1)} collective-permute-done((bf16[6,16,2176]{2,1,0:T(8,128)(2,1)S(1)}, bf16[6,16,2176]{2,1,0:T(8,128)(2,1)S(1)}, u32[]{:S(2)}, u32[]{:S(2)}) %collective-permute-start.2) | collective-permute-done | bytes 417824 | tf_op jit(solution)/shard_map/ppermute | solution.py:749
  123.8 3.4 %join_slots.2 = bf16[8,16,4096]{2,1,0:T(8,128)(2,1)} custom-call(s32[16]{0:T(128)S(1)} %copy-done, bf16[8,16,4224]{2,1,0:T(8,128)(2,1)S(1)} %all-to-all-done.recv_ref, bf16[6,16,2176]{2,1,0:T(8,128)(2,1)S(1)} %collective-permute-done.2.main_ref, bf16[6,16,2176]{2,1,0:T(8,128)(2,1)S(1)} %copy-done.3), custom_call_target="tpu_custom_call" | custom-call | flops 5242880 | bytes 2097152 | tf_op jit(solution)/shard_map/join_slots/pallas_call | solution.py:558
  127.2 6.1 %all-to-all-start.2 = ((bf16[8,16,4096]{2,1,0:T(8,128)(2,1)}), bf16[8,16,4096]{2,1,0:T(8,128)(2,1)S(1)}, u32[]{:S(2)}, u32[]{:S(2)}) async-start(bf16[8,16,4096]{2,1,0:T(8,128)(2,1)} %join_slots.2), calls=%async_computation.2 | async-start | bytes 2097152 | tf_op jit(solution)/shard_map/all_to_all | solution.py:739
  133.3 6.8 %node_inner.5 = (bf16[512,4096]{1,0:T(8,128)(2,1)}, bf16[512,4096]{1,0:T(8,128)(2,1)}, f32[512,128]{1,0:T(8,128)}, f32[512,128]{1,0:T(8,128)}) custom-call(bf16[512,4096]{1,0:T(8,128)(2,1)} %x_ref.15, bf16[512,4096]{1,0:T(8,128)(2,1)} %cot_ref.15, bf16[512,128]{1,0:T(8,128)(2,1)} %b_ref.15, ...), custom_call_target="tpu_custom_call", output_to_operand_aliasing={{0}: (7, {}), {1}: (8, {})} | custom-call | flops 6442450944 | bytes 6291456 | tf_op jit(solution)/shard_map/node_inner/pallas_call | solution.py:306
  140.2 6.9 %node_inner.6 = (bf16[512,4096]{1,0:T(8,128)(2,1)}, bf16[512,4096]{1,0:T(8,128)(2,1)}, f32[512,128]{1,0:T(8,128)}, f32[512,128]{1,0:T(8,128)}) custom-call(bf16[512,4096]{1,0:T(8,128)(2,1)} %x_ref.15, bf16[512,4096]{1,0:T(8,128)(2,1)} %cot_ref.15, bf16[512,128]{1,0:T(8,128)(2,1)} %b_ref.15, ...), custom_call_target="tpu_custom_call", output_to_operand_aliasing={{0}: (7, {}), {1}: (8, {})} | custom-call | flops 6442450944 | bytes 6291456 | tf_op jit(solution)/shard_map/node_inner/pallas_call | solution.py:306
  147.0 6.9 %node_inner.7 = (bf16[512,4096]{1,0:T(8,128)(2,1)}, bf16[512,4096]{1,0:T(8,128)(2,1)}, f32[512,128]{1,0:T(8,128)}, f32[512,128]{1,0:T(8,128)}) custom-call(bf16[512,4096]{1,0:T(8,128)(2,1)} %x_ref.15, bf16[512,4096]{1,0:T(8,128)(2,1)} %cot_ref.15, bf16[512,128]{1,0:T(8,128)(2,1)} %b_ref.15, ...), custom_call_target="tpu_custom_call", output_to_operand_aliasing={{0}: (7, {}), {1}: (8, {})} | custom-call | flops 6442450944 | bytes 6291456 | tf_op jit(solution)/shard_map/node_inner/pallas_call | solution.py:306
  153.9 9.6 %node_outer.2 = (bf16[512,4096]{1,0:T(8,128)(2,1)}, bf16[512,4096]{1,0:T(8,128)(2,1)}, f32[512,128]{1,0:T(8,128)}, f32[512,128]{1,0:T(8,128)}) custom-call(bf16[512,4096]{1,0:T(8,128)(2,1)} %x_ref.15, bf16[512,4096]{1,0:T(8,128)(2,1)} %cot_ref.15, bf16[512,128]{1,0:T(8,128)(2,1)} %b_ref.15, bf16[512,128]{1,0:T(8,128)(2,1)} %c_ref.15, ...), custom_call_target="tpu_custom_call" | custom-call | flops 1073741824 | bytes 12582912 | tf_op jit(solution)/shard_map/node_outer/pallas_call | solution.py:701
  163.6 1.0 copy-done.2
  164.6 9.3 %node_outer.3 = (bf16[512,4096]{1,0:T(8,128)(2,1)}, bf16[512,4096]{1,0:T(8,128)(2,1)}, f32[256,128]{1,0:T(8,128)}, f32[256,128]{1,0:T(8,128)}, bf16[2,256,128]{2,1,0:T(8,128)(2,1)}) custom-call(bf16[512,4096]{1,0:T(8,128)(2,1)} %x_ref.15, bf16[512,4096]{1,0:T(8,128)(2,1)} %cot_ref.15, ...), custom_call_target="tpu_custom_call", output_to_operand_aliasing={{0}: (15, {}), {1}: (16, {})} | custom-call | flops 1073741824 | bytes 12582912 | tf_op jit(solution)/shard_map/node_outer/pallas_call | solution.py:701
  174.0 1.5 collective-permute-done.4
  175.6 1.7 fusion
  (14 shorter events, 0.1 us)
Async XLA Ops:
  7.3 21.3 %all-to-all-start.1 = ((bf16[8,16,4224]{2,1,0:T(8,128)(2,1)}), bf16[8,16,4224]{2,1,0:T(8,128)(2,1)S(1)}, u32[]{:S(2)}, u32[]{:S(2)}) async-start(bf16[8,16,4224]{2,1,0:T(8,128)(2,1)} %bitcast.18), calls=%async_computation.1 | async-start | bytes 2162688 | tf_op jit(solution)/shard_map/all_to_all | solution.py:739
  13.5 18.6 %copy-start = (s32[16]{0:T(128)S(1)}, s32[16]{0:T(128)}, u32[]{:S(2)}) copy-start(s32[16]{0:T(128)} %parents_ref.7) | copy-start | bytes 196
  28.6 26.7 %all-to-all-start = ((bf16[8,16,4224]{2,1,0:T(8,128)(2,1)}), bf16[8,16,4224]{2,1,0:T(8,128)(2,1)S(1)}, u32[]{:S(2)}, u32[]{:S(2)}) async-start(bf16[8,16,4224]{2,1,0:T(8,128)(2,1)} %bitcast.17), calls=%async_computation | async-start | bytes 2162688 | tf_op jit(solution)/shard_map/all_to_all | solution.py:739
  34.7 60.9 %collective-permute-start.3 = (bf16[6,16,2176]{2,1,0:T(8,128)(2,1)S(1)}, bf16[6,16,2176]{2,1,0:T(8,128)(2,1)S(1)}, u32[]{:S(2)}, u32[]{:S(2)}) collective-permute-start(bf16[6,16,2176]{2,1,0:T(8,128)(2,1)S(1)} %get-tuple-element.85), channel_id=1, source_target_pairs={{0,16},{2,18},{4,20},{6,22},{8,24},{10,26},{12,28},{14,30},{16,0},... | collective-permute-start | bytes 1253384 | tf_op jit(solution)/shard_map/ppermute | solution.py:749
  57.8 28.1 %collective-permute-start = (bf16[6,16,2176]{2,1,0:T(8,128)(2,1)}, bf16[6,16,2176]{2,1,0:T(8,128)(2,1)S(1)}, u32[]{:S(2)}, u32[]{:S(2)}) collective-permute-start(bf16[6,16,2176]{2,1,0:T(8,128)(2,1)} %get-tuple-element.8), channel_id=1, source_target_pairs={{0,16},{2,18},{4,20},{6,22},{8,24},{10,26},{12,28},{14,30},{16,0},... | collective-permute-start | bytes 1253384 | tf_op jit(solution)/shard_map/cond/branch_1_fun/ppermute | solution.py:749
  57.8 37.0 %collective-permute-start.1 = (bf16[6,16,2176]{2,1,0:T(8,128)(2,1)}, bf16[6,16,2176]{2,1,0:T(8,128)(2,1)S(1)}, u32[]{:S(2)}, u32[]{:S(2)}) collective-permute-start(bf16[6,16,2176]{2,1,0:T(8,128)(2,1)} %get-tuple-element.9), channel_id=1, source_target_pairs={{0,16},{2,18},{4,20},{6,22},{8,24},{10,26},{12,28},{14,30},{16,0},... | collective-permute-start | bytes 1253384 | tf_op jit(solution)/shard_map/cond/branch_1_fun/ppermute | solution.py:749
  99.4 27.8 %all-to-all-start.3 = ((bf16[8,16,4096]{2,1,0:T(8,128)(2,1)}), bf16[8,16,4096]{2,1,0:T(8,128)(2,1)S(1)}, u32[]{:S(2)}, u32[]{:S(2)}) async-start(bf16[8,16,4096]{2,1,0:T(8,128)(2,1)} %join_slots.3), calls=%async_computation.3 | async-start | bytes 2097152 | tf_op jit(solution)/shard_map/all_to_all | solution.py:739
  103.0 20.8 %collective-permute-start.2 = (bf16[6,16,2176]{2,1,0:T(8,128)(2,1)S(1)}, bf16[6,16,2176]{2,1,0:T(8,128)(2,1)S(1)}, u32[]{:S(2)}, u32[]{:S(2)}) collective-permute-start(bf16[6,16,2176]{2,1,0:T(8,128)(2,1)S(1)} %get-tuple-element.63), channel_id=1, source_target_pairs={{0,16},{2,18},{4,20},{6,22},{8,24},{10,26},{12,28},{14,30},{16,0},... | collective-permute-start | bytes 1253384 | tf_op jit(solution)/shard_map/ppermute | solution.py:749
  104.8 19.1 %copy-start.3 = (bf16[6,16,2176]{2,1,0:T(8,128)(2,1)S(1)}, bf16[6,16,2176]{2,1,0:T(8,128)(2,1)}, u32[]{:S(2)}) copy-start(bf16[6,16,2176]{2,1,0:T(8,128)(2,1)} %get-tuple-element.67.more_ref) | copy-start | bytes 1253380
  127.2 12.9 %copy-start.1 = (bf16[8,16,4096]{2,1,0:T(8,128)(2,1)}, bf16[8,16,4096]{2,1,0:T(8,128)(2,1)S(1)}, u32[]{:S(2)}) copy-start(bf16[8,16,4096]{2,1,0:T(8,128)(2,1)S(1)} %all-to-all-done.3) | copy-start | bytes 3145732
  127.2 36.4 %all-to-all-start.2 = ((bf16[8,16,4096]{2,1,0:T(8,128)(2,1)}), bf16[8,16,4096]{2,1,0:T(8,128)(2,1)S(1)}, u32[]{:S(2)}, u32[]{:S(2)}) async-start(bf16[8,16,4096]{2,1,0:T(8,128)(2,1)} %join_slots.2), calls=%async_computation.2 | async-start | bytes 2097152 | tf_op jit(solution)/shard_map/all_to_all | solution.py:739
  163.6 1.0 copy-start.2
  173.9 1.6 collective-permute-start.4

commit v8 on v7

--- a/solution.py
+++ b/solution.py
@@ -56,77 +56,107 @@
     return steps[:1], steps[SUBLANES : SUBLANES + 1]
 
 
-def states_kernel(
-    heads,
-    head_width,
-    chunk,
-    x_ref,
-    cot_ref,
-    b_ref,
-    c_ref,
-    step_ref,
-    rate_ref,
-    send_ref,
-    low_ref,
-    src_ref,
-    grow_ref,
-    tail_ref,
-    gram_ref,
-    keep_ref,
-    step_out_ref,
-    bt_ref,
-    ct_ref,
-):
-    block = x_ref.shape[1]
+class Copies:
+    def __init__(self, sems):
+        self.sems = sems
+        self.made = []
+
+    def start(self, source, target):
+        copy = pltpu.make_async_copy(source, target, self.sems.at[len(self.made)])
+        copy.start()
+        self.made.append(copy)
+        return copy
+
+
+def wait_all(copies):
+    for copy in copies:
+        copy.wait()
+
+
+def states_kernel(heads, head_width, chunk, block, *refs):
+    x_hbm, cot_hbm, b_hbm, c_hbm, step_hbm, rate_hbm = refs[:6]
+    outs = refs[6:14]
+    x_ref, cot_ref, b_ref, c_ref, step_ref, rate_ref = refs[14:20]
+    send_ref, low_ref, src_ref, grow_ref, tail_ref, gram_ref, keep_ref, steps_ref = refs[20:28]
+    sems = refs[28]
     length = step_ref.shape[1]
     middle = length // 2
-    index = pl.program_id(0)
     width = heads * head_width
-
-    @pl.when(index == 0)
-    def _():
-        step = step_ref[...]
-        rates = jnp.broadcast_to(rate_ref[...], (LANES, rate_ref.shape[1])).T
-        terms = -step * rates[chunk * heads : (chunk + 1) * heads, :1]
-        row = lax.broadcasted_iota(jnp.int32, (length, length), 0)
-        col = lax.broadcasted_iota(jnp.int32, (length, length), 1)
-        upper = (row <= col).astype(bf16)
-        first = terms.astype(bf16)
-        rest = terms - first.astype(f32)
-        second, third = split_two(rest)
-        cumulative = mm(third, upper) + mm(second, upper) + mm(first, upper)
-        last = cumulative[:, length - 1 :]
-        mid = cumulative[:, middle - 1 : middle]
-        late = lax.broadcasted_iota(jnp.int32, cumulative.shape, 1) >= middle
-        low_ref[...] = pad_lanes(cumulative * LOG2E)
-        src_ref[...] = (cumulative - jnp.log(step)) * LOG2E
-        grow_ref[...] = pad_lanes(jnp.exp(cumulative - jnp.where(late, mid, 0.0))).astype(bf16)
-        tail = jnp.exp(jnp.where(late, last, mid) - cumulative) * step
-        tail_ref[...] = pad_lanes(tail).astype(bf16)
-        bt_ref[...] = b_ref[...].T
-        ct_ref[...] = c_ref[...].T
-        total = jnp.exp(jnp.broadcast_to(last, (heads, send_ref.shape[0])))
-        send_ref[:, 2 * width :] = pad_lanes(total).astype(bf16)
-        each = (heads, SUBLANES)
-        steps = [jnp.broadcast_to(mid, each), jnp.broadcast_to(last - mid, each)]
-        step_out_ref[...] = pad_lanes(jnp.exp(jnp.concatenate(steps, axis=1))).astype(bf16)
-        for rows in (slice(0, middle), slice(middle, length)):
-            gram_ref[rows] = mm(c_ref[rows], b_ref[rows], NT).astype(bf16)
-
-    spread = spread_matrix(LANES, block, head_width, index * block)
-    tailed = mm(tail_ref[...], spread).astype(bf16) * x_ref[...]
-    emitted = mm(grow_ref[...], spread).astype(bf16) * cot_ref[...]
-    early_step, late_step = half_steps(step_out_ref, spread)
-    early_state = mm(bt_ref[:, :middle], tailed[:middle])
-    late_state = mm(bt_ref[:, middle:], tailed[middle:])
-    early_seed = mm(ct_ref[:, :middle], emitted[:middle])
-    late_seed = mm(ct_ref[:, middle:], emitted[middle:])
-    here = pl.ds(pl.multiple_of(index * block, block), block)
-    there = pl.ds(pl.multiple_of(index * block + width, LANES), block)
-    send_ref[:, here] = (late_step * early_state + late_state).astype(bf16)
-    send_ref[:, there] = (early_seed + early_step * late_seed).astype(bf16)
-    keep_ref[:, here] = early_state.astype(bf16)
-    keep_ref[:, there] = late_seed.astype(bf16)
+    count = width // block
+    copies = Copies(sems)
+    first_in = [
+        copies.start(step_hbm.at[pl.ds(chunk * heads, heads)], step_ref),
+        copies.start(rate_hbm, rate_ref),
+    ]
+    later_in = [copies.start(b_hbm, b_ref), copies.start(c_hbm, c_ref)]
+    loads = []
+    for i in range(count):
+        lanes = pl.ds(i * block, block)
+        there = pl.ds(chunk * width + i * block, block)
+        loads.append(
+            [
+                copies.start(x_hbm.at[:, there], x_ref.at[:, lanes]),
+                copies.start(cot_hbm.at[:, there], cot_ref.at[:, lanes]),
+            ]
+        )
+    wait_all(first_in)
+    step = step_ref[...]
+    rates = jnp.broadcast_to(rate_ref[...], (LANES, rate_ref.shape[1])).T
+    terms = -step * rates[chunk * heads : (chunk + 1) * heads, :1]
+    row = lax.broadcasted_iota(jnp.int32, (length, length), 0)
+    col = lax.broadcasted_iota(jnp.int32, (length, length), 1)
+    upper = (row <= col).astype(bf16)
+    first = terms.astype(bf16)
+    rest = terms - first.astype(f32)
+    second, third = split_two(rest)
+    cumulative = mm(third, upper) + mm(second, upper) + mm(first, upper)
+    last = cumulative[:, length - 1 :]
+    mid = cumulative[:, middle - 1 : middle]
+    late = lax.broadcasted_iota(jnp.int32, cumulative.shape, 1) >= middle
+    low_ref[...] = pad_lanes(cumulative * LOG2E)
+    src_ref[...] = (cumulative - jnp.log(step)) * LOG2E
+    grow_ref[...] = pad_lanes(jnp.exp(cumulative - jnp.where(late, mid, 0.0))).astype(bf16)
+    tail = jnp.exp(jnp.where(late, last, mid) - cumulative) * step
+    tail_ref[...] = pad_lanes(tail).astype(bf16)
+    total = jnp.exp(jnp.broadcast_to(last, (heads, send_ref.shape[0])))
+    send_ref[:, 2 * width :] = pad_lanes(total).astype(bf16)
+    each = (heads, SUBLANES)
+    steps = [jnp.broadcast_to(mid, each), jnp.broadcast_to(last - mid, each)]
+    steps_ref[...] = pad_lanes(jnp.exp(jnp.concatenate(steps, axis=1))).astype(bf16)
+    wait_all(later_in)
+    b_turned = b_ref[...].T
+    c_turned = c_ref[...].T
+    for rows in (slice(0, middle), slice(middle, length)):
+        gram_ref[rows] = mm(c_ref[rows], b_ref[rows], NT).astype(bf16)
+    small = (1, 2, 3, 4, 5, 7)
+    made = (send_ref, low_ref, src_ref, grow_ref, tail_ref, gram_ref, keep_ref, steps_ref)
+    stores = []
+    ready = [(made[n], outs[n]) for n in small]
+    ready.append((send_ref.at[:, pl.ds(2 * width, LANES)], outs[0].at[:, pl.ds(2 * width, LANES)]))
+    for i in range(count):
+        here = pl.ds(i * block, block)
+        there = pl.ds(i * block + width, block)
+        wait_all(loads[i])
+        spread = spread_matrix(LANES, block, head_width, i * block)
+        tailed = mm(tail_ref[...], spread).astype(bf16) * x_ref[:, here]
+        emitted = mm(grow_ref[...], spread).astype(bf16) * cot_ref[:, here]
+        early_step, late_step = half_steps(steps_ref, spread)
+        early_state = mm(b_turned[:, :middle], tailed[:middle])
+        late_state = mm(b_turned[:, middle:], tailed[middle:])
+        early_seed = mm(c_turned[:, :middle], emitted[:middle])
+        late_seed = mm(c_turned[:, middle:], emitted[middle:])
+        send_ref[:, here] = (late_step * early_state + late_state).astype(bf16)
+        send_ref[:, there] = (early_seed + early_step * late_seed).astype(bf16)
+        keep_ref[:, here] = early_state.astype(bf16)
+        keep_ref[:, there] = late_seed.astype(bf16)
+        stores += [copies.start(*pair) for pair in ready]
+        ready = [
+            (ref.at[:, lanes], out.at[:, lanes])
+            for ref, out in ((send_ref, outs[0]), (keep_ref, outs[6]))
+            for lanes in (here, there)
+        ]
+    stores += [copies.start(*pair) for pair in ready]
+    wait_all(stores)
 
 
 def node_states(x, cot, b, c, step, rate, chunk, heads, head_width):
@@ -134,43 +164,32 @@
     width = heads * head_width
     block = min(width, 4 * LANES)
     count = width // block
-    whole = lambda i: (0, 0)
+    out_shape = [
+        jax.ShapeDtypeStruct((state, 2 * width + LANES), bf16),
+        jax.ShapeDtypeStruct((length, LANES), f32),
+        jax.ShapeDtypeStruct((heads, length), f32),
+        jax.ShapeDtypeStruct((length, LANES), bf16),
+        jax.ShapeDtypeStruct((length, LANES), bf16),
+        jax.ShapeDtypeStruct((length, length // 2), bf16),
+        jax.ShapeDtypeStruct((state, 2 * width), bf16),
+        jax.ShapeDtypeStruct((2 * SUBLANES, LANES), bf16),
+    ]
+    held = [(length, width)] * 2 + [b.shape] * 2
+    scratch = [pltpu.VMEM(shape, bf16) for shape in held]
+    scratch += [pltpu.VMEM((heads, length), f32), pltpu.VMEM(rate.shape, f32)]
+    scratch += [pltpu.VMEM(v.shape, v.dtype) for v in out_shape]
+    scratch.append(pltpu.SemaphoreType.DMA((11 + 6 * count,)))
+    anywhere = pl.BlockSpec(memory_space=pl.ANY)
     return pl.pallas_call(
-        functools.partial(states_kernel, heads, head_width, chunk),
-        grid=(count,),
-        in_specs=[
-            pl.BlockSpec((length, block), lambda i: (0, chunk * count + i)),
-            pl.BlockSpec((length, block), lambda i: (0, chunk * count + i)),
-            pl.BlockSpec((length, state), whole),
-            pl.BlockSpec((length, state), whole),
-            pl.BlockSpec((heads, length), lambda i: (chunk, 0)),
-            pl.BlockSpec(rate.shape, whole),
-        ],
-        out_specs=[
-            pl.BlockSpec((state, 2 * width + LANES), whole),
-            pl.BlockSpec((length, LANES), whole),
-            pl.BlockSpec((heads, length), whole),
-            pl.BlockSpec((length, LANES), whole),
-            pl.BlockSpec((length, LANES), whole),
-            pl.BlockSpec((length, length // 2), whole),
-            pl.BlockSpec((state, 2 * width), whole),
-            pl.BlockSpec((2 * SUBLANES, LANES), whole),
-        ],
-        out_shape=[
-            jax.ShapeDtypeStruct((state, 2 * width + LANES), bf16),
-            jax.ShapeDtypeStruct((length, LANES), f32),
-            jax.ShapeDtypeStruct((heads, length), f32),
-            jax.ShapeDtypeStruct((length, LANES), bf16),
-            jax.ShapeDtypeStruct((length, LANES), bf16),
-            jax.ShapeDtypeStruct((length, length // 2), bf16),
-            jax.ShapeDtypeStruct((state, 2 * width), bf16),
-            jax.ShapeDtypeStruct((2 * SUBLANES, LANES), bf16),
-        ],
-        scratch_shapes=[pltpu.VMEM((state, length), bf16), pltpu.VMEM((state, length), bf16)],
+        functools.partial(states_kernel, heads, head_width, chunk, block),
+        in_specs=[anywhere] * 6,
+        out_specs=[anywhere] * len(out_shape),
+        out_shape=out_shape,
+        scratch_shapes=scratch,
         name="node_states",
         cost_estimate=pl.CostEstimate(
             flops=4 * length * state * width,
-            bytes_accessed=4 * length * width + 4 * state * width,
+            bytes_accessed=4 * length * width + 8 * state * width,
             transcendentals=0,
         ),
     )(x, cot, b, c, step, rate)
@@ -577,75 +596,91 @@
     )(*operands)
 
 
-def outer_kernel(
-    head_width,
-    extras,
-    final,
-    x_ref,
-    cot_ref,
-    b_ref,
-    c_ref,
-    grow_ref,
-    tail_ref,
-    start_ref,
-    back_ref,
-    early_ref,
-    late_ref,
-    step_ref,
-    inner_ref,
-    grad_ref,
-    *refs,
-):
-    added = refs[: 2 * extras]
-    refs = refs[2 * extras :]
-    if not final:
-        out_ref, gx_ref, gc_ref, gb_ref = refs
+def outer_kernel(heads, head_width, chunk, block, extras, final, *refs):
+    given = 13 + 2 * extras
+    sources = refs[:given]
+    refs = refs[given:]
+    if final:
+        outs, owns, pieces = refs[2:4], refs[4:6], refs[6 : -(given + 5)]
+        gc_ref, gb_ref = refs[-2:]
+        refs = refs[-(given + 5) : -2]
     else:
-        out_ref, gx_ref = refs[2:4]
-        owns = refs[4:6]
-        pieces = refs[6:-2]
-        gc_ref, gb_ref = refs[-2:]
-    block = x_ref.shape[1]
-    index = pl.program_id(0)
-
-    @pl.when(index == 0)
-    def _():
-        gc_ref[...] = sum(ref[...] for ref in added[:extras])
-        gb_ref[...] = sum(ref[...] for ref in added[extras:])
-
-    spread = spread_matrix(LANES, block, head_width, index * block)
-    grow_wide = mm(grow_ref[...], spread)
-    tail_wide = mm(tail_ref[...], spread)
-    early_step, late_step = half_steps(step_ref, spread)
-    start = start_ref[...]
-    back = back_ref[...]
-    starts = (start, (early_step * start.astype(f32) + early_ref[...].astype(f32)).astype(bf16))
-    backs = ((late_step * back.astype(f32) + late_ref[...].astype(f32)).astype(bf16), back)
+        outs, (gc_ref, gb_ref) = refs[:2], refs[2:4]
+        refs = refs[4:]
+    held, results, sems = refs[:given], refs[given : given + 2], refs[-1]
+    b_ref, c_ref, grow_ref, tail_ref, step_ref = held[:5]
+    added = held[5 : 5 + 2 * extras]
+    x_ref, cot_ref, inner_ref, grad_ref, start_ref, back_ref, early_ref, late_ref = held[-8:]
+    width = heads * head_width
+    count = width // block
     middle = x_ref.shape[0] // 2
-    for n, part in enumerate((slice(0, middle), slice(middle, 2 * middle))):
-        grow = grow_wide[part]
-        tail = tail_wide[part]
-        carried = grow * mm(c_ref[part], starts[n])
-        out_ref[part] = (inner_ref[part].astype(f32) + carried).astype(bf16)
-        carried = tail * mm(b_ref[part], backs[n])
-        gx_ref[part] = (grad_ref[part].astype(f32) + carried).astype(bf16)
-        gc_ref[part] += mm(grow.astype(bf16) * cot_ref[part], starts[n], NT)
-        gb_ref[part] += mm(tail.astype(bf16) * x_ref[part], backs[n], NT)
-
+    copies = Copies(sems)
+    small = [copies.start(sources[n], held[n]) for n in range(5)]
+    loads = []
+    for i in range(count):
+        lanes = pl.ds(i * block, block)
+        over = pl.ds(width + i * block, block)
+        column = pl.ds(chunk * width + i * block, block)
+        spots = (column,) * 4 + (lanes, over) * 2
+        loads.append(
+            [
+                copies.start(source.at[:, spot], ref.at[:, lanes])
+                for source, spot, ref in zip(sources[-8:], spots, held[-8:])
+            ]
+        )
+    sums = [copies.start(sources[5 + n], ref) for n, ref in enumerate(added)]
+    wait_all(small)
+    stores = []
+    ready = []
+    for i in range(count):
+        here = pl.ds(i * block, block)
+        column = pl.ds(chunk * width + i * block, block)
+        wait_all(loads[i])
+        spread = spread_matrix(LANES, block, head_width, i * block)
+        grow_wide = mm(grow_ref[...], spread)
+        tail_wide = mm(tail_ref[...], spread)
+        early_step, late_step = half_steps(step_ref, spread)
+        start = start_ref[:, here]
+        back = back_ref[:, here]
+        after = (early_step * start.astype(f32) + early_ref[:, here].astype(f32)).astype(bf16)
+        before = (late_step * back.astype(f32) + late_ref[:, here].astype(f32)).astype(bf16)
+        for n, part in enumerate((slice(0, middle), slice(middle, 2 * middle))):
+            grow = grow_wide[part]
+            tail = tail_wide[part]
+            begin = (start, after)[n]
+            end = (before, back)[n]
+            carried = grow * mm(c_ref[part], begin)
+            results[0][part, here] = (inner_ref[part, here].astype(f32) + carried).astype(bf16)
+            carried = tail * mm(b_ref[part], end)
+            results[1][part, here] = (grad_ref[part, here].astype(f32) + carried).astype(bf16)
+            gc = mm(grow.astype(bf16) * cot_ref[part, here], begin, NT)
+            gb = mm(tail.astype(bf16) * x_ref[part, here], end, NT)
+            if i == 0:
+                gc_ref[part] = gc
+                gb_ref[part] = gb
+            else:
+                gc_ref[part] += gc
+                gb_ref[part] += gb
+        stores += [copies.start(*pair) for pair in ready]
+        ready = [
+            (result.at[:, here], out.at[:, column]) for result, out in zip(results, outs)
+        ]
+    wait_all(sums)
+    gc_ref[...] += sum(ref[...] for ref in added[:extras])
+    gb_ref[...] += sum(ref[...] for ref in added[extras:])
+    stores += [copies.start(*pair) for pair in ready]
     if final:
-
-        @pl.when(index == pl.num_programs(0) - 1)
-        def _():
-            size = len(pieces) + 1
-            me = lax.axis_index("head")
-            rows = owns[0].shape[0]
-            for shift in range(size):
-                at = pl.multiple_of(lax.rem(me + shift, size) * rows, rows)
-                for n, ref in enumerate((gb_ref, gc_ref)):
-                    if shift == 0:
-                        owns[n][...] = ref[pl.ds(at, rows)]
-                    else:
-                        pieces[shift - 1][n] = ref[pl.ds(at, rows)].astype(bf16)
+        size = len(pieces) + 1
+        me = lax.axis_index("head")
+        rows = owns[0].shape[0]
+        for shift in range(size):
+            at = pl.multiple_of(lax.rem(me + shift, size) * rows, rows)
+            for n, ref in enumerate((gb_ref, gc_ref)):
+                if shift == 0:
+                    owns[n][...] = ref[pl.ds(at, rows)]
+                else:
+                    pieces[shift - 1][n] = ref[pl.ds(at, rows)].astype(bf16)
+    wait_all(stores)
 
 
 def node_outer(
@@ -655,53 +690,34 @@
     width = heads * head_width
     block = min(width, 4 * LANES)
     count = width // block
-    whole = lambda i: (0, 0)
-    spot = lambda i: (0, i)
-    place = lambda i: (0, chunk * count + i)
     final = prior is not None
-    operands = [x, cot, b, c, grow, tail, states, states, keep, keep, steps, inner, grad]
-    in_specs = [
-        pl.BlockSpec((length, block), place),
-        pl.BlockSpec((length, block), place),
-        pl.BlockSpec((length, state), whole),
-        pl.BlockSpec((length, state), whole),
-        pl.BlockSpec((length, LANES), whole),
-        pl.BlockSpec((length, LANES), whole),
-        pl.BlockSpec((state, block), spot),
-        pl.BlockSpec((state, block), lambda i: (0, count + i)),
-        pl.BlockSpec((state, block), spot),
-        pl.BlockSpec((state, block), lambda i: (0, count + i)),
-        pl.BlockSpec((2 * SUBLANES, LANES), whole),
-        pl.BlockSpec((length, block), place),
-        pl.BlockSpec((length, block), place),
-    ]
-    operands += [v[1] for v in found] + [v[0] for v in found]
-    in_specs += [pl.BlockSpec((length, state), whole)] * (2 * len(found))
-    out_specs = [pl.BlockSpec((length, block), place)] * 2
+    small = [b, c, grow, tail, steps] + [v[1] for v in found] + [v[0] for v in found]
+    operands = small + [x, cot, inner, grad, states, states, keep, keep]
+    given = len(operands)
+    anywhere = pl.BlockSpec(memory_space=pl.ANY)
+    local = pl.BlockSpec(memory_space=pltpu.VMEM)
+    out_specs = [anywhere] * 2
     out_shape = [jax.ShapeDtypeStruct(x.shape, bf16)] * 2
-    grads = jax.ShapeDtypeStruct((length, state), f32)
-    scratch = []
+    scratch = [pltpu.VMEM(v.shape, v.dtype) for v in small]
+    scratch += [pltpu.VMEM((length, width), bf16)] * 4 + [pltpu.VMEM((state, width), bf16)] * 4
+    scratch += [pltpu.VMEM((length, width), bf16)] * 2
+    scratch.append(pltpu.SemaphoreType.DMA((len(small) + 10 * count,)))
     aliases = {}
     if final:
-        aliases = {len(operands): 0, len(operands) + 1: 1}
+        aliases = {given: 0, given + 1: 1}
         operands += list(prior)
-        in_specs += [pl.BlockSpec(memory_space=pl.ANY)] * 2
         size = lax.axis_size("head")
         kept = (2, length // size, state)
-        cube = lambda i: (0, 0, 0)
-        out_specs += [pl.BlockSpec(kept[1:], whole)] * 2
-        out_specs += [pl.BlockSpec(kept, cube)] * (size - 1)
+        out_specs += [local] * (size + 1)
         out_shape += [jax.ShapeDtypeStruct(kept[1:], f32)] * 2
         out_shape += [jax.ShapeDtypeStruct(kept, bf16)] * (size - 1)
-        scratch = [pltpu.VMEM((length, state), f32)] * 2
+        scratch += [pltpu.VMEM((length, state), f32)] * 2
     else:
-        out_specs += [pl.BlockSpec((length, state), whole)] * 2
-        out_shape += [grads] * 2
-    kernel = functools.partial(outer_kernel, head_width, len(found), final)
+        out_specs += [local] * 2
+        out_shape += [jax.ShapeDtypeStruct((length, state), f32)] * 2
     return pl.pallas_call(
-        kernel,
-        grid=(count,),
-        in_specs=in_specs,
+        functools.partial(outer_kernel, heads, head_width, chunk, block, len(found), final),
+        in_specs=[anywhere] * len(operands),
         out_specs=out_specs,
         out_shape=out_shape,
         scratch_shapes=scratch,
@@ -709,7 +725,7 @@
         name="node_outer",
         cost_estimate=pl.CostEstimate(
             flops=8 * length * state * width,
-            bytes_accessed=12 * length * width,
+            bytes_accessed=14 * length * width,
             transcendentals=0,
         ),
     )(*operands)
@@ -754,7 +770,9 @@
         (places[:, None] < half) != (places[None, :] < half),
     )
     crossing = jnp.sum(jnp.any(child, axis=0).astype(jnp.int32))
-    crowded = crossing > slot_counts(nodes)[0]
+    main_count, more_count = slot_counts(nodes)
+    few = more_count // 3
+    crowded = (crossing > main_count).astype(jnp.int32) + (crossing > main_count + few)
 
     shared = (inputs, cotangent, b_matrix, c_matrix)
     sizes = (heads, head_width)
@@ -775,10 +793,13 @@
     for k in range(CHUNKS):
         main, more = pack_slots(parents, received[k], nodes, *sizes)
         packed.append((main, more, cross(main)))
-    others = lax.cond(
+    others = lax.switch(
         crowded,
-        lambda vs: tuple(cross(v) for v in vs),
-        lambda vs: vs,
+        (
+            lambda vs: vs,
+            lambda vs: tuple(jnp.concatenate([cross(v[:few]), v[few:]]) for v in vs),
+            lambda vs: tuple(cross(v) for v in vs),
+        ),
         tuple(p[1] for p in packed),
     )
     states = []

time: 178 us -> 153 us (0.86)
  waiting for transfers between devices: 71.8 us -> 44.7 us
  Pallas kernels: 72.1 us -> 69.1 us
  local copies, waits for them, and re-layouts: 2.52 us -> 4.79 us
    ppermute x4, waiting for transfers between devices: 45.5 us -> 18.1 us  [cross(): return lax.ppermute(v, 'node', across)]
    slice x0 -> x4, local copies, waits for them, and re-layouts: none -> 3.79 us  [the longest x2 1.95 us: one_device(): v[few:]]
    pallas_call x4, Pallas kernels: 32.3 us -> 29.2 us  [the longest x2 18 us: node_outer(): pl.pallas_call(functools.partial(outer_kernel, heads, head_width, chunk,...]
  transfers between devices with their start and end apart: 9 -> 9, of which waited for: 6 -> 6; matrix products, arithmetic and copies ran while one was open for 1% -> 4% of each run, Pallas kernels for 29% -> 33%
where the time goes in v8:
time: 153 us; the launch traced here: 152 us
  Pallas kernels  69.1 us (45%)
  waiting for transfers between devices  44.7 us (29%)
  starting transfers between devices  27.4 us (18%)
  local copies, waits for them, and re-layouts  4.79 us (3%)
  other arithmetic  4.15 us (3%)
  between operations  2.13 us (1%)
    pallas_call x4, Pallas kernels, node_inner(): pl.pallas_call(kernel, grid=(count,), in_specs=in_specs, out_specs=[pl.Bl...  27.5 us
    all_to_all x4, waiting for transfers between devices, swap(): lax.all_to_all(v.reshape(half, state // half, v.shape[-1]), 'node', split...  25.1 us
    all_to_all x4, starting transfers between devices, swap(): lax.all_to_all(v.reshape(half, state // half, v.shape[-1]), 'node', split...  19.8 us
    ppermute x4, waiting for transfers between devices, cross(): return lax.ppermute(v, 'node', across)  18.1 us
    pallas_call x2, Pallas kernels, node_outer(): pl.pallas_call(functools.partial(outer_kernel, heads, head_width, chunk,...  18 us
    pallas_call x2, Pallas kernels, node_states(): pl.pallas_call(functools.partial(states_kernel, heads, head_width, chunk,...  11.3 us
    ppermute x4, starting transfers between devices, cross(): return lax.ppermute(v, 'node', across)  7.51 us
    pallas_call x2, Pallas kernels, join_slots(): pl.pallas_call(kernel, in_specs=in_specs, out_specs=pl.BlockSpec(memory_s...  7.2 us
  transfers between devices with their start and end apart: 9, of which 6 were waited for; matrix products, arithmetic and copies ran while one was open for 4% of the time, Pallas kernels for 33%

profile of v8, /device:TPU:0, one launch (start us, length us, event | category | flops | bytes accessed | tf_op | source)
XLA Modules:
  0.0 152.2 jit_solution(12934872358042947475)
XLA Ops:
  0.6 5.6 %node_states.3 = (bf16[128,4224]{1,0:T(8,128)(2,1)}, f32[512,128]{1,0:T(8,128)}, f32[32,512]{1,0:T(8,128)}, bf16[512,128]{1,0:T(8,128)(2,1)}, bf16[512,128]{1,0:...) custom-call(bf16[512,4096]{1,0:T(8,128)(2,1)} %refs_7_.1, ...), custom_call_target="tpu_custom_call" | custom-call | flops 536870912 | bytes 6291456 | tf_op jit(solution)/shard_map/node_states/pallas_call | solution.py:183
  6.3 6.2 %all-to-all-start = ((bf16[8,16,4224]{2,1,0:T(8,128)(2,1)}), bf16[8,16,4224]{2,1,0:T(8,128)(2,1)S(1)}, u32[]{:S(2)}, u32[]{:S(2)}) async-start(bf16[8,16,4224]{2,1,0:T(8,128)(2,1)} %bitcast.18), calls=%async_computation | async-start | bytes 2162688 | tf_op jit(solution)/shard_map/all_to_all | solution.py:755
  12.5 5.6 %node_states.2 = (bf16[128,4224]{1,0:T(8,128)(2,1)}, f32[512,128]{1,0:T(8,128)}, f32[32,512]{1,0:T(8,128)}, bf16[512,128]{1,0:T(8,128)(2,1)}, bf16[512,128]{1,0:...) custom-call(bf16[512,4096]{1,0:T(8,128)(2,1)} %refs_7_.1, ...), custom_call_target="tpu_custom_call" | custom-call | flops 536870912 | bytes 6291456 | tf_op jit(solution)/shard_map/node_states/pallas_call | solution.py:183
  18.1 9.4 %all-to-all-done.recv_ref = bf16[8,16,4224]{2,1,0:T(8,128)(2,1)S(1)} async-done(((bf16[8,16,4224]{2,1,0:T(8,128)(2,1)}), bf16[8,16,4224]{2,1,0:T(8,128)(2,1)S(1)}, u32[]{:S(2)}, u32[]{:S(2)}) %all-to-all-start) | async-done | bytes 1081376 | tf_op jit(solution)/shard_map/all_to_all | solution.py:755
  27.5 3.6 %all-to-all-start.1 = ((bf16[8,16,4224]{2,1,0:T(8,128)(2,1)}), bf16[8,16,4224]{2,1,0:T(8,128)(2,1)S(1)}, u32[]{:S(2)}, u32[]{:S(2)}) async-start(bf16[8,16,4224]{2,1,0:T(8,128)(2,1)} %bitcast.17), calls=%async_computation.1 | async-start | bytes 2162688 | tf_op jit(solution)/shard_map/all_to_all | solution.py:755
  31.1 2.6 %pack_slots.2 = (bf16[6,16,2176]{2,1,0:T(8,128)(2,1)S(1)}, bf16[6,16,2176]{2,1,0:T(8,128)(2,1)}) custom-call(s32[16]{0:T(128)S(1)} %copy-done, bf16[8,16,4224]{2,1,0:T(8,128)(2,1)S(1)} %all-to-all-done.recv_ref), custom_call_target="tpu_custom_call" | custom-call | flops 5242880 | bytes 2097152 | tf_op jit(solution)/shard_map/pack_slots/pallas_call | solution.py:467
  33.7 2.7 %collective-permute-start.4 = (bf16[6,16,2176]{2,1,0:T(8,128)(2,1)S(1)}, bf16[6,16,2176]{2,1,0:T(8,128)(2,1)S(1)}, u32[]{:S(2)}, u32[]{:S(2)}) collective-permute-start(bf16[6,16,2176]{2,1,0:T(8,128)(2,1)S(1)} %get-tuple-element.94), channel_id=1, source_target_pairs={{0,16},{2,18},{4,20},{6,22},{8,24},{10,26},{12,28},{14,30},{16,0},... | collective-permute-start | bytes 1253384 | tf_op jit(solution)/shard_map/ppermute | solution.py:765
  38.6 15.6 %all-to-all-done.1.recv_ref = bf16[8,16,4224]{2,1,0:T(8,128)(2,1)S(1)} async-done(((bf16[8,16,4224]{2,1,0:T(8,128)(2,1)}), bf16[8,16,4224]{2,1,0:T(8,128)(2,1)S(1)}, u32[]{:S(2)}, u32[]{:S(2)}) %all-to-all-start.1) | async-done | bytes 1081376 | tf_op jit(solution)/shard_map/all_to_all | solution.py:755
  54.2 2.6 %pack_slots.3 = (bf16[6,16,2176]{2,1,0:T(8,128)(2,1)S(1)}, bf16[6,16,2176]{2,1,0:T(8,128)(2,1)}) custom-call(s32[16]{0:T(128)S(1)} %copy-done, bf16[8,16,4224]{2,1,0:T(8,128)(2,1)S(1)} %all-to-all-done.1.recv_ref), custom_call_target="tpu_custom_call" | custom-call | flops 5242880 | bytes 2097152 | tf_op jit(solution)/shard_map/pack_slots/pallas_call | solution.py:467
  56.8 14.7 %conditional.1 = ((bf16[6,16,2176]{2,1,0:T(8,128)(2,1)}, bf16[6,16,2176]{2,1,0:T(8,128)(2,1)})) conditional(s32[]{:T(128)} %clamp.3, (bf16[6,16,2176]{2,1,0:T(8,128)(2,1)}, bf16[6,16,2176]{2,1,0:T(8,128)(2,1)}) %tuple.19, (bf16[6,16,2176]{2,1,0:T(8,128)(2,1)}, bf16[6,16,2176]{2,1,0:T(8,128)(2,1)}) %tuple.19, ...), branch_computations={%region_2.0_spmd, %region_3.0_spmd, %region_4.0_spmd} | conditional | flops 417792 | bytes 5013608 | solution.py:796
  56.8 0.9 slice.14
  57.8 0.9 slice.12
  58.7 3.0 %collective-permute-start.2 = (bf16[2,16,2176]{2,1,0:T(8,128)(2,1)S(1)}, bf16[2,16,2176]{2,1,0:T(8,128)(2,1)S(1)}, u32[]{:S(2)}, u32[]{:S(2)}) collective-permute-start(bf16[2,16,2176]{2,1,0:T(8,128)(2,1)S(1)} %slice.12), channel_id=1, source_target_pairs={{0,16},{2,18},{4,20},{6,22},{8,24},{10,26},{12,28},{14,30},{16,0},... | collective-permute-start | bytes 417800 | tf_op jit(solution)/shard_map/cond/branch_1_fun/ppermute | solution.py:765
  61.7 1.0 slice.13
  62.7 1.0 slice.15
  63.7 4.3 %collective-permute-done.3 = bf16[2,16,2176]{2,1,0:T(8,128)(2,1)S(1)} collective-permute-done((bf16[2,16,2176]{2,1,0:T(8,128)(2,1)S(1)}, bf16[2,16,2176]{2,1,0:T(8,128)(2,1)S(1)}, u32[]{:S(2)}, u32[]{:S(2)}) %collective-permute-start.3) | collective-permute-done | bytes 139296 | tf_op jit(solution)/shard_map/cond/branch_1_fun/ppermute | solution.py:765
  68.8 1.9 %collective-permute-done.2 = bf16[2,16,2176]{2,1,0:T(8,128)(2,1)S(1)} collective-permute-done((bf16[2,16,2176]{2,1,0:T(8,128)(2,1)S(1)}, bf16[2,16,2176]{2,1,0:T(8,128)(2,1)S(1)}, u32[]{:S(2)}, u32[]{:S(2)}) %collective-permute-start.2) | collective-permute-done | bytes 139296 | tf_op jit(solution)/shard_map/cond/branch_1_fun/ppermute | solution.py:765
  71.5 3.8 %join_slots.2 = bf16[8,16,4096]{2,1,0:T(8,128)(2,1)} custom-call(s32[16]{0:T(128)S(1)} %copy-done, bf16[8,16,4224]{2,1,0:T(8,128)(2,1)S(1)} %all-to-all-done.recv_ref, bf16[6,16,2176]{2,1,0:T(8,128)(2,1)S(1)} %collective-permute-done.4.main_ref, bf16[6,16,2176]{2,1,0:T(8,128)(2,1)} %get-tuple-element.98.more_ref), custom_call_target="tpu_custom_call" | custom-call | flops 5242880 | bytes 2097152 | tf_op jit(solution)/shard_map/join_slots/pallas_call | solution.py:577
  75.3 3.6 %all-to-all-start.2 = ((bf16[8,16,4096]{2,1,0:T(8,128)(2,1)}), bf16[8,16,4096]{2,1,0:T(8,128)(2,1)S(1)}, u32[]{:S(2)}, u32[]{:S(2)}) async-start(bf16[8,16,4096]{2,1,0:T(8,128)(2,1)} %join_slots.2), calls=%async_computation.2 | async-start | bytes 2097152 | tf_op jit(solution)/shard_map/all_to_all | solution.py:755
  78.9 1.8 %collective-permute-start.5 = (bf16[6,16,2176]{2,1,0:T(8,128)(2,1)S(1)}, bf16[6,16,2176]{2,1,0:T(8,128)(2,1)S(1)}, u32[]{:S(2)}, u32[]{:S(2)}) collective-permute-start(bf16[6,16,2176]{2,1,0:T(8,128)(2,1)S(1)} %get-tuple-element.102), channel_id=1, source_target_pairs={{0,16},{2,18},{4,20},{6,22},{8,24},{10,26},{12,28},{14,30},{16,0},... | collective-permute-start | bytes 1253384 | tf_op jit(solution)/shard_map/ppermute | solution.py:765
  80.7 6.9 %node_inner.4 = (bf16[512,4096]{1,0:T(8,128)(2,1)}, bf16[512,4096]{1,0:T(8,128)(2,1)}, f32[512,128]{1,0:T(8,128)}, f32[512,128]{1,0:T(8,128)}) custom-call(bf16[512,4096]{1,0:T(8,128)(2,1)} %refs_7_.1, bf16[512,4096]{1,0:T(8,128)(2,1)} %refs_8_.1, bf16[512,128]{1,0:T(8,128)(2,1)} %refs_0_.7, bf16[512,128]{1,0:T(8,128)(2,1)} %refs_1_.7, ...), custom_call_target="tpu_custom_call" | custom-call | flops 6442450944 | bytes 6291456 | tf_op jit(solution)/shard_map/node_inner/pallas_call | solution.py:325
  87.6 11.9 %collective-permute-done.5.main_ref = bf16[6,16,2176]{2,1,0:T(8,128)(2,1)S(1)} collective-permute-done((bf16[6,16,2176]{2,1,0:T(8,128)(2,1)S(1)}, bf16[6,16,2176]{2,1,0:T(8,128)(2,1)S(1)}, u32[]{:S(2)}, u32[]{:S(2)}) %collective-permute-start.5) | collective-permute-done | bytes 417824 | tf_op jit(solution)/shard_map/ppermute | solution.py:765
  99.5 3.4 %join_slots.3 = bf16[8,16,4096]{2,1,0:T(8,128)(2,1)} custom-call(s32[16]{0:T(128)S(1)} %copy-done, bf16[8,16,4224]{2,1,0:T(8,128)(2,1)S(1)} %all-to-all-done.1.recv_ref, bf16[6,16,2176]{2,1,0:T(8,128)(2,1)S(1)} %collective-permute-done.5.main_ref, bf16[6,16,2176]{2,1,0:T(8,128)(2,1)S(1)} %copy-done.3), custom_call_target="tpu_custom_call" | custom-call | flops 5242880 | bytes 2097152 | tf_op jit(solution)/shard_map/join_slots/pallas_call | solution.py:577
  102.8 6.4 %all-to-all-start.3 = ((bf16[8,16,4096]{2,1,0:T(8,128)(2,1)}), bf16[8,16,4096]{2,1,0:T(8,128)(2,1)S(1)}, u32[]{:S(2)}, u32[]{:S(2)}) async-start(bf16[8,16,4096]{2,1,0:T(8,128)(2,1)} %join_slots.3), calls=%async_computation.3 | async-start | bytes 2097152 | tf_op jit(solution)/shard_map/all_to_all | solution.py:755
  109.3 6.9 %node_inner.5 = (bf16[512,4096]{1,0:T(8,128)(2,1)}, bf16[512,4096]{1,0:T(8,128)(2,1)}, f32[512,128]{1,0:T(8,128)}, f32[512,128]{1,0:T(8,128)}) custom-call(bf16[512,4096]{1,0:T(8,128)(2,1)} %refs_7_.1, bf16[512,4096]{1,0:T(8,128)(2,1)} %refs_8_.1, bf16[512,128]{1,0:T(8,128)(2,1)} %refs_0_.7, ...), custom_call_target="tpu_custom_call", output_to_operand_aliasing={{0}: (7, {}), {1}: (8, {})} | custom-call | flops 6442450944 | bytes 6291456 | tf_op jit(solution)/shard_map/node_inner/pallas_call | solution.py:325
  116.1 6.9 %node_inner.6 = (bf16[512,4096]{1,0:T(8,128)(2,1)}, bf16[512,4096]{1,0:T(8,128)(2,1)}, f32[512,128]{1,0:T(8,128)}, f32[512,128]{1,0:T(8,128)}) custom-call(bf16[512,4096]{1,0:T(8,128)(2,1)} %refs_7_.1, bf16[512,4096]{1,0:T(8,128)(2,1)} %refs_8_.1, bf16[512,128]{1,0:T(8,128)(2,1)} %refs_0_.7, ...), custom_call_target="tpu_custom_call", output_to_operand_aliasing={{0}: (7, {}), {1}: (8, {})} | custom-call | flops 6442450944 | bytes 6291456 | tf_op jit(solution)/shard_map/node_inner/pallas_call | solution.py:325
  123.0 6.9 %node_inner.7 = (bf16[512,4096]{1,0:T(8,128)(2,1)}, bf16[512,4096]{1,0:T(8,128)(2,1)}, f32[512,128]{1,0:T(8,128)}, f32[512,128]{1,0:T(8,128)}) custom-call(bf16[512,4096]{1,0:T(8,128)(2,1)} %refs_7_.1, bf16[512,4096]{1,0:T(8,128)(2,1)} %refs_8_.1, bf16[512,128]{1,0:T(8,128)(2,1)} %refs_0_.7, ...), custom_call_target="tpu_custom_call", output_to_operand_aliasing={{0}: (7, {}), {1}: (8, {})} | custom-call | flops 6442450944 | bytes 6291456 | tf_op jit(solution)/shard_map/node_inner/pallas_call | solution.py:325
  129.9 9.1 %node_outer.2 = (bf16[512,4096]{1,0:T(8,128)(2,1)}, bf16[512,4096]{1,0:T(8,128)(2,1)}, f32[512,128]{1,0:T(8,128)}, f32[512,128]{1,0:T(8,128)}) custom-call(bf16[512,128]{1,0:T(8,128)(2,1)} %refs_0_.7, bf16[512,128]{1,0:T(8,128)(2,1)} %refs_1_.7, bf16[512,128]{1,0:T(8,128)(2,1)} %get-tuple-element.69.refs_2_, bf16[512,128]{1,0:T(8,128)(2,1)} %get-tuple-element.70.refs_3_, ...), custom_call_target="tpu_custom_call" | custom-call | flops 1073741824 | bytes 14680064 | tf_op jit(solution)/shard_map/node_outer/pallas_call | solution.py:718
  139.0 1.0 copy-done.2
  140.0 8.9 %node_outer.3 = (bf16[512,4096]{1,0:T(8,128)(2,1)}, bf16[512,4096]{1,0:T(8,128)(2,1)}, f32[256,128]{1,0:T(8,128)}, f32[256,128]{1,0:T(8,128)}, bf16[2,256,128]{2,1,0:T(8,128)(2,1)}) custom-call(bf16[512,128]{1,0:T(8,128)(2,1)} %refs_0_.7, bf16[512,128]{1,0:T(8,128)(2,1)} %refs_1_.7, ...), custom_call_target="tpu_custom_call", output_to_operand_aliasing={{0}: (15, {}), {1}: (16, {})} | custom-call | flops 1073741824 | bytes 14680064 | tf_op jit(solution)/shard_map/node_outer/pallas_call | solution.py:718
  148.9 1.5 %collective-permute-done.6 = bf16[2,256,128]{2,1,0:T(8,128)(2,1)S(1)} collective-permute-done((bf16[2,256,128]{2,1,0:T(8,128)(2,1)}, bf16[2,256,128]{2,1,0:T(8,128)(2,1)S(1)}, u32[]{:S(2)}, u32[]{:S(2)}) %collective-permute-start.6) | collective-permute-done | bytes 131104 | tf_op jit(solution)/shard_map/ppermute | solution.py:738
  150.5 1.7 %fusion = (f32[256,128]{1,0:T(8,128)}, f32[256,128]{1,0:T(8,128)}) fusion(f32[256,128]{1,0:T(8,128)} %get-tuple-element.111, f32[2,256,128]{2,1,0:T(8,128)S(1)} %convert_element_type.15, f32[256,128]{1,0:T(8,128)} %get-tuple-element.109), kind=kLoop, calls=%fused_computation.3 | loop fusion | flops 65536 | bytes 786432 | tf_op jit(solution)/shard_map/add | solution.py:739
  (18 shorter events, 2.6 us)
Async XLA Ops:
  6.3 21.3 %all-to-all-start = ((bf16[8,16,4224]{2,1,0:T(8,128)(2,1)}), bf16[8,16,4224]{2,1,0:T(8,128)(2,1)S(1)}, u32[]{:S(2)}, u32[]{:S(2)}) async-start(bf16[8,16,4224]{2,1,0:T(8,128)(2,1)} %bitcast.18), calls=%async_computation | async-start | bytes 2162688 | tf_op jit(solution)/shard_map/all_to_all | solution.py:755
  12.5 18.6 %copy-start = (s32[16]{0:T(128)S(1)}, s32[16]{0:T(128)}, u32[]{:S(2)}) copy-start(s32[16]{0:T(128)} %parents_ref.7) | copy-start | bytes 196
  27.5 26.7 %all-to-all-start.1 = ((bf16[8,16,4224]{2,1,0:T(8,128)(2,1)}), bf16[8,16,4224]{2,1,0:T(8,128)(2,1)S(1)}, u32[]{:S(2)}, u32[]{:S(2)}) async-start(bf16[8,16,4224]{2,1,0:T(8,128)(2,1)} %bitcast.17), calls=%async_computation.1 | async-start | bytes 2162688 | tf_op jit(solution)/shard_map/all_to_all | solution.py:755
  33.7 37.8 %collective-permute-start.4 = (bf16[6,16,2176]{2,1,0:T(8,128)(2,1)S(1)}, bf16[6,16,2176]{2,1,0:T(8,128)(2,1)S(1)}, u32[]{:S(2)}, u32[]{:S(2)}) collective-permute-start(bf16[6,16,2176]{2,1,0:T(8,128)(2,1)S(1)} %get-tuple-element.94), channel_id=1, source_target_pairs={{0,16},{2,18},{4,20},{6,22},{8,24},{10,26},{12,28},{14,30},{16,0},... | collective-permute-start | bytes 1253384 | tf_op jit(solution)/shard_map/ppermute | solution.py:765
  57.7 10.2 %collective-permute-start.3 = (bf16[2,16,2176]{2,1,0:T(8,128)(2,1)S(1)}, bf16[2,16,2176]{2,1,0:T(8,128)(2,1)S(1)}, u32[]{:S(2)}, u32[]{:S(2)}) collective-permute-start(bf16[2,16,2176]{2,1,0:T(8,128)(2,1)S(1)} %slice.14), channel_id=1, source_target_pairs={{0,16},{2,18},{4,20},{6,22},{8,24},{10,26},{12,28},{14,30},{16,0},... | collective-permute-start | bytes 417800 | tf_op jit(solution)/shard_map/cond/branch_1_fun/ppermute | solution.py:765
  58.7 12.0 %collective-permute-start.2 = (bf16[2,16,2176]{2,1,0:T(8,128)(2,1)S(1)}, bf16[2,16,2176]{2,1,0:T(8,128)(2,1)S(1)}, u32[]{:S(2)}, u32[]{:S(2)}) collective-permute-start(bf16[2,16,2176]{2,1,0:T(8,128)(2,1)S(1)} %slice.12), channel_id=1, source_target_pairs={{0,16},{2,18},{4,20},{6,22},{8,24},{10,26},{12,28},{14,30},{16,0},... | collective-permute-start | bytes 417800 | tf_op jit(solution)/shard_map/cond/branch_1_fun/ppermute | solution.py:765
  75.3 27.5 %all-to-all-start.2 = ((bf16[8,16,4096]{2,1,0:T(8,128)(2,1)}), bf16[8,16,4096]{2,1,0:T(8,128)(2,1)S(1)}, u32[]{:S(2)}, u32[]{:S(2)}) async-start(bf16[8,16,4096]{2,1,0:T(8,128)(2,1)} %join_slots.2), calls=%async_computation.2 | async-start | bytes 2097152 | tf_op jit(solution)/shard_map/all_to_all | solution.py:755
  78.9 20.5 %collective-permute-start.5 = (bf16[6,16,2176]{2,1,0:T(8,128)(2,1)S(1)}, bf16[6,16,2176]{2,1,0:T(8,128)(2,1)S(1)}, u32[]{:S(2)}, u32[]{:S(2)}) collective-permute-start(bf16[6,16,2176]{2,1,0:T(8,128)(2,1)S(1)} %get-tuple-element.102), channel_id=1, source_target_pairs={{0,16},{2,18},{4,20},{6,22},{8,24},{10,26},{12,28},{14,30},{16,0},... | collective-permute-start | bytes 1253384 | tf_op jit(solution)/shard_map/ppermute | solution.py:765
  80.7 18.8 %copy-start.3 = (bf16[6,16,2176]{2,1,0:T(8,128)(2,1)S(1)}, bf16[6,16,2176]{2,1,0:T(8,128)(2,1)}, u32[]{:S(2)}) copy-start(bf16[6,16,2176]{2,1,0:T(8,128)(2,1)} %get-tuple-element.103.more_ref) | copy-start | bytes 1253380
  102.8 13.3 %copy-start.1 = (bf16[8,16,4096]{2,1,0:T(8,128)(2,1)}, bf16[8,16,4096]{2,1,0:T(8,128)(2,1)S(1)}, u32[]{:S(2)}) copy-start(bf16[8,16,4096]{2,1,0:T(8,128)(2,1)S(1)} %all-to-all-done.2) | copy-start | bytes 3145732
  102.8 36.1 %all-to-all-start.3 = ((bf16[8,16,4096]{2,1,0:T(8,128)(2,1)}), bf16[8,16,4096]{2,1,0:T(8,128)(2,1)S(1)}, u32[]{:S(2)}, u32[]{:S(2)}) async-start(bf16[8,16,4096]{2,1,0:T(8,128)(2,1)} %join_slots.3), calls=%async_computation.3 | async-start | bytes 2097152 | tf_op jit(solution)/shard_map/all_to_all | solution.py:755
  139.0 1.0 copy-start.2
  148.9 1.6 %collective-permute-start.6 = (bf16[2,256,128]{2,1,0:T(8,128)(2,1)}, bf16[2,256,128]{2,1,0:T(8,128)(2,1)S(1)}, u32[]{:S(2)}, u32[]{:S(2)}) collective-permute-start(bf16[2,256,128]{2,1,0:T(8,128)(2,1)} %get-tuple-element.110), channel_id=1, source_target_pairs={{0,1},{1,0},{2,3},{3,2},{4,5},{5,4},{6,7},{7,6},{8,9},{9,8},{10,11... | collective-permute-start | bytes 393224 | tf_op jit(solution)/shard_map/ppermute | solution.py:738

commit v9 on v8

--- a/solution.py
+++ b/solution.py
@@ -454,7 +454,8 @@
 
 def slot_counts(nodes):
     most = nodes * LEVELS // (LEVELS + 1)
-    return most // 2, most - most // 2
+    main = nodes // 2 - nodes // 16
+    return main, most - main
 
 
 def pack_slots(parents, recv, nodes, heads, head_width):
@@ -770,9 +771,7 @@
         (places[:, None] < half) != (places[None, :] < half),
     )
     crossing = jnp.sum(jnp.any(child, axis=0).astype(jnp.int32))
-    main_count, more_count = slot_counts(nodes)
-    few = more_count // 3
-    crowded = (crossing > main_count).astype(jnp.int32) + (crossing > main_count + few)
+    crowded = crossing > slot_counts(nodes)[0]
 
     shared = (inputs, cotangent, b_matrix, c_matrix)
     sizes = (heads, head_width)
@@ -793,13 +792,10 @@
     for k in range(CHUNKS):
         main, more = pack_slots(parents, received[k], nodes, *sizes)
         packed.append((main, more, cross(main)))
-    others = lax.switch(
+    others = lax.cond(
         crowded,
-        (
-            lambda vs: vs,
-            lambda vs: tuple(jnp.concatenate([cross(v[:few]), v[few:]]) for v in vs),
-            lambda vs: tuple(cross(v) for v in vs),
-        ),
+        lambda vs: tuple(cross(v) for v in vs),
+        lambda vs: vs,
         tuple(p[1] for p in packed),
     )
     states = []

time: 153 us -> 142 us (0.928)
  waiting for transfers between devices: 44.7 us -> 38.7 us
  local copies, waits for them, and re-layouts: 4.79 us -> 0.99 us
  starting transfers between devices: 27.4 us -> 29.2 us
  other arithmetic: 4.15 us -> 2.46 us
    ppermute x4 -> x2, waiting for transfers between devices: 18.1 us -> 10.4 us  [cross(): return lax.ppermute(v, 'node', across)]
    slice x4 -> x0, local copies, waits for them, and re-layouts: 3.79 us -> none  [the longest x2 1.95 us: one_device(): v[few:]]
    all_to_all x4, starting transfers between devices: 19.8 us -> 22.8 us  [swap(): lax.all_to_all(v.reshape(half, state // half, v.shape[-1]), 'node', split...]
    all_to_all x4, waiting for transfers between devices: 25.1 us -> 26.8 us  [swap(): lax.all_to_all(v.reshape(half, state // half, v.shape[-1]), 'node', split...]
    concatenate x2 -> x0, other arithmetic: 1.61 us -> none  [one_device(): jnp.concatenate([cross(v[:few]), v[few:]])]
    ppermute x4 -> x2, starting transfers between devices: 7.51 us -> 6.3 us  [cross(): return lax.ppermute(v, 'node', across)]
  transfers between devices with their start and end apart: 9 -> 7, of which waited for: 6 -> 5; matrix products, arithmetic and copies ran while one was open for 4% -> 1% of each run, Pallas kernels for 33% -> 36%
where the time goes in v9:
time: 142 us; the launch traced here: 141 us
  Pallas kernels  68.6 us (48%)
  waiting for transfers between devices  38.7 us (27%)
  starting transfers between devices  29.2 us (21%)
  other arithmetic  2.46 us (2%)
    pallas_call x4, Pallas kernels, node_inner(): pl.pallas_call(kernel, grid=(count,), in_specs=in_specs, out_specs=[pl.Bl...  27.5 us
    all_to_all x4, waiting for transfers between devices, swap(): lax.all_to_all(v.reshape(half, state // half, v.shape[-1]), 'node', split...  26.8 us
    all_to_all x4, starting transfers between devices, swap(): lax.all_to_all(v.reshape(half, state // half, v.shape[-1]), 'node', split...  22.8 us
    pallas_call x2, Pallas kernels, node_outer(): pl.pallas_call(functools.partial(outer_kernel, heads, head_width, chunk,...  17.9 us
    pallas_call x2, Pallas kernels, node_states(): pl.pallas_call(functools.partial(states_kernel, heads, head_width, chunk,...  11.3 us
    ppermute x2, waiting for transfers between devices, cross(): return lax.ppermute(v, 'node', across)  10.4 us
    pallas_call x2, Pallas kernels, join_slots(): pl.pallas_call(kernel, in_specs=in_specs, out_specs=pl.BlockSpec(memory_s...  6.72 us
    ppermute x2, starting transfers between devices, cross(): return lax.ppermute(v, 'node', across)  6.3 us
  transfers between devices with their start and end apart: 7, of which 5 were waited for; matrix products, arithmetic and copies ran while one was open for 1% of the time, Pallas kernels for 36%

profile of v9, /device:TPU:0, one launch (start us, length us, event | category | flops | bytes accessed | tf_op | source)
XLA Modules:
  0.0 141.3 jit_solution(13098858754296059708)
XLA Ops:
  0.6 5.7 %node_states.3 = (bf16[128,4224]{1,0:T(8,128)(2,1)}, f32[512,128]{1,0:T(8,128)}, f32[32,512]{1,0:T(8,128)}, bf16[512,128]{1,0:T(8,128)(2,1)}, bf16[512,128]{1,0:...) custom-call(bf16[512,4096]{1,0:T(8,128)(2,1)} %refs_7_.1, ...), custom_call_target="tpu_custom_call" | custom-call | flops 536870912 | bytes 6291456 | tf_op jit(solution)/shard_map/node_states/pallas_call | solution.py:183
  6.3 6.2 %all-to-all-start = ((bf16[8,16,4224]{2,1,0:T(8,128)(2,1)}), bf16[8,16,4224]{2,1,0:T(8,128)(2,1)S(1)}, u32[]{:S(2)}, u32[]{:S(2)}) async-start(bf16[8,16,4224]{2,1,0:T(8,128)(2,1)} %bitcast.18), calls=%async_computation | async-start | bytes 2162688 | tf_op jit(solution)/shard_map/all_to_all | solution.py:756
  12.5 5.6 %node_states.2 = (bf16[128,4224]{1,0:T(8,128)(2,1)}, f32[512,128]{1,0:T(8,128)}, f32[32,512]{1,0:T(8,128)}, bf16[512,128]{1,0:T(8,128)(2,1)}, bf16[512,128]{1,0:...) custom-call(bf16[512,4096]{1,0:T(8,128)(2,1)} %refs_7_.1, ...), custom_call_target="tpu_custom_call" | custom-call | flops 536870912 | bytes 6291456 | tf_op jit(solution)/shard_map/node_states/pallas_call | solution.py:183
  18.2 9.4 %all-to-all-done.recv_ref = bf16[8,16,4224]{2,1,0:T(8,128)(2,1)S(1)} async-done(((bf16[8,16,4224]{2,1,0:T(8,128)(2,1)}), bf16[8,16,4224]{2,1,0:T(8,128)(2,1)S(1)}, u32[]{:S(2)}, u32[]{:S(2)}) %all-to-all-start) | async-done | bytes 1081376 | tf_op jit(solution)/shard_map/all_to_all | solution.py:756
  27.6 3.6 %all-to-all-start.1 = ((bf16[8,16,4224]{2,1,0:T(8,128)(2,1)}), bf16[8,16,4224]{2,1,0:T(8,128)(2,1)S(1)}, u32[]{:S(2)}, u32[]{:S(2)}) async-start(bf16[8,16,4224]{2,1,0:T(8,128)(2,1)} %bitcast.17), calls=%async_computation.1 | async-start | bytes 2162688 | tf_op jit(solution)/shard_map/all_to_all | solution.py:756
  31.1 0.0 copy-done
  31.1 2.6 %pack_slots.2 = (bf16[7,16,2176]{2,1,0:T(8,128)(2,1)}, bf16[5,16,2176]{2,1,0:T(8,128)(2,1)S(1)}) custom-call(s32[16]{0:T(128)S(1)} %copy-done, bf16[8,16,4224]{2,1,0:T(8,128)(2,1)S(1)} %all-to-all-done.recv_ref), custom_call_target="tpu_custom_call" | custom-call | flops 5242880 | bytes 2097152 | tf_op jit(solution)/shard_map/pack_slots/pallas_call | solution.py:468
  33.7 2.7 %collective-permute-start.2 = (bf16[7,16,2176]{2,1,0:T(8,128)(2,1)}, bf16[7,16,2176]{2,1,0:T(8,128)(2,1)S(1)}, u32[]{:S(2)}, u32[]{:S(2)}) collective-permute-start(bf16[7,16,2176]{2,1,0:T(8,128)(2,1)} %get-tuple-element.88), channel_id=1, source_target_pairs={{0,16},{2,18},{4,20},{6,22},{8,24},{10,26},{12,28},{14,30},{16,0},... | collective-permute-start | bytes 1462280 | tf_op jit(solution)/shard_map/ppermute | solution.py:766
  36.5 0.1 fusion.3
  36.6 0.6 convert_reduce_fusion
  37.8 17.4 %all-to-all-done.1.recv_ref = bf16[8,16,4224]{2,1,0:T(8,128)(2,1)S(1)} async-done(((bf16[8,16,4224]{2,1,0:T(8,128)(2,1)}), bf16[8,16,4224]{2,1,0:T(8,128)(2,1)S(1)}, u32[]{:S(2)}, u32[]{:S(2)}) %all-to-all-start.1) | async-done | bytes 1081376 | tf_op jit(solution)/shard_map/all_to_all | solution.py:756
  55.2 2.5 %pack_slots.3 = (bf16[7,16,2176]{2,1,0:T(8,128)(2,1)S(1)}, bf16[5,16,2176]{2,1,0:T(8,128)(2,1)}) custom-call(s32[16]{0:T(128)S(1)} %copy-done, bf16[8,16,4224]{2,1,0:T(8,128)(2,1)S(1)} %all-to-all-done.1.recv_ref), custom_call_target="tpu_custom_call" | custom-call | flops 5242880 | bytes 2097152 | tf_op jit(solution)/shard_map/pack_slots/pallas_call | solution.py:468
  57.7 0.1 collective-permute-done.2.main_ref
  57.9 3.4 %join_slots.2 = bf16[8,16,4096]{2,1,0:T(8,128)(2,1)} custom-call(s32[16]{0:T(128)S(1)} %copy-done, bf16[8,16,4224]{2,1,0:T(8,128)(2,1)S(1)} %all-to-all-done.recv_ref, bf16[7,16,2176]{2,1,0:T(8,128)(2,1)S(1)} %collective-permute-done.2.main_ref, bf16[5,16,2176]{2,1,0:T(8,128)(2,1)S(1)} %get-tuple-element.92.more_ref), custom_call_target="tpu_custom_call" | custom-call | flops 5242880 | bytes 2097152 | tf_op jit(solution)/shard_map/join_slots/pallas_call | solution.py:578
  61.2 4.2 %all-to-all-start.2 = ((bf16[8,16,4096]{2,1,0:T(8,128)(2,1)}), bf16[8,16,4096]{2,1,0:T(8,128)(2,1)S(1)}, u32[]{:S(2)}, u32[]{:S(2)}) async-start(bf16[8,16,4096]{2,1,0:T(8,128)(2,1)} %join_slots.2), calls=%async_computation.2 | async-start | bytes 2097152 | tf_op jit(solution)/shard_map/all_to_all | solution.py:756
  65.4 3.6 %collective-permute-start.3 = (bf16[7,16,2176]{2,1,0:T(8,128)(2,1)S(1)}, bf16[7,16,2176]{2,1,0:T(8,128)(2,1)S(1)}, u32[]{:S(2)}, u32[]{:S(2)}) collective-permute-start(bf16[7,16,2176]{2,1,0:T(8,128)(2,1)S(1)} %get-tuple-element.96), channel_id=1, source_target_pairs={{0,16},{2,18},{4,20},{6,22},{8,24},{10,26},{12,28},{14,30},{16,0},... | collective-permute-start | bytes 1462280 | tf_op jit(solution)/shard_map/ppermute | solution.py:766
  69.0 6.9 %node_inner.4 = (bf16[512,4096]{1,0:T(8,128)(2,1)}, bf16[512,4096]{1,0:T(8,128)(2,1)}, f32[512,128]{1,0:T(8,128)}, f32[512,128]{1,0:T(8,128)}) custom-call(bf16[512,4096]{1,0:T(8,128)(2,1)} %refs_7_.1, bf16[512,4096]{1,0:T(8,128)(2,1)} %refs_8_.1, bf16[512,128]{1,0:T(8,128)(2,1)} %refs_0_.7, bf16[512,128]{1,0:T(8,128)(2,1)} %refs_1_.7, ...), custom_call_target="tpu_custom_call" | custom-call | flops 6442450944 | bytes 6291456 | tf_op jit(solution)/shard_map/node_inner/pallas_call | solution.py:325
  75.9 10.2 %collective-permute-done.3.main_ref = bf16[7,16,2176]{2,1,0:T(8,128)(2,1)S(1)} collective-permute-done((bf16[7,16,2176]{2,1,0:T(8,128)(2,1)S(1)}, bf16[7,16,2176]{2,1,0:T(8,128)(2,1)S(1)}, u32[]{:S(2)}, u32[]{:S(2)}) %collective-permute-start.3) | collective-permute-done | bytes 487456 | tf_op jit(solution)/shard_map/ppermute | solution.py:766
  86.1 0.0 copy-done.3
  86.1 3.4 %join_slots.3 = bf16[8,16,4096]{2,1,0:T(8,128)(2,1)} custom-call(s32[16]{0:T(128)S(1)} %copy-done, bf16[8,16,4224]{2,1,0:T(8,128)(2,1)S(1)} %all-to-all-done.1.recv_ref, bf16[7,16,2176]{2,1,0:T(8,128)(2,1)S(1)} %collective-permute-done.3.main_ref, bf16[5,16,2176]{2,1,0:T(8,128)(2,1)S(1)} %copy-done.3), custom_call_target="tpu_custom_call" | custom-call | flops 5242880 | bytes 2097152 | tf_op jit(solution)/shard_map/join_slots/pallas_call | solution.py:578
  89.5 0.0 all-to-all-done.2
  89.5 8.9 %all-to-all-start.3 = ((bf16[8,16,4096]{2,1,0:T(8,128)(2,1)}), bf16[8,16,4096]{2,1,0:T(8,128)(2,1)S(1)}, u32[]{:S(2)}, u32[]{:S(2)}) async-start(bf16[8,16,4096]{2,1,0:T(8,128)(2,1)} %join_slots.3), calls=%async_computation.3 | async-start | bytes 2097152 | tf_op jit(solution)/shard_map/all_to_all | solution.py:756
  98.4 6.8 %node_inner.5 = (bf16[512,4096]{1,0:T(8,128)(2,1)}, bf16[512,4096]{1,0:T(8,128)(2,1)}, f32[512,128]{1,0:T(8,128)}, f32[512,128]{1,0:T(8,128)}) custom-call(bf16[512,4096]{1,0:T(8,128)(2,1)} %refs_7_.1, bf16[512,4096]{1,0:T(8,128)(2,1)} %refs_8_.1, bf16[512,128]{1,0:T(8,128)(2,1)} %refs_0_.7, ...), custom_call_target="tpu_custom_call", output_to_operand_aliasing={{0}: (7, {}), {1}: (8, {})} | custom-call | flops 6442450944 | bytes 6291456 | tf_op jit(solution)/shard_map/node_inner/pallas_call | solution.py:325
  105.2 6.9 %node_inner.6 = (bf16[512,4096]{1,0:T(8,128)(2,1)}, bf16[512,4096]{1,0:T(8,128)(2,1)}, f32[512,128]{1,0:T(8,128)}, f32[512,128]{1,0:T(8,128)}) custom-call(bf16[512,4096]{1,0:T(8,128)(2,1)} %refs_7_.1, bf16[512,4096]{1,0:T(8,128)(2,1)} %refs_8_.1, bf16[512,128]{1,0:T(8,128)(2,1)} %refs_0_.7, ...), custom_call_target="tpu_custom_call", output_to_operand_aliasing={{0}: (7, {}), {1}: (8, {})} | custom-call | flops 6442450944 | bytes 6291456 | tf_op jit(solution)/shard_map/node_inner/pallas_call | solution.py:325
  112.1 6.9 %node_inner.7 = (bf16[512,4096]{1,0:T(8,128)(2,1)}, bf16[512,4096]{1,0:T(8,128)(2,1)}, f32[512,128]{1,0:T(8,128)}, f32[512,128]{1,0:T(8,128)}) custom-call(bf16[512,4096]{1,0:T(8,128)(2,1)} %refs_7_.1, bf16[512,4096]{1,0:T(8,128)(2,1)} %refs_8_.1, bf16[512,128]{1,0:T(8,128)(2,1)} %refs_0_.7, ...), custom_call_target="tpu_custom_call", output_to_operand_aliasing={{0}: (7, {}), {1}: (8, {})} | custom-call | flops 6442450944 | bytes 6291456 | tf_op jit(solution)/shard_map/node_inner/pallas_call | solution.py:325
  119.0 9.1 %node_outer.2 = (bf16[512,4096]{1,0:T(8,128)(2,1)}, bf16[512,4096]{1,0:T(8,128)(2,1)}, f32[512,128]{1,0:T(8,128)}, f32[512,128]{1,0:T(8,128)}) custom-call(bf16[512,128]{1,0:T(8,128)(2,1)} %refs_0_.7, bf16[512,128]{1,0:T(8,128)(2,1)} %refs_1_.7, bf16[512,128]{1,0:T(8,128)(2,1)} %get-tuple-element.63.refs_2_, bf16[512,128]{1,0:T(8,128)(2,1)} %get-tuple-element.64.refs_3_, ...), custom_call_target="tpu_custom_call" | custom-call | flops 1073741824 | bytes 14680064 | tf_op jit(solution)/shard_map/node_outer/pallas_call | solution.py:719
  128.1 0.0 all-to-all-done.3
  128.1 1.0 copy-done.2
  129.1 8.9 %node_outer.3 = (bf16[512,4096]{1,0:T(8,128)(2,1)}, bf16[512,4096]{1,0:T(8,128)(2,1)}, f32[256,128]{1,0:T(8,128)}, f32[256,128]{1,0:T(8,128)}, bf16[2,256,128]{2,1,0:T(8,128)(2,1)}) custom-call(bf16[512,128]{1,0:T(8,128)(2,1)} %refs_0_.7, bf16[512,128]{1,0:T(8,128)(2,1)} %refs_1_.7, ...), custom_call_target="tpu_custom_call", output_to_operand_aliasing={{0}: (15, {}), {1}: (16, {})} | custom-call | flops 1073741824 | bytes 14680064 | tf_op jit(solution)/shard_map/node_outer/pallas_call | solution.py:719
  138.0 0.1 collective-permute-start.4
  138.0 1.5 %collective-permute-done.4 = bf16[2,256,128]{2,1,0:T(8,128)(2,1)S(1)} collective-permute-done((bf16[2,256,128]{2,1,0:T(8,128)(2,1)}, bf16[2,256,128]{2,1,0:T(8,128)(2,1)S(1)}, u32[]{:S(2)}, u32[]{:S(2)}) %collective-permute-start.4) | collective-permute-done | bytes 131104 | tf_op jit(solution)/shard_map/ppermute | solution.py:739
  139.6 1.7 %fusion = (f32[256,128]{1,0:T(8,128)}, f32[256,128]{1,0:T(8,128)}) fusion(f32[256,128]{1,0:T(8,128)} %get-tuple-element.105, f32[2,256,128]{2,1,0:T(8,128)S(1)} %convert_element_type.11, f32[256,128]{1,0:T(8,128)} %get-tuple-element.103), kind=kLoop, calls=%fused_computation.1 | loop fusion | flops 65536 | bytes 786432 | tf_op jit(solution)/shard_map/add | solution.py:740
  (8 shorter events, 0.0 us)
Async XLA Ops:
  6.3 21.3 %all-to-all-start = ((bf16[8,16,4224]{2,1,0:T(8,128)(2,1)}), bf16[8,16,4224]{2,1,0:T(8,128)(2,1)S(1)}, u32[]{:S(2)}, u32[]{:S(2)}) async-start(bf16[8,16,4224]{2,1,0:T(8,128)(2,1)} %bitcast.18), calls=%async_computation | async-start | bytes 2162688 | tf_op jit(solution)/shard_map/all_to_all | solution.py:756
  12.5 18.6 %copy-start = (s32[16]{0:T(128)S(1)}, s32[16]{0:T(128)}, u32[]{:S(2)}) copy-start(s32[16]{0:T(128)} %parents_ref.7) | copy-start | bytes 196
  27.6 27.6 %all-to-all-start.1 = ((bf16[8,16,4224]{2,1,0:T(8,128)(2,1)}), bf16[8,16,4224]{2,1,0:T(8,128)(2,1)S(1)}, u32[]{:S(2)}, u32[]{:S(2)}) async-start(bf16[8,16,4224]{2,1,0:T(8,128)(2,1)} %bitcast.17), calls=%async_computation.1 | async-start | bytes 2162688 | tf_op jit(solution)/shard_map/all_to_all | solution.py:756
  33.7 24.1 %collective-permute-start.2 = (bf16[7,16,2176]{2,1,0:T(8,128)(2,1)}, bf16[7,16,2176]{2,1,0:T(8,128)(2,1)S(1)}, u32[]{:S(2)}, u32[]{:S(2)}) collective-permute-start(bf16[7,16,2176]{2,1,0:T(8,128)(2,1)} %get-tuple-element.88), channel_id=1, source_target_pairs={{0,16},{2,18},{4,20},{6,22},{8,24},{10,26},{12,28},{14,30},{16,0},... | collective-permute-start | bytes 1462280 | tf_op jit(solution)/shard_map/ppermute | solution.py:766
  61.2 28.2 %all-to-all-start.2 = ((bf16[8,16,4096]{2,1,0:T(8,128)(2,1)}), bf16[8,16,4096]{2,1,0:T(8,128)(2,1)S(1)}, u32[]{:S(2)}, u32[]{:S(2)}) async-start(bf16[8,16,4096]{2,1,0:T(8,128)(2,1)} %join_slots.2), calls=%async_computation.2 | async-start | bytes 2097152 | tf_op jit(solution)/shard_map/all_to_all | solution.py:756
  65.4 20.7 %collective-permute-start.3 = (bf16[7,16,2176]{2,1,0:T(8,128)(2,1)S(1)}, bf16[7,16,2176]{2,1,0:T(8,128)(2,1)S(1)}, u32[]{:S(2)}, u32[]{:S(2)}) collective-permute-start(bf16[7,16,2176]{2,1,0:T(8,128)(2,1)S(1)} %get-tuple-element.96), channel_id=1, source_target_pairs={{0,16},{2,18},{4,20},{6,22},{8,24},{10,26},{12,28},{14,30},{16,0},... | collective-permute-start | bytes 1462280 | tf_op jit(solution)/shard_map/ppermute | solution.py:766
  69.0 17.1 %copy-start.3 = (bf16[5,16,2176]{2,1,0:T(8,128)(2,1)S(1)}, bf16[5,16,2176]{2,1,0:T(8,128)(2,1)}, u32[]{:S(2)}) copy-start(bf16[5,16,2176]{2,1,0:T(8,128)(2,1)} %get-tuple-element.97.more_ref) | copy-start | bytes 1044484
  89.5 15.7 %copy-start.1 = (bf16[8,16,4096]{2,1,0:T(8,128)(2,1)}, bf16[8,16,4096]{2,1,0:T(8,128)(2,1)S(1)}, u32[]{:S(2)}) copy-start(bf16[8,16,4096]{2,1,0:T(8,128)(2,1)S(1)} %all-to-all-done.2) | copy-start | bytes 3145732
  89.5 38.6 %all-to-all-start.3 = ((bf16[8,16,4096]{2,1,0:T(8,128)(2,1)}), bf16[8,16,4096]{2,1,0:T(8,128)(2,1)S(1)}, u32[]{:S(2)}, u32[]{:S(2)}) async-start(bf16[8,16,4096]{2,1,0:T(8,128)(2,1)} %join_slots.3), calls=%async_computation.3 | async-start | bytes 2097152 | tf_op jit(solution)/shard_map/all_to_all | solution.py:756
  128.1 1.0 copy-start.2
  138.0 1.6 %collective-permute-start.4 = (bf16[2,256,128]{2,1,0:T(8,128)(2,1)}, bf16[2,256,128]{2,1,0:T(8,128)(2,1)S(1)}, u32[]{:S(2)}, u32[]{:S(2)}) collective-permute-start(bf16[2,256,128]{2,1,0:T(8,128)(2,1)} %get-tuple-element.104), channel_id=1, source_target_pairs={{0,1},{1,0},{2,3},{3,2},{4,5},{5,4},{6,7},{7,6},{8,9},{9,8},{10,11... | collective-permute-start | bytes 393224 | tf_op jit(solution)/shard_map/ppermute | solution.py:739

commit v10 on v9

--- a/solution.py
+++ b/solution.py
@@ -126,9 +126,11 @@
     wait_all(later_in)
     b_turned = b_ref[...].T
     c_turned = c_ref[...].T
-    for rows in (slice(0, middle), slice(middle, length)):
-        gram_ref[rows] = mm(c_ref[rows], b_ref[rows], NT).astype(bf16)
-    small = (1, 2, 3, 4, 5, 7)
+    small = (1, 2, 3, 4, 7)
+    if chunk == CHUNKS - 1:
+        small = (1, 2, 3, 4, 5, 7)
+        for rows in (slice(0, middle), slice(middle, length)):
+            gram_ref[rows] = mm(c_ref[rows], b_ref[rows], NT).astype(bf16)
     made = (send_ref, low_ref, src_ref, grow_ref, tail_ref, gram_ref, keep_ref, steps_ref)
     stores = []
     ready = [(made[n], outs[n]) for n in small]
@@ -509,8 +511,8 @@
     base = lax.axis_index("node") // half * half
     rank_nodes(parents_ref, rank_ref, half)
     decay_ref[...] = widen(recv_ref[:, :, 2 * width :], heads, head_width)
-    slot_ref[:main] = main_ref[:, :, :width].astype(f32)
-    slot_ref[main:] = more_ref[:, :, :width].astype(f32)
+    slot_ref[:main] = main_ref[:, :, :width]
+    slot_ref[main:] = more_ref[:, :, :width]
     chain_ref[:main] = widen(main_ref[:, :, width:], heads, head_width)
     chain_ref[main:] = widen(more_ref[:, :, width:], heads, head_width)
     back_ref[...] = jnp.zeros_like(back_ref)
@@ -534,8 +536,8 @@
                 back_ref[where] = back_ref[where] + flow
 
             if start is not None:
-                value = jnp.where(near, recv_ref[where, :, :width].astype(f32), slot_ref[slot])
-                value = jnp.where(live, value, 0.0)
+                value = jnp.where(near, recv_ref[where, :, :width], slot_ref[slot])
+                value = jnp.where(live, value.astype(f32), 0.0)
                 start = start + (value if factor is None else factor * value)
             if level < LEVELS - 1:
                 step = jnp.where(near, decay_ref[pl.ds(where, 1)], chain_ref[pl.ds(slot, 1)])
@@ -558,7 +560,7 @@
 
         @pl.when(rank_ref[node] >= 0)
         def _():
-            extra = slot_ref[rank_ref[node]]
+            extra = slot_ref[rank_ref[node]].astype(f32)
             back_ref[m] = back_ref[m] + extra
             climb(node, extra * decay_ref[pl.ds(m, 1)], None)
 
@@ -582,7 +584,7 @@
         out_shape=jax.ShapeDtypeStruct((half, rows, 2 * width), bf16),
         scratch_shapes=[
             pltpu.VMEM((half, width), f32),
-            pltpu.VMEM((slots, rows, width), f32),
+            pltpu.VMEM((slots, rows, width), bf16),
             pltpu.VMEM((slots, width), f32),
             pltpu.VMEM((half, rows, width), f32),
             pltpu.SMEM((nodes,), jnp.int32),
@@ -784,14 +786,15 @@
     for k in range(CHUNKS):
         for part in range(PARTS):
             *prior, gc, gb = node_inner(
-                *shared, made[0][5], made[k][1], made[k][2], prior, k, part, PARTS, *sizes
+                *shared, made[-1][5], made[k][1], made[k][2], prior, k, part, PARTS, *sizes
             )
             found.append((gb, gc))
     inner = prior
     packed = []
     for k in range(CHUNKS):
         main, more = pack_slots(parents, received[k], nodes, *sizes)
-        packed.append((main, more, cross(main)))
+        held = pltpu.with_memory_space_constraint(main, pltpu.HBM)
+        packed.append((main, more, cross(held)))
     others = lax.cond(
         crowded,
         lambda vs: tuple(cross(v) for v in vs),

time: 142 us -> 143 us (level)
  starting transfers between devices: 29.2 us -> 27.3 us
  waiting for transfers between devices: 38.7 us -> 40.5 us
  transfers between devices with their start and end apart: 7 -> 7, of which waited for: 5 -> 4; matrix products, arithmetic and copies ran while one was open for 1% -> 1% of each run, Pallas kernels for 36% -> 35%
where the time goes in v10:
time: 143 us; the launch traced here: 142 us
  Pallas kernels  68.5 us (48%)
  waiting for transfers between devices  40.5 us (28%)
  starting transfers between devices  27.3 us (19%)
  other arithmetic  2.45 us (2%)
  local copies, waits for them, and re-layouts  1.77 us (1%)
    all_to_all x4, waiting for transfers between devices, swap(): lax.all_to_all(v.reshape(half, state // half, v.shape[-1]), 'node', split...  28 us
    pallas_call x4, Pallas kernels, node_inner(): pl.pallas_call(kernel, grid=(count,), in_specs=in_specs, out_specs=[pl.Bl...  27.5 us
    all_to_all x4, starting transfers between devices, swap(): lax.all_to_all(v.reshape(half, state // half, v.shape[-1]), 'node', split...  21.5 us
    pallas_call x2, Pallas kernels, node_outer(): pl.pallas_call(functools.partial(outer_kernel, heads, head_width, chunk,...  17.9 us
    pallas_call x2, Pallas kernels, node_states(): pl.pallas_call(functools.partial(states_kernel, heads, head_width, chunk,...  11.1 us
    ppermute x2, waiting for transfers between devices, cross(): return lax.ppermute(v, 'node', across)  11 us
    pallas_call x2, Pallas kernels, join_slots(): pl.pallas_call(kernel, in_specs=in_specs, out_specs=pl.BlockSpec(memory_s...  7.58 us
    ppermute x2, starting transfers between devices, cross(): return lax.ppermute(v, 'node', across)  5.74 us
  transfers between devices with their start and end apart: 7, of which 4 were waited for; matrix products, arithmetic and copies ran while one was open for 1% of the time, Pallas kernels for 35%

profile of v10, /device:TPU:0, one launch (start us, length us, event | category | flops | bytes accessed | tf_op | source)
XLA Modules:
  0.0 142.0 jit_solution(2734029338635576515)
XLA Ops:
  0.6 5.5 %node_states.3 = (bf16[128,4224]{1,0:T(8,128)(2,1)}, f32[512,128]{1,0:T(8,128)}, f32[32,512]{1,0:T(8,128)}, bf16[512,128]{1,0:T(8,128)(2,1)}, bf16[512,128]{1,0:...) custom-call(bf16[512,4096]{1,0:T(8,128)(2,1)} %refs_7_.1, ...), custom_call_target="tpu_custom_call" | custom-call | flops 536870912 | bytes 6291456 | tf_op jit(solution)/shard_map/node_states/pallas_call | solution.py:185
  6.1 6.2 %all-to-all-start = ((bf16[8,16,4224]{2,1,0:T(8,128)(2,1)}), bf16[8,16,4224]{2,1,0:T(8,128)(2,1)S(1)}, u32[]{:S(2)}, u32[]{:S(2)}) async-start(bf16[8,16,4224]{2,1,0:T(8,128)(2,1)} %bitcast.18), calls=%async_computation | async-start | bytes 2162688 | tf_op jit(solution)/shard_map/all_to_all | solution.py:758
  12.3 5.6 %node_states.2 = (bf16[128,4224]{1,0:T(8,128)(2,1)}, f32[512,128]{1,0:T(8,128)}, f32[32,512]{1,0:T(8,128)}, bf16[512,128]{1,0:T(8,128)(2,1)}, bf16[512,128]{1,0:...) custom-call(bf16[512,4096]{1,0:T(8,128)(2,1)} %refs_7_.1, ...), custom_call_target="tpu_custom_call" | custom-call | flops 536870912 | bytes 6291456 | tf_op jit(solution)/shard_map/node_states/pallas_call | solution.py:185
  18.0 9.4 %all-to-all-done.recv_ref = bf16[8,16,4224]{2,1,0:T(8,128)(2,1)S(1)} async-done(((bf16[8,16,4224]{2,1,0:T(8,128)(2,1)}), bf16[8,16,4224]{2,1,0:T(8,128)(2,1)S(1)}, u32[]{:S(2)}, u32[]{:S(2)}) %all-to-all-start) | async-done | bytes 1081376 | tf_op jit(solution)/shard_map/all_to_all | solution.py:758
  27.4 3.6 %all-to-all-start.1 = ((bf16[8,16,4224]{2,1,0:T(8,128)(2,1)}), bf16[8,16,4224]{2,1,0:T(8,128)(2,1)S(1)}, u32[]{:S(2)}, u32[]{:S(2)}) async-start(bf16[8,16,4224]{2,1,0:T(8,128)(2,1)} %bitcast.17), calls=%async_computation.1 | async-start | bytes 2162688 | tf_op jit(solution)/shard_map/all_to_all | solution.py:758
  30.9 0.0 copy-done
  30.9 1.9 %pack_slots.2 = (bf16[7,16,2176]{2,1,0:T(8,128)(2,1)S(1)}, bf16[5,16,2176]{2,1,0:T(8,128)(2,1)S(1)}) custom-call(s32[16]{0:T(128)S(1)} %copy-done, bf16[8,16,4224]{2,1,0:T(8,128)(2,1)S(1)} %all-to-all-done.recv_ref), custom_call_target="tpu_custom_call" | custom-call | flops 5242880 | bytes 2097152 | tf_op jit(solution)/shard_map/pack_slots/pallas_call | solution.py:470
  32.8 2.8 %collective-permute-start.2 = (bf16[7,16,2176]{2,1,0:T(8,128)(2,1)S(1)}, bf16[7,16,2176]{2,1,0:T(8,128)(2,1)}, u32[]{:S(2)}, u32[]{:S(2)}) collective-permute-start(bf16[7,16,2176]{2,1,0:T(8,128)(2,1)S(1)} %get-tuple-element.88), channel_id=1, source_target_pairs={{0,16},{2,18},{4,20},{6,22},{8,24},{10,26},{12,28},{14,30},{16,0},... | collective-permute-start | bytes 1462280 | tf_op jit(solution)/shard_map/ppermute | solution.py:768
  35.6 0.1 fusion.3
  35.7 0.6 convert_reduce_fusion
  37.0 18.6 %all-to-all-done.1.recv_ref = bf16[8,16,4224]{2,1,0:T(8,128)(2,1)S(1)} async-done(((bf16[8,16,4224]{2,1,0:T(8,128)(2,1)}), bf16[8,16,4224]{2,1,0:T(8,128)(2,1)S(1)}, u32[]{:S(2)}, u32[]{:S(2)}) %all-to-all-start.1) | async-done | bytes 1081376 | tf_op jit(solution)/shard_map/all_to_all | solution.py:758
  55.6 2.5 %pack_slots.3 = (bf16[7,16,2176]{2,1,0:T(8,128)(2,1)S(1)}, bf16[5,16,2176]{2,1,0:T(8,128)(2,1)}) custom-call(s32[16]{0:T(128)S(1)} %copy-done, bf16[8,16,4224]{2,1,0:T(8,128)(2,1)S(1)} %all-to-all-done.1.recv_ref), custom_call_target="tpu_custom_call" | custom-call | flops 5242880 | bytes 2097152 | tf_op jit(solution)/shard_map/pack_slots/pallas_call | solution.py:470
  58.1 0.0 collective-permute-done.2.main_ref
  58.1 3.8 %join_slots.2 = bf16[8,16,4096]{2,1,0:T(8,128)(2,1)} custom-call(s32[16]{0:T(128)S(1)} %copy-done, bf16[8,16,4224]{2,1,0:T(8,128)(2,1)S(1)} %all-to-all-done.recv_ref, bf16[7,16,2176]{2,1,0:T(8,128)(2,1)} %collective-permute-done.2.main_ref, bf16[5,16,2176]{2,1,0:T(8,128)(2,1)S(1)} %get-tuple-element.92.more_ref), custom_call_target="tpu_custom_call" | custom-call | flops 5242880 | bytes 2097152 | tf_op jit(solution)/shard_map/join_slots/pallas_call | solution.py:580
  61.9 3.6 %all-to-all-start.2 = ((bf16[8,16,4096]{2,1,0:T(8,128)(2,1)}), bf16[8,16,4096]{2,1,0:T(8,128)(2,1)S(1)}, u32[]{:S(2)}, u32[]{:S(2)}) async-start(bf16[8,16,4096]{2,1,0:T(8,128)(2,1)} %join_slots.2), calls=%async_computation.2 | async-start | bytes 2097152 | tf_op jit(solution)/shard_map/all_to_all | solution.py:758
  65.5 3.0 %collective-permute-start.3 = (bf16[7,16,2176]{2,1,0:T(8,128)(2,1)S(1)}, bf16[7,16,2176]{2,1,0:T(8,128)(2,1)S(1)}, u32[]{:S(2)}, u32[]{:S(2)}) collective-permute-start(bf16[7,16,2176]{2,1,0:T(8,128)(2,1)S(1)} %get-tuple-element.96), channel_id=1, source_target_pairs={{0,16},{2,18},{4,20},{6,22},{8,24},{10,26},{12,28},{14,30},{16,0},... | collective-permute-start | bytes 1462280 | tf_op jit(solution)/shard_map/ppermute | solution.py:768
  68.4 6.9 %node_inner.4 = (bf16[512,4096]{1,0:T(8,128)(2,1)}, bf16[512,4096]{1,0:T(8,128)(2,1)}, f32[512,128]{1,0:T(8,128)}, f32[512,128]{1,0:T(8,128)}) custom-call(bf16[512,4096]{1,0:T(8,128)(2,1)} %refs_7_.1, bf16[512,4096]{1,0:T(8,128)(2,1)} %refs_8_.1, bf16[512,128]{1,0:T(8,128)(2,1)} %refs_0_.7, bf16[512,128]{1,0:T(8,128)(2,1)} %refs_1_.7, ...), custom_call_target="tpu_custom_call" | custom-call | flops 6442450944 | bytes 6291456 | tf_op jit(solution)/shard_map/node_inner/pallas_call | solution.py:327
  75.3 11.0 %collective-permute-done.3.main_ref = bf16[7,16,2176]{2,1,0:T(8,128)(2,1)S(1)} collective-permute-done((bf16[7,16,2176]{2,1,0:T(8,128)(2,1)S(1)}, bf16[7,16,2176]{2,1,0:T(8,128)(2,1)S(1)}, u32[]{:S(2)}, u32[]{:S(2)}) %collective-permute-start.3) | collective-permute-done | bytes 487456 | tf_op jit(solution)/shard_map/ppermute | solution.py:768
  86.3 0.8 copy-done.3
  87.1 3.8 %join_slots.3 = bf16[8,16,4096]{2,1,0:T(8,128)(2,1)} custom-call(s32[16]{0:T(128)S(1)} %copy-done, bf16[8,16,4224]{2,1,0:T(8,128)(2,1)S(1)} %all-to-all-done.1.recv_ref, bf16[7,16,2176]{2,1,0:T(8,128)(2,1)} %copy-done.3, bf16[5,16,2176]{2,1,0:T(8,128)(2,1)S(1)} %copy-done.4), custom_call_target="tpu_custom_call" | custom-call | flops 5242880 | bytes 2097152 | tf_op jit(solution)/shard_map/join_slots/pallas_call | solution.py:580
  90.9 0.0 all-to-all-done.2
  90.9 8.1 %all-to-all-start.3 = ((bf16[8,16,4096]{2,1,0:T(8,128)(2,1)}), bf16[8,16,4096]{2,1,0:T(8,128)(2,1)S(1)}, u32[]{:S(2)}, u32[]{:S(2)}) async-start(bf16[8,16,4096]{2,1,0:T(8,128)(2,1)} %join_slots.3), calls=%async_computation.3 | async-start | bytes 2097152 | tf_op jit(solution)/shard_map/all_to_all | solution.py:758
  99.0 6.8 %node_inner.5 = (bf16[512,4096]{1,0:T(8,128)(2,1)}, bf16[512,4096]{1,0:T(8,128)(2,1)}, f32[512,128]{1,0:T(8,128)}, f32[512,128]{1,0:T(8,128)}) custom-call(bf16[512,4096]{1,0:T(8,128)(2,1)} %refs_7_.1, bf16[512,4096]{1,0:T(8,128)(2,1)} %refs_8_.1, bf16[512,128]{1,0:T(8,128)(2,1)} %refs_0_.7, ...), custom_call_target="tpu_custom_call", output_to_operand_aliasing={{0}: (7, {}), {1}: (8, {})} | custom-call | flops 6442450944 | bytes 6291456 | tf_op jit(solution)/shard_map/node_inner/pallas_call | solution.py:327
  105.9 6.9 %node_inner.6 = (bf16[512,4096]{1,0:T(8,128)(2,1)}, bf16[512,4096]{1,0:T(8,128)(2,1)}, f32[512,128]{1,0:T(8,128)}, f32[512,128]{1,0:T(8,128)}) custom-call(bf16[512,4096]{1,0:T(8,128)(2,1)} %refs_7_.1, bf16[512,4096]{1,0:T(8,128)(2,1)} %refs_8_.1, bf16[512,128]{1,0:T(8,128)(2,1)} %refs_0_.7, ...), custom_call_target="tpu_custom_call", output_to_operand_aliasing={{0}: (7, {}), {1}: (8, {})} | custom-call | flops 6442450944 | bytes 6291456 | tf_op jit(solution)/shard_map/node_inner/pallas_call | solution.py:327
  112.8 6.9 %node_inner.7 = (bf16[512,4096]{1,0:T(8,128)(2,1)}, bf16[512,4096]{1,0:T(8,128)(2,1)}, f32[512,128]{1,0:T(8,128)}, f32[512,128]{1,0:T(8,128)}) custom-call(bf16[512,4096]{1,0:T(8,128)(2,1)} %refs_7_.1, bf16[512,4096]{1,0:T(8,128)(2,1)} %refs_8_.1, bf16[512,128]{1,0:T(8,128)(2,1)} %refs_0_.7, ...), custom_call_target="tpu_custom_call", output_to_operand_aliasing={{0}: (7, {}), {1}: (8, {})} | custom-call | flops 6442450944 | bytes 6291456 | tf_op jit(solution)/shard_map/node_inner/pallas_call | solution.py:327
  119.7 9.1 %node_outer.2 = (bf16[512,4096]{1,0:T(8,128)(2,1)}, bf16[512,4096]{1,0:T(8,128)(2,1)}, f32[512,128]{1,0:T(8,128)}, f32[512,128]{1,0:T(8,128)}) custom-call(bf16[512,128]{1,0:T(8,128)(2,1)} %refs_0_.7, bf16[512,128]{1,0:T(8,128)(2,1)} %refs_1_.7, bf16[512,128]{1,0:T(8,128)(2,1)} %get-tuple-element.63.refs_2_, bf16[512,128]{1,0:T(8,128)(2,1)} %get-tuple-element.64.refs_3_, ...), custom_call_target="tpu_custom_call" | custom-call | flops 1073741824 | bytes 14680064 | tf_op jit(solution)/shard_map/node_outer/pallas_call | solution.py:721
  128.7 0.0 all-to-all-done.3
  128.8 1.0 copy-done.2
  129.7 8.9 %node_outer.3 = (bf16[512,4096]{1,0:T(8,128)(2,1)}, bf16[512,4096]{1,0:T(8,128)(2,1)}, f32[256,128]{1,0:T(8,128)}, f32[256,128]{1,0:T(8,128)}, bf16[2,256,128]{2,1,0:T(8,128)(2,1)}) custom-call(bf16[512,128]{1,0:T(8,128)(2,1)} %refs_0_.7, bf16[512,128]{1,0:T(8,128)(2,1)} %refs_1_.7, ...), custom_call_target="tpu_custom_call", output_to_operand_aliasing={{0}: (15, {}), {1}: (16, {})} | custom-call | flops 1073741824 | bytes 14680064 | tf_op jit(solution)/shard_map/node_outer/pallas_call | solution.py:721
  138.6 0.1 collective-permute-start.4
  138.7 1.5 %collective-permute-done.4 = bf16[2,256,128]{2,1,0:T(8,128)(2,1)S(1)} collective-permute-done((bf16[2,256,128]{2,1,0:T(8,128)(2,1)}, bf16[2,256,128]{2,1,0:T(8,128)(2,1)S(1)}, u32[]{:S(2)}, u32[]{:S(2)}) %collective-permute-start.4) | collective-permute-done | bytes 131104 | tf_op jit(solution)/shard_map/ppermute | solution.py:741
  140.3 1.7 %fusion = (f32[256,128]{1,0:T(8,128)}, f32[256,128]{1,0:T(8,128)}) fusion(f32[256,128]{1,0:T(8,128)} %get-tuple-element.105, f32[2,256,128]{2,1,0:T(8,128)S(1)} %convert_element_type.11, f32[256,128]{1,0:T(8,128)} %get-tuple-element.103), kind=kLoop, calls=%fused_computation.1 | loop fusion | flops 65536 | bytes 786432 | tf_op jit(solution)/shard_map/add | solution.py:742
  (10 shorter events, 0.0 us)
Async XLA Ops:
  6.1 21.3 %all-to-all-start = ((bf16[8,16,4224]{2,1,0:T(8,128)(2,1)}), bf16[8,16,4224]{2,1,0:T(8,128)(2,1)S(1)}, u32[]{:S(2)}, u32[]{:S(2)}) async-start(bf16[8,16,4224]{2,1,0:T(8,128)(2,1)} %bitcast.18), calls=%async_computation | async-start | bytes 2162688 | tf_op jit(solution)/shard_map/all_to_all | solution.py:758
  12.3 18.6 %copy-start = (s32[16]{0:T(128)S(1)}, s32[16]{0:T(128)}, u32[]{:S(2)}) copy-start(s32[16]{0:T(128)} %parents_ref.7) | copy-start | bytes 196
  27.4 28.2 %all-to-all-start.1 = ((bf16[8,16,4224]{2,1,0:T(8,128)(2,1)}), bf16[8,16,4224]{2,1,0:T(8,128)(2,1)S(1)}, u32[]{:S(2)}, u32[]{:S(2)}) async-start(bf16[8,16,4224]{2,1,0:T(8,128)(2,1)} %bitcast.17), calls=%async_computation.1 | async-start | bytes 2162688 | tf_op jit(solution)/shard_map/all_to_all | solution.py:758
  32.8 25.3 %collective-permute-start.2 = (bf16[7,16,2176]{2,1,0:T(8,128)(2,1)S(1)}, bf16[7,16,2176]{2,1,0:T(8,128)(2,1)}, u32[]{:S(2)}, u32[]{:S(2)}) collective-permute-start(bf16[7,16,2176]{2,1,0:T(8,128)(2,1)S(1)} %get-tuple-element.88), channel_id=1, source_target_pairs={{0,16},{2,18},{4,20},{6,22},{8,24},{10,26},{12,28},{14,30},{16,0},... | collective-permute-start | bytes 1462280 | tf_op jit(solution)/shard_map/ppermute | solution.py:768
  61.9 29.0 %all-to-all-start.2 = ((bf16[8,16,4096]{2,1,0:T(8,128)(2,1)}), bf16[8,16,4096]{2,1,0:T(8,128)(2,1)S(1)}, u32[]{:S(2)}, u32[]{:S(2)}) async-start(bf16[8,16,4096]{2,1,0:T(8,128)(2,1)} %join_slots.2), calls=%async_computation.2 | async-start | bytes 2097152 | tf_op jit(solution)/shard_map/all_to_all | solution.py:758
  65.5 20.8 %collective-permute-start.3 = (bf16[7,16,2176]{2,1,0:T(8,128)(2,1)S(1)}, bf16[7,16,2176]{2,1,0:T(8,128)(2,1)S(1)}, u32[]{:S(2)}, u32[]{:S(2)}) collective-permute-start(bf16[7,16,2176]{2,1,0:T(8,128)(2,1)S(1)} %get-tuple-element.96), channel_id=1, source_target_pairs={{0,16},{2,18},{4,20},{6,22},{8,24},{10,26},{12,28},{14,30},{16,0},... | collective-permute-start | bytes 1462280 | tf_op jit(solution)/shard_map/ppermute | solution.py:768
  68.4 18.6 %copy-start.4 = (bf16[5,16,2176]{2,1,0:T(8,128)(2,1)S(1)}, bf16[5,16,2176]{2,1,0:T(8,128)(2,1)}, u32[]{:S(2)}) copy-start(bf16[5,16,2176]{2,1,0:T(8,128)(2,1)} %get-tuple-element.97.more_ref) | copy-start | bytes 1044484
  86.3 0.8 copy-start.3
  90.9 15.0 %copy-start.1 = (bf16[8,16,4096]{2,1,0:T(8,128)(2,1)}, bf16[8,16,4096]{2,1,0:T(8,128)(2,1)S(1)}, u32[]{:S(2)}) copy-start(bf16[8,16,4096]{2,1,0:T(8,128)(2,1)S(1)} %all-to-all-done.2) | copy-start | bytes 3145732
  90.9 37.8 %all-to-all-start.3 = ((bf16[8,16,4096]{2,1,0:T(8,128)(2,1)}), bf16[8,16,4096]{2,1,0:T(8,128)(2,1)S(1)}, u32[]{:S(2)}, u32[]{:S(2)}) async-start(bf16[8,16,4096]{2,1,0:T(8,128)(2,1)} %join_slots.3), calls=%async_computation.3 | async-start | bytes 2097152 | tf_op jit(solution)/shard_map/all_to_all | solution.py:758
  128.7 1.0 copy-start.2
  138.6 1.6 %collective-permute-start.4 = (bf16[2,256,128]{2,1,0:T(8,128)(2,1)}, bf16[2,256,128]{2,1,0:T(8,128)(2,1)S(1)}, u32[]{:S(2)}, u32[]{:S(2)}) collective-permute-start(bf16[2,256,128]{2,1,0:T(8,128)(2,1)} %get-tuple-element.104), channel_id=1, source_target_pairs={{0,1},{1,0},{2,3},{3,2},{4,5},{5,4},{6,7},{7,6},{8,9},{9,8},{10,11... | collective-permute-start | bytes 393224 | tf_op jit(solution)/shard_map/ppermute | solution.py:741
